TPU v7x, 32 devices: a whole 2x2x4 slice. The times are simulated.
32 devices in a mesh: group: 2 (over x), dom: 16 (over z, y, core).
Axes of the slice: x: 2, y: 2, z: 4, core: 2. Of those that a mesh axis runs over, the one named last changes fastest.
Arguments:
- features: bfloat16 [8192, 512], P(('group', 'dom')), may hold values from -6 to 6
- tile_columns: int32 [32, 2, 4], P(('group', 'dom')), may hold values from 0 to 1
- tile_values: bfloat16 [32, 2, 4, 128, 128], P(('group', 'dom')), as said below
- send_rows: int32 [32, 16, 16], P(('group', 'dom')), may hold values from 0 to 255
- send_count: int32 [32, 16], P(('group', 'dom')), may hold values from 0 to 16, as said below
- ghost_target: int32 [32, 16, 16], P(('group', 'dom')), may hold values from 0 to 255
- query_rows: int32 [32, 512], P(('group', 'dom')), may hold values from 0 to 255
- positive_cand: int32 [32, 512], P(('group', 'dom')), may hold values from 0 to 63
- negative_rows: int32 [32, 32], P(('group', 'dom')), may hold values from 0 to 255
- weight_self: bfloat16 [512, 512], replicated, may hold values from -0.25 to 0.25
- weight_neigh: bfloat16 [512, 512], replicated, may hold values from -0.75 to 0.75
Outputs:
- embeddings: bfloat16 [8192, 512], P(('group', 'dom'))
- weight_grads: bfloat16 [1024, 512], P('dom')
Inputs may be any that keep to these rules, and one draw needn't show every extreme that they name: `send_count`: no device sends rows to its own index of dom; in every group one index of dom receives exactly 16 rows from every other index. `tile_values`: weights are zero or between 0.5 and 1.
All inputs are finite; a program needn't handle non-finite values.
Results may differ from a plain program's by a relative error of at most 0.015.
Values may be sent and summed in bfloat16 or wider, within the bound.
No kernel may reach another device: no remote copies, remote signals or barrier semaphores. Data moves between devices by JAX's collectives and lax.ppermute only.
A program may use at most 64 MiB of HBM per device.

v0:
```python
import math

import jax
import jax.numpy as jnp
from jax import lax
from jax.sharding import PartitionSpec as P

LOSS_FACTOR = 64.0
EPSILON = 1e-05


def score_grads(scores, positive, cand_total, query_total):
    sigma = jax.nn.sigmoid(scores)
    dscore = jnp.where(positive, sigma - 1.0, sigma / (cand_total - 1.0)) * (
        LOSS_FACTOR / query_total
    )
    return dscore.astype(jnp.bfloat16)


def transpose_dot(left, right):
    return lax.dot_general(
        left, right, (((0,), (0,)), ((), ())), preferred_element_type=jnp.float32
    )


def on_device(
    features,
    tile_columns,
    tile_values,
    send_rows,
    send_count,
    ghost_target,
    query_rows,
    positive_cand,
    negative_rows,
    weight_self,
    weight_neigh,
):
    node_count, width = features.shape
    row_blocks, tiles_row, tile_size = (
        tile_values.shape[1],
        tile_values.shape[2],
        tile_values.shape[3],
    )
    slot_count = send_rows.shape[2]
    group_count = lax.axis_size("group")
    score_factor = 1.0 / math.sqrt(width)
    outgoing = features[send_rows[0]]
    flags = (jnp.arange(slot_count, dtype=jnp.int32)[None, :] < send_count[0][:, None]).astype(
        jnp.bfloat16
    )
    received, flags_in = (
        lax.all_to_all(outgoing, "dom", split_axis=0, concat_axis=0, tiled=True),
        lax.all_to_all(flags, "dom", split_axis=0, concat_axis=0, tiled=True),
    )
    blocks = features.reshape(row_blocks, tile_size, width)
    picked = blocks[tile_columns[0]]
    local = jnp.einsum(
        "rtij,rtjd->rid", tile_values[0], picked, preferred_element_type=jnp.float32
    ).reshape(node_count, width)
    row_weight = jnp.sum(tile_values[0].astype(jnp.float32), axis=(1, 3)).reshape(node_count)
    live = flags_in.astype(jnp.float32)
    targets = ghost_target[0].reshape(-1)
    weighted = (received.astype(jnp.float32) * live[:, :, None]).reshape(-1, width)
    ghost_sum = jnp.zeros((node_count, width), jnp.float32).at[targets].add(weighted)
    ghost_count = jnp.zeros((node_count,), jnp.float32).at[targets].add(live.reshape(-1))
    degree = 1.0 + row_weight + ghost_count
    aggregate = ((local + ghost_sum) / degree[:, None]).astype(jnp.bfloat16)
    pre = jnp.dot(features, weight_self, preferred_element_type=jnp.float32) + jnp.dot(
        aggregate, weight_neigh, preferred_element_type=jnp.float32
    )
    scale = lax.rsqrt(jnp.mean(pre * pre, axis=-1, keepdims=True) + EPSILON)
    embeds = (pre * scale).astype(jnp.bfloat16)
    queries = embeds[query_rows[0]]
    own_negs = embeds[negative_rows[0]]
    neg_count = own_negs.shape[0]
    query_total = queries.shape[0]
    cand_total = neg_count * group_count
    targets_pos = positive_cand[0][:, None]
    all_negs = lax.all_gather(own_negs, "group", axis=0, tiled=True)
    scores = score_factor * jnp.dot(queries, all_negs.T, preferred_element_type=jnp.float32)
    positive = targets_pos == jnp.arange(cand_total, dtype=jnp.int32)[None, :]
    dscore = score_grads(scores, positive, cand_total, query_total)
    query_grad = score_factor * jnp.dot(dscore, all_negs, preferred_element_type=jnp.float32)
    neg_grad = lax.psum_scatter(
        (score_factor * transpose_dot(dscore, queries)).astype(jnp.bfloat16),
        "group",
        scatter_dimension=0,
        tiled=True,
    ).astype(jnp.float32)
    emb_grad = jnp.zeros((node_count, width), jnp.float32)
    emb_grad = emb_grad.at[query_rows[0]].add(query_grad)
    emb_grad = emb_grad.at[negative_rows[0]].add(neg_grad)
    inner = jnp.mean(pre * emb_grad, axis=-1, keepdims=True)
    pre_grad = (scale * emb_grad - pre * scale * scale * scale * inner).astype(jnp.bfloat16)
    stacked = jnp.concatenate([features, aggregate], axis=1)
    shard = lax.psum_scatter(
        transpose_dot(stacked, pre_grad), "dom", scatter_dimension=0, tiled=True
    )
    summed = lax.psum(shard.astype(jnp.bfloat16), "group")
    return (embeds, summed)


def solution(mesh):
    placed = (
        P(("group", "dom"), None),
        P(("group", "dom"), None, None),
        P(("group", "dom"), None, None, None, None),
        P(("group", "dom"), None, None),
        P(("group", "dom"), None),
        P(("group", "dom"), None, None),
        P(("group", "dom"), None),
        P(("group", "dom"), None),
        P(("group", "dom"), None),
        P(),
        P(),
    )
    return jax.shard_map(
        on_device,
        mesh=mesh,
        in_specs=placed,
        out_specs=(P(("group", "dom"), None), P("dom", None)),
        check_vma=False,
    )
```

profile of v0, /device:TPU:0, one launch (start us, length us, event | category | flops | bytes accessed | tf_op | source)
XLA Modules:
  0.0 157.0 jit_solution(12821754926774188139)
XLA Ops:
  7.2 0.0 copy-start
  7.2 0.0 copy-start.2
  7.2 1.4 compare_convert_fusion
  8.6 7.4 %all-to-all-start.1 = ((bf16[16,1,16]{2,1,0:T(2,128)(2,1)}), bf16[16,1,16]{2,1,0:T(2,128)(2,1)S(1)}, u32[]{:S(2)}, u32[]{:S(2)}) async-start(bf16[16,1,16]{2,1,0:T(2,128)(2,1)} %compare_convert_fusion), calls=%async_computation.1 | async-start | bytes 16384 | tf_op jit(solution)/shard_map/all_to_all | solution.py:54
  16.0 0.7 fusion.17
  16.7 0.7 compare_select_fusion.3
  17.4 0.1 reshape.231
  17.4 0.8 reshape_squeeze.3
  18.2 1.1 convert_reduce_fusion
  19.3 0.7 compare_select_fusion.1
  20.0 0.7 compare_select_fusion
  20.7 0.1 reshape.239
  20.8 1.4 fusion.19
  22.3 0.0 copy-start.3
  22.3 1.9 %gather_fusion.1 = bf16[256,512]{1,0:T(8,128)(2,1)} fusion(bf16[256,512]{1,0:T(8,128)(2,1)S(1)} %copy-done.2, s32[1024]{0:T(1024)S(1)} %pad_clamp_fusion.2), kind=kCustom, calls=%fused_computation.1 | custom fusion | bytes 525312 | tf_op jit(solution)/shard_map/gather | solution.py:48
  24.1 0.6 gather_fusion
  24.8 6.0 %all-to-all-start = ((bf16[16,16,512]{2,1,0:T(8,128)(2,1)}), bf16[16,16,512]{2,1,0:T(8,128)(2,1)S(1)}, u32[]{:S(2)}, u32[]{:S(2)}) async-start(bf16[16,16,512]{2,1,0:T(8,128)(2,1)} %bitcast.10), calls=%async_computation | async-start | bytes 524288 | tf_op jit(solution)/shard_map/all_to_all | solution.py:53
  30.8 0.0 reduce-scatter.3.cloned.1.call-start
  30.9 0.3 fusion.9
  31.2 0.1 reshape.273
  31.3 2.3 %scatter_fusion.1 = f32[256]{0:T(256)S(1)} fusion(f32[256]{0:T(256)S(1)} %add_bitcast_fusion, s32[256]{0:T(256)S(1)} %bitcast.51, f32[256]{0:T(256)S(1)} %reshape.273), kind=kCustom, calls=%fused_computation.5 | custom fusion | flops 256 | bytes 4096 | tf_op jit(solution)/shard_map/scatter-add | solution.py:66
  33.6 7.2 %all-to-all-done = bf16[16,16,512]{2,1,0:T(8,128)(2,1)S(1)} async-done(((bf16[16,16,512]{2,1,0:T(8,128)(2,1)}), bf16[16,16,512]{2,1,0:T(8,128)(2,1)S(1)}, u32[]{:S(2)}, u32[]{:S(2)}) %all-to-all-start) | async-done | bytes 262176 | tf_op jit(solution)/shard_map/all_to_all | solution.py:53
  40.8 0.1 convert_multiply_fusion
  40.9 2.3 %scatter_fusion = f32[256,512]{1,0:T(8,128)S(1)} fusion(f32[256,512]{1,0:T(8,128)S(1)} %bitcast.46, s32[256]{0:T(256)S(1)} %bitcast.52, f32[256,512]{1,0:T(8,128)S(1)} %bitcast.49), kind=kCustom, calls=%fused_computation.4 | custom fusion | flops 131072 | bytes 1573888 | tf_op jit(solution)/shard_map/scatter-add | solution.py:65
  43.2 0.1 divide_convert_fusion
  43.3 0.4 multiply_reduce_fusion.1
  43.7 0.1 multiply_convert_fusion
  43.9 0.0 copy-start.1
  43.9 0.6 gather_fusion.3
  44.5 4.6 %all-gather = bf16[64,512]{1,0:T(8,128)(2,1)S(1)} all-gather(bf16[32,512]{1,0:T(8,128)(2,1)S(1)} %gather_fusion.3), channel_id=2, replica_groups=mesh['group'=2,'dom'=16] {'group'}, dimensions={0}, use_global_device_ids=true | all-gather | bytes 98304 | tf_op jit(solution)/shard_map/all_gather | solution.py:80
  49.1 2.0 %gather_fusion.2 = bf16[512,512]{1,0:T(8,128)(2,1)S(1)} fusion(bf16[256,512]{1,0:T(8,128)(2,1)S(1)} %multiply_convert_fusion, s32[1024]{0:T(1024)S(1)} %pad_clamp_fusion.1), kind=kCustom, calls=%fused_computation.2 | custom fusion | bytes 1050624 | tf_op jit(solution)/shard_map/gather | solution.py:74
  51.1 0.3 multiply_convert_fusion.1
  51.4 0.8 fusion.4
  52.3 0.0 reduce-scatter.3.cloned.1.call-update
  52.3 0.0 reduce-scatter.5.cloned.1.call-start
  52.3 0.3 convolution_multiply_fusion
  52.6 3.7 %scatter_custom_fusion.2 = f32[256,512]{1,0:T(8,128)S(1)} fusion(s32[512]{0:T(512)S(1)} %bitcast.54, f32[512,512]{1,0:T(8,128)S(1)} %convolution_multiply_fusion, f32[]{:T(128)} %constant.14.clone.1), kind=kCustom, calls=%fused_computation.31 | custom fusion | flops 262144 | bytes 524292 | tf_op jit(solution)/shard_map/scatter-add | solution.py:92
  56.4 4.3 %reduce-scatter.3.cloned.1.call-done = bf16[32,512]{1,0:T(8,128)(2,1)} async-done(((bf16[64,512]{1,0:T(8,128)(2,1)}), bf16[32,512]{1,0:T(8,128)(2,1)}) %reduce-scatter.3.cloned.1.call-update) | async-done | bytes 32784 | tf_op jit(solution)/shard_map/reduce_scatter | solution.py:85
  60.6 1.2 scatter_custom_fusion.3
  61.9 0.1 multiply_reduce_fusion
  62.0 2.0 %fusion.5 = f32[1024,512]{1,0:T(8,128)} fusion(bf16[256,512]{1,0:T(8,128)(2,1)S(1)} %divide_convert_fusion, bf16[256,512]{1,0:T(8,128)(2,1)S(1)} %copy-done.2, f32[256,512]{1,0:T(8,128)S(1)} %scatter_custom_fusion.3, f32[256,512]{1,0:T(8,128)S(1)} %get-tuple-element.3, f32[256]{0:T(256)S(1)} %broadcast_multiply_fusion, f32[256]{0:T(256)S(1)} %add_rsqrt_fusion), kind=kOutput, calls=%fused_computation.17 | convolution fusion | flops 270401536 | bytes 3672064 | tf_op jit(solution)/shard_map/dot_general | solution.py:21
  64.0 0.0 reduce-scatter.5.cloned.1.call-update
  64.0 0.0 all-reduce.2.cloned.1.call-start
  64.0 62.2 %reduce-scatter.5.cloned.1.call-done = f32[64,512]{1,0:T(8,128)} async-done(((f32[1024,512]{1,0:T(8,128)}), f32[64,512]{1,0:T(8,128)}) %reduce-scatter.5.cloned.1.call-update) | async-done | bytes 131088 | tf_op jit(solution)/shard_map/reduce_scatter | solution.py:97
  126.2 1.5 convert_element_type.66
  127.8 0.0 all-reduce.2.cloned.1.call-update
  127.8 21.2 %all-reduce.2.cloned.1.call-done = bf16[64,512]{1,0:T(8,128)(2,1)} async-done(((bf16[64,512]{1,0:T(8,128)(2,1)}), bf16[64,512]{1,0:T(8,128)(2,1)}) %all-reduce.2.cloned.1.call-update) | async-done | bytes 65552 | tf_op jit(solution)/shard_map/psum | solution.py:100
  149.0 1.5 copy.18
  (17 shorter events, 0.1 us)
Async XLA Ops:
  7.2 36.2 %copy-start = (bf16[512,512]{1,0:T(8,128)(2,1)S(1)}, bf16[512,512]{1,0:T(8,128)(2,1)}, u32[]{:S(2)}) copy-start(bf16[512,512]{1,0:T(8,128)(2,1)} %param.21) | copy-start | bytes 1572868
  7.2 15.1 %copy-start.2 = (bf16[256,512]{1,0:T(8,128)(2,1)S(1)}, bf16[256,512]{1,0:T(8,128)(2,1)}, u32[]{:S(2)}) copy-start(bf16[256,512]{1,0:T(8,128)(2,1)} %param.11) | copy-start | bytes 786436
  8.6 16.1 %all-to-all-start.1 = ((bf16[16,1,16]{2,1,0:T(2,128)(2,1)}), bf16[16,1,16]{2,1,0:T(2,128)(2,1)S(1)}, u32[]{:S(2)}, u32[]{:S(2)}) async-start(bf16[16,1,16]{2,1,0:T(2,128)(2,1)} %compare_convert_fusion), calls=%async_computation.1 | async-start | bytes 16384 | tf_op jit(solution)/shard_map/all_to_all | solution.py:54
  22.3 8.6 %copy-start.3 = (bf16[1,2,4,128,128]{4,3,2,1,0:T(8,128)(2,1)S(1)}, bf16[1,2,4,128,128]{4,3,2,1,0:T(8,128)(2,1)}, u32[]{:S(2)}) copy-start(bf16[1,2,4,128,128]{4,3,2,1,0:T(8,128)(2,1)} %param.13) | copy-start | bytes 786436
  24.8 16.0 %all-to-all-start = ((bf16[16,16,512]{2,1,0:T(8,128)(2,1)}), bf16[16,16,512]{2,1,0:T(8,128)(2,1)S(1)}, u32[]{:S(2)}, u32[]{:S(2)}) async-start(bf16[16,16,512]{2,1,0:T(8,128)(2,1)} %bitcast.10), calls=%async_computation | async-start | bytes 524288 | tf_op jit(solution)/shard_map/all_to_all | solution.py:53
  30.8 29.9 %reduce-scatter.3.cloned.1.call-start = ((), (), s32[]{:S(2)}) async-start(), calls=%async_computation.4 | async-start | bytes 98304 | tf_op jit(solution)/shard_map/reduce_scatter | solution.py:85
  43.9 7.2 %copy-start.1 = (bf16[256,512]{1,0:T(8,128)(2,1)}, bf16[256,512]{1,0:T(8,128)(2,1)S(1)}, u32[]{:S(2)}) copy-start(bf16[256,512]{1,0:T(8,128)(2,1)S(1)} %multiply_convert_fusion) | copy-start | bytes 786436
  49.1 2.0 %copy-start.4 = (s32[1,512]{1,0:T(1,128)S(1)}, s32[1,512]{1,0:T(1,128)}, u32[]{:S(2)}) copy-start(s32[1,512]{1,0:T(1,128)} %param.18) | copy-start | bytes 6148
  52.3 74.0 %reduce-scatter.5.cloned.1.call-start = ((), (), s32[]{:S(2)}) async-start(), calls=%async_computation.5 | async-start | bytes 2228224 | tf_op jit(solution)/shard_map/reduce_scatter | solution.py:97
  64.0 85.0 %all-reduce.2.cloned.1.call-start = ((), (), s32[]{:S(2)}) async-start(), calls=%async_computation.6 | async-start | bytes 131072 | tf_op jit(solution)/shard_map/psum | solution.py:100
Sparse Core Ops, SparseCore 0:
  52.4 8.1 reduce-scatter.2
  64.4 61.8 reduce-scatter.4
  129.1 19.8 all-reduce.1
where the time goes:
time: 158 us; the launch traced here: 157 us
  waiting for transfers between devices  94.9 us (60%)
  other arithmetic  16.8 us (11%)
  between operations  14 us (9%)
  starting transfers between devices  13.6 us (9%)
  local copies, waits for them, and re-layouts  7.58 us (5%)
  matrix products  5.54 us (4%)
  blocking collectives  4.58 us (3%)
    reduce_scatter x1, waiting for transfers between devices, on_device(): lax.psum_scatter(transpose_dot(stacked, pre_grad), 'dom', scatter_dimensi...  62.2 us
    psum x1, waiting for transfers between devices, on_device(): summed = lax.psum(shard.astype(jnp.bfloat16), 'group')  21.2 us
    all_to_all x1, starting transfers between devices, on_device(): lax.all_to_all(flags, 'dom', split_axis=0, concat_axis=0, tiled=True)  7.41 us
    all_to_all x1, waiting for transfers between devices, on_device(): lax.all_to_all(outgoing, 'dom', split_axis=0, concat_axis=0, tiled=True)  7.18 us
    all_to_all x1, starting transfers between devices, on_device(): lax.all_to_all(outgoing, 'dom', split_axis=0, concat_axis=0, tiled=True)  6.02 us
    all_gather x1, blocking collectives, on_device(): all_negs = lax.all_gather(own_negs, 'group', axis=0, tiled=True)  4.58 us
    reduce_scatter x1, waiting for transfers between devices, on_device(): lax.psum_scatter((score_factor * transpose_dot(dscore, queries)).astype(j...  4.28 us
    scatter-add x1, other arithmetic, on_device(): emb_grad = emb_grad.at[query_rows[0]].add(query_grad)  3.71 us
  transfers between devices with their start and end apart: 5, of which 4 were waited for; matrix products, arithmetic and copies ran while one was open for 10% of the time, Pallas kernels for 0%

commit v1 on v0

v1 whole, which is shorter than its diff:
```python
import functools
import math

import jax
import jax.numpy as jnp
from jax import lax
from jax.experimental import pallas as pl
from jax.experimental.pallas import tpu as pltpu
from jax.sharding import PartitionSpec as P

LOSS_FACTOR = 64.0
EPSILON = 1e-05
DEAD = 256.0
DEAD_FLOOR = 128.0

F32 = jnp.float32
BF16 = jnp.bfloat16


def iota(shape, axis):
    return lax.broadcasted_iota(jnp.int32, shape, axis)


def dot(left, right, left_axis=1, right_axis=0):
    return lax.dot_general(
        left, right, (((left_axis,), (right_axis,)), ((), ())), preferred_element_type=F32
    )


def one_hot(condition):
    return jnp.where(condition, 1.0, 0.0).astype(BF16)


def slot_selector(peers, slots):
    shape = (peers * slots, peers)
    row, peer = iota(shape, 0), iota(shape, 1)
    mine = (row >= peer * slots) & (row < (peer + 1) * slots)
    first = jnp.sum(jnp.where(mine, (peer * slots).astype(F32), 0.0), axis=1, keepdims=True)
    return mine, row[:, :1].astype(F32) - first


def pack_kernel(rows_ref, count_ref, x_ref, out_ref):
    peers, slots = rows_ref.shape[1:]
    nodes = x_ref.shape[0]
    total = peers * slots
    mine, place = slot_selector(peers, slots)
    table = dot(one_hot(mine), rows_ref[0].astype(F32).astype(BF16))
    at_place = iota((total, slots), 1).astype(F32) == place
    row = jnp.sum(jnp.where(at_place, table, 0.0), axis=1, keepdims=True)
    count = jnp.sum(jnp.where(mine, count_ref[...].astype(F32), 0.0), axis=1, keepdims=True)
    pick = one_hot(iota((total, nodes), 1).astype(F32) == row)
    out = dot(pick, x_ref[...])
    out_ref[...] = jnp.where(place < count, out, DEAD).astype(BF16)


def local_kernel(
    columns_ref,
    group_ref,
    values_ref,
    x_ref,
    weight_self_ref,
    target_ref,
    query_ref,
    positive_ref,
    negative_ref,
    local_ref,
    degree_ref,
    self_ref,
    pair_ref,
    target_hot_ref,
    negative_hot_ref,
    x_negative_ref,
    x_turned_ref,
):
    row_blocks, tiles_row, tile = values_ref.shape[1:4]
    nodes = x_ref.shape[0]
    peers, slots = target_ref.shape[1:]
    negatives = negative_ref.shape[1]
    queries = query_ref.shape[1]
    candidates = pair_ref.shape[1]

    relative = positive_ref[...] - group_ref[0] * negatives
    relative = jnp.where(relative < 0, relative + candidates, relative)
    query_hot = one_hot(iota((nodes, queries), 0) == query_ref[...])
    positive_hot = one_hot(iota((candidates, queries), 0) == relative)
    pair_ref[...] = dot(query_hot, positive_hot, 1, 1)

    square = (negatives, negatives)
    negative = jnp.sum(
        jnp.where(iota(square, 0) == iota(square, 1), negative_ref[...].astype(F32), 0.0),
        axis=1,
        keepdims=True,
    )
    negative_hot = one_hot(iota((negatives, nodes), 1).astype(F32) == negative)
    negative_hot_ref[...] = negative_hot
    x_negative_ref[...] = dot(negative_hot, x_ref[...]).astype(BF16)

    ones = jnp.ones((tile, 128), BF16)
    for block in range(row_blocks):
        total = jnp.zeros((tile, x_ref.shape[1]), F32)
        weight = jnp.ones((tile, 128), F32)
        for t in range(tiles_row):
            first = pl.multiple_of(columns_ref[0, block, t] * tile, tile)
            values = values_ref[0, block, t]
            total += dot(values, x_ref[pl.ds(first, tile), :])
            weight += dot(values, ones)
        local_ref[block * tile : (block + 1) * tile, :] = total
        degree_ref[block * tile : (block + 1) * tile, :] = weight

    self_ref[...] = dot(x_ref[...], weight_self_ref[...])
    x_turned_ref[...] = x_ref[...].T.reshape(x_turned_ref.shape)

    total = peers * slots
    shape = (peers, total)
    peer, column = iota(shape, 0), iota(shape, 1)
    mine = (column >= peer * slots) & (column < (peer + 1) * slots)
    first = jnp.sum(jnp.where(mine, (peer * slots).astype(F32), 0.0), axis=0, keepdims=True)
    place = iota((1, total), 1).astype(F32) - first
    spread = one_hot(iota((slots, total), 0).astype(F32) == place)
    table = dot(target_ref[0].astype(F32).astype(BF16), spread)
    target = jnp.sum(jnp.where(mine, table, 0.0), axis=0, keepdims=True)
    target_hot_ref[...] = one_hot(iota((nodes, total), 0).astype(F32) == target)


def aggregate_kernel(
    received_ref, target_hot_ref, local_ref, degree_ref, negative_hot_ref, out_ref, negative_ref
):
    received = received_ref[...].astype(F32)
    live = received[:, :1] < DEAD_FLOOR
    weighted = jnp.where(live, received, 0.0).astype(BF16)
    flags = jnp.broadcast_to(jnp.where(live, 1.0, 0.0), (received.shape[0], 128)).astype(BF16)
    hot = target_hot_ref[...]
    degree = degree_ref[...] + dot(hot, flags)
    summed = local_ref[...] + dot(hot, weighted)
    width = summed.shape[1]
    for first in range(0, width, 128):
        out_ref[:, first : first + 128] = (summed[:, first : first + 128] / degree).astype(BF16)
    negative_ref[...] = dot(negative_hot_ref[...], out_ref[...]).astype(BF16)


def embed_kernel(
    self_ref, aggregate_ref, weight_neigh_ref, embeds_ref, exact_ref, scale_ref, turned_ref
):
    aggregate = aggregate_ref[...]
    pre = self_ref[...] + dot(aggregate, weight_neigh_ref[...])
    scale = lax.rsqrt(jnp.mean(pre * pre, axis=1, keepdims=True) + EPSILON)
    exact = pre * scale
    exact_ref[...] = exact
    embeds_ref[...] = exact.astype(BF16)
    scale_ref[...] = jnp.broadcast_to(scale, scale_ref.shape)
    turned_ref[...] = aggregate.T.reshape(turned_ref.shape)


def split_dot(left, right, left_axis):
    high = left.astype(BF16)
    low = (left - high.astype(F32)).astype(BF16)
    return dot(high, right, left_axis, 0) + dot(low, right, left_axis, 0)


def gradient_kernel(
    query_total,
    core_ref,
    x_cand_ref,
    aggregate_cand_ref,
    weight_self_ref,
    weight_neigh_ref,
    embeds_ref,
    exact_ref,
    scale_ref,
    pair_ref,
    x_turned_ref,
    aggregate_turned_ref,
    keep_ref,
    send_ref,
    x_cand_turned_ref,
    aggregate_cand_turned_ref,
):
    width = embeds_ref.shape[1]
    score_factor = 1.0 / math.sqrt(width)
    candidates = x_cand_ref.shape[0]

    x_cand, aggregate_cand = x_cand_ref[...], aggregate_cand_ref[...]
    pre = dot(x_cand, weight_self_ref[...]) + dot(aggregate_cand, weight_neigh_ref[...])
    scale_cand = lax.rsqrt(jnp.mean(pre * pre, axis=1, keepdims=True) + EPSILON)
    exact_cand = pre * scale_cand
    cand = exact_cand.astype(BF16)

    embeds = embeds_ref[...]
    scores = score_factor * dot(embeds, cand, 1, 1)
    sigma = jax.nn.sigmoid(scores)
    factor = LOSS_FACTOR / query_total
    at_positive = ((sigma - 1.0) * factor).astype(BF16).astype(F32)
    elsewhere = ((sigma / (candidates - 1.0)) * factor).astype(BF16).astype(F32)
    pair = pair_ref[...]
    count = jnp.sum(pair, axis=1, keepdims=True)
    grad = (count - pair) * elsewhere + pair * at_positive

    emb_grad = score_factor * split_dot(grad, cand, 1)
    cand_grad = score_factor * split_dot(grad, embeds, 0)

    def through_norm(given, exact, scale):
        inner = jnp.mean(exact * given, axis=1, keepdims=True)
        return (scale * (given - exact * inner)).astype(BF16)

    pre_grad = through_norm(emb_grad, exact_ref[...], scale_ref[:, :1])
    pre_grad_cand = through_norm(cand_grad, exact_cand, scale_cand)

    half, _, rows, _ = x_turned_ref.shape
    x_cand_turned_ref[...] = x_cand.T.reshape(half, 2, rows, candidates)
    aggregate_cand_turned_ref[...] = aggregate_cand.T.reshape(half, 2, rows, candidates)
    own = core_ref[0]
    parts = (
        (x_turned_ref, x_cand_turned_ref),
        (aggregate_turned_ref, aggregate_cand_turned_ref),
    )
    for ref, core in ((send_ref, 1 - own), (keep_ref, own)):
        for part, (turned_ref, cand_turned_ref) in enumerate(parts):
            left = turned_ref[:, core].reshape(half * rows, turned_ref.shape[3])
            left_cand = cand_turned_ref[:, core].reshape(half * rows, candidates)
            block = dot(left, pre_grad) + dot(left_cand, pre_grad_cand)
            ref[part * half : (part + 1) * half] = block.reshape(half, rows, width).astype(BF16)


VMEM = pl.BlockSpec(memory_space=pltpu.VMEM)
SMEM = pl.BlockSpec(memory_space=pltpu.SMEM)


def call(kernel, name, outs, args, scalars=0, flops=0, scratch=()):
    shapes = [jax.ShapeDtypeStruct(shape, kind) for shape, kind in outs]
    moved = sum(math.prod(a.shape) * a.dtype.itemsize for a in list(args) + shapes)
    return pl.pallas_call(
        kernel,
        name=name,
        out_shape=shapes,
        in_specs=[SMEM] * scalars + [VMEM] * (len(args) - scalars),
        out_specs=[VMEM] * len(outs),
        scratch_shapes=[pltpu.VMEM(shape, kind) for shape, kind in scratch],
        cost_estimate=pl.CostEstimate(flops=flops, bytes_accessed=moved, transcendentals=0),
    )(*args)


def on_device(
    features,
    tile_columns,
    tile_values,
    send_rows,
    send_count,
    ghost_target,
    query_rows,
    positive_cand,
    negative_rows,
    weight_self,
    weight_neigh,
):
    nodes, width = features.shape
    peers, slots = send_rows.shape[1:]
    total = peers * slots
    negatives = negative_rows.shape[1]
    groups = lax.axis_size("group")
    candidates = negatives * groups
    chips = peers // 2
    rows = 2 * width // peers
    half = chips // 2
    group = lax.axis_index("group").astype(jnp.int32).reshape(1)
    core = (lax.axis_index("dom") % 2).astype(jnp.int32).reshape(1)

    (outgoing,) = call(
        pack_kernel,
        "pack",
        [((total, width), BF16)],
        [send_rows, send_count, features],
        flops=2 * total * nodes * width,
    )
    received = lax.all_to_all(
        outgoing.reshape(peers, slots, width), "dom", split_axis=0, concat_axis=0, tiled=True
    ).reshape(total, width)

    local, degree, own_pre, pair, target_hot, negative_hot, x_negative, x_turned = call(
        local_kernel,
        "local",
        [
            ((nodes, width), F32),
            ((nodes, 128), F32),
            ((nodes, width), F32),
            ((nodes, candidates), F32),
            ((nodes, total), BF16),
            ((negatives, nodes), BF16),
            ((negatives, width), BF16),
            ((half, 2, rows, nodes), BF16),
        ],
        [
            tile_columns,
            group,
            tile_values,
            features,
            weight_self,
            ghost_target,
            query_rows,
            positive_cand,
            negative_rows,
        ],
        scalars=2,
        flops=2 * nodes * width * (width + tile_values.shape[2] * tile_values.shape[3]),
    )

    def gathered(own):
        blocks = [own]
        for k in range(1, groups):
            pairs = [((g + k) % groups, g) for g in range(groups)]
            blocks.append(lax.ppermute(own, "group", pairs))
        return jnp.concatenate(blocks, axis=0)

    x_cand = gathered(x_negative)
    aggregate, aggregate_negative = call(
        aggregate_kernel,
        "aggregate",
        [((nodes, width), BF16), ((negatives, width), BF16)],
        [received, target_hot, local, degree, negative_hot],
        flops=2 * nodes * total * width,
    )
    aggregate_cand = gathered(aggregate_negative)
    embeds, exact, scale, aggregate_turned = call(
        embed_kernel,
        "embed",
        [
            ((nodes, width), BF16),
            ((nodes, width), F32),
            ((nodes, 128), F32),
            ((half, 2, rows, nodes), BF16),
        ],
        [own_pre, aggregate, weight_neigh],
        flops=2 * nodes * width * width,
    )
    keep, send = call(
        functools.partial(gradient_kernel, query_rows.shape[1]),
        "gradient",
        [((chips, rows, width), BF16)] * 2,
        [
            core,
            x_cand,
            aggregate_cand,
            weight_self,
            weight_neigh,
            embeds,
            exact,
            scale,
            pair,
            x_turned,
            aggregate_turned,
        ],
        scalars=1,
        flops=4 * nodes * width * width,
        scratch=[((half, 2, rows, candidates), BF16)] * 2,
    )

    swap = [(i, i ^ 1) for i in range(peers)]
    chip_sum = (keep.astype(F32) + lax.ppermute(send, "dom", swap).astype(F32)).astype(BF16)
    same_core = [[c + 2 * chip for chip in range(chips)] for c in range(2)]
    parts = lax.all_to_all(
        chip_sum,
        "dom",
        split_axis=0,
        concat_axis=0,
        axis_index_groups=same_core,
        tiled=True,
    )
    shard = jnp.sum(parts.astype(F32), axis=0).astype(BF16)
    if groups == 2:
        other = lax.ppermute(shard, "group", [(0, 1), (1, 0)])
        summed = (shard.astype(F32) + other.astype(F32)).astype(BF16)
    else:
        summed = lax.psum(shard, "group")
    return (embeds, summed)


def solution(mesh):
    placed = (
        P(("group", "dom"), None),
        P(("group", "dom"), None, None),
        P(("group", "dom"), None, None, None, None),
        P(("group", "dom"), None, None),
        P(("group", "dom"), None),
        P(("group", "dom"), None, None),
        P(("group", "dom"), None),
        P(("group", "dom"), None),
        P(("group", "dom"), None),
        P(),
        P(),
    )
    return jax.shard_map(
        on_device,
        mesh=mesh,
        in_specs=placed,
        out_specs=(P(("group", "dom"), None), P("dom", None)),
        check_vma=False,
    )
```

time: 158 us -> 59.3 us (0.38)
  waiting for transfers between devices: 94.9 us -> 11.1 us
  Pallas kernels: 0 us -> 14.5 us
  other arithmetic: 16.8 us -> 3.18 us
  between operations: 14 us -> 0.67 us
  blocking collectives: 4.58 us -> 17.5 us
  local copies, waits for them, and re-layouts: 7.58 us -> 0.71 us
  matrix products: 5.54 us -> 0 us
  starting transfers between devices: 13.6 us -> 11.3 us
    reduce_scatter x2 -> x0, waiting for transfers between devices: 66.5 us -> none  [the longest x1 62.2 us: on_device(): lax.psum_scatter(transpose_dot(stacked, pre_grad), 'dom', scatter_dimensi...]
    psum x1 -> x0, waiting for transfers between devices: 21.2 us -> none  [on_device(): summed = lax.psum(shard.astype(jnp.bfloat16), 'group')]
    all_to_all x0 -> x1, blocking collectives: none -> 17.5 us  [on_device(): lax.all_to_all(chip_sum, 'dom', split_axis=0, concat_axis=0, axis_index_g...]
    pallas_call x0 -> x5, Pallas kernels: none -> 14.5 us  [call(): pl.pallas_call(kernel, name=name, out_shape=shapes, in_specs=[SMEM] * sca...]
    scatter-add x4 -> x0, other arithmetic: 9.56 us -> none  [the longest x1 3.71 us: on_device(): emb_grad = emb_grad.at[query_rows[0]].add(query_grad)]
    all_to_all x2 -> x1, starting transfers between devices: 13.4 us -> 7.41 us  [on_device(): lax.all_to_all(outgoing.reshape(peers, slots, width), 'dom', split_axis=0...]
    ppermute x0 -> x4, waiting for transfers between devices: none -> 5.62 us  [the longest x1 3.49 us: on_device(): other = lax.ppermute(shard, 'group', [(0, 1), (1, 0)])]
    dot_general x7 -> x0, matrix products: 5.54 us -> none  [the longest x2 2.8 us: transpose_dot(): lax.dot_general(left, right, (((0,), (0,)), ((), ())), preferred_element_...]
  transfers between devices with their start and end apart: 5 -> 5, of which waited for: 4 -> 3; matrix products, arithmetic and copies ran while one was open for 10% -> 1% of each run, Pallas kernels for 0% -> 14%
where the time goes in v1:
time: 59.3 us; the launch traced here: 58.9 us
  blocking collectives  17.5 us (30%)
  Pallas kernels  14.5 us (24%)
  starting transfers between devices  11.3 us (19%)
  waiting for transfers between devices  11.1 us (19%)
  other arithmetic  3.18 us (5%)
  local copies, waits for them, and re-layouts  0.71 us (1%)
  between operations  0.67 us (1%)
    all_to_all x1, blocking collectives, on_device(): lax.all_to_all(chip_sum, 'dom', split_axis=0, concat_axis=0, axis_index_g...  17.5 us
    pallas_call x5, Pallas kernels, call(): pl.pallas_call(kernel, name=name, out_shape=shapes, in_specs=[SMEM] * sca...  14.5 us
    all_to_all x1, starting transfers between devices, on_device(): lax.all_to_all(outgoing.reshape(peers, slots, width), 'dom', split_axis=0...  7.41 us
    all_to_all x1, waiting for transfers between devices, on_device(): lax.all_to_all(outgoing.reshape(peers, slots, width), 'dom', split_axis=0...  5.48 us
    ppermute x1, waiting for transfers between devices, on_device(): other = lax.ppermute(shard, 'group', [(0, 1), (1, 0)])  3.49 us
    ppermute x2, starting transfers between devices, gathered(): blocks.append(lax.ppermute(own, 'group', pairs))  3.03 us
    ppermute x1, waiting for transfers between devices, on_device(): lax.ppermute(send, 'dom', swap).astype(F32)  2.12 us
    concatenate x2, other arithmetic, gathered(): return jnp.concatenate(blocks, axis=0)  1.27 us
  transfers between devices with their start and end apart: 5, of which 3 were waited for; matrix products, arithmetic and copies ran while one was open for 1% of the time, Pallas kernels for 14%

profile of v1, /device:TPU:0, one launch (start us, length us, event | category | flops | bytes accessed | tf_op | source)
XLA Modules:
  0.0 58.9 jit_solution(9826431643736579475)
XLA Ops:
  0.6 2.1 %pack.1 = bf16[256,512]{1,0:T(8,128)(2,1)} custom-call(s32[1,16,16]{2,1,0:T(8,128)} %rows_ref.1, s32[1,16]{1,0:T(1,128)} %count_ref.1, bf16[256,512]{1,0:T(8,128)(2,1)} %x_ref.3), custom_call_target="tpu_custom_call" | custom-call | flops 67108864 | bytes 525376 | tf_op jit(solution)/shard_map/pack/pallas_call | solution.py:231
  2.7 7.4 %all-to-all-start = ((bf16[16,16,512]{2,1,0:T(8,128)(2,1)}), bf16[16,16,512]{2,1,0:T(8,128)(2,1)S(1)}, u32[]{:S(2)}, u32[]{:S(2)}) async-start(bf16[16,16,512]{2,1,0:T(8,128)(2,1)} %bitcast.4), calls=%async_computation | async-start | bytes 524288 | tf_op jit(solution)/shard_map/all_to_all | solution.py:274
  10.2 3.0 %local.1 = (f32[256,512]{1,0:T(8,128)}, f32[256,128]{1,0:T(8,128)}, f32[256,512]{1,0:T(8,128)}, f32[256,64]{1,0:T(8,128)}, bf16[256,256]{1,0:T(8,128)(2,1)}, /*i...) custom-call(s32[1,2,4]{2,1,0:T(2,128)} %columns_ref.1, s32[1]{0:T(128)} %bitcast.group_ref, ...), custom_call_target="tpu_custom_call" | custom-call | flops 268435456 | bytes 2741412 | tf_op jit(solution)/shard_map/local/pallas_call | solution.py:231
  13.2 1.5 %collective-permute-start = (bf16[32,512]{1,0:T(8,128)(2,1)}, bf16[32,512]{1,0:T(8,128)(2,1)S(1)}, u32[]{:S(2)}, u32[]{:S(2)}) collective-permute-start(bf16[32,512]{1,0:T(8,128)(2,1)} %get-tuple-element.25), channel_id=1, source_target_pairs={{16,0},{0,16},{17,1},{1,17},{18,2},{2,18},{19,3},{3,19},{20,4},{4,... | collective-permute-start | bytes 98312 | tf_op jit(solution)/shard_map/ppermute | solution.py:310
  14.7 5.5 %all-to-all-done = bf16[16,16,512]{2,1,0:T(8,128)(2,1)S(1)} async-done(((bf16[16,16,512]{2,1,0:T(8,128)(2,1)}), bf16[16,16,512]{2,1,0:T(8,128)(2,1)S(1)}, u32[]{:S(2)}, u32[]{:S(2)}) %all-to-all-start) | async-done | bytes 262176 | tf_op jit(solution)/shard_map/all_to_all | solution.py:274
  20.2 0.0 copy-start
  20.2 0.7 %copy-done = bf16[16,16,512]{2,1,0:T(8,128)(2,1)} copy-done((bf16[16,16,512]{2,1,0:T(8,128)(2,1)}, bf16[16,16,512]{2,1,0:T(8,128)(2,1)S(1)}, u32[]{:S(2)}) %copy-start) | copy-done | bytes 262168
  20.9 0.0 copy-start.1
  20.9 2.4 %aggregate.1 = (bf16[256,512]{1,0:T(8,128)(2,1)}, bf16[32,512]{1,0:T(8,128)(2,1)}) custom-call(bf16[256,512]{1,0:T(8,128)(2,1)} %bitcast.5, bf16[256,256]{1,0:T(8,128)(2,1)} %get-tuple-element.19.target_hot_ref, f32[256,512]{1,0:T(8,128)} %get-tuple-element.20.local_ref, f32[256,128]{1,0:T(8,128)} %get-tuple-element.21.degree_ref, ...), custom_call_target="tpu_custom_call" | custom-call | flops 67108864 | bytes 1359872 | tf_op jit(solution)/shard_map/aggregate/pallas_call | solution.py:231
  23.3 1.5 %collective-permute-start.1 = (bf16[32,512]{1,0:T(8,128)(2,1)}, bf16[32,512]{1,0:T(8,128)(2,1)S(1)}, u32[]{:S(2)}, u32[]{:S(2)}) collective-permute-start(bf16[32,512]{1,0:T(8,128)(2,1)} %get-tuple-element.26), channel_id=1, source_target_pairs={{16,0},{0,16},{17,1},{1,17},{18,2},{2,18},{19,3},{3,19},{20,4},{4,... | collective-permute-start | bytes 98312 | tf_op jit(solution)/shard_map/ppermute | solution.py:310
  24.8 0.0 collective-permute-done
  24.8 0.0 copy-done.1
  24.8 0.6 %pad_maximum_fusion.x_cand_ref = bf16[64,512]{1,0:T(8,128)(2,1)} fusion(bf16[32,512]{1,0:T(8,128)(2,1)S(1)} %collective-permute-done, bf16[32,512]{1,0:T(8,128)(2,1)S(1)} %copy-done.1), kind=kLoop, calls=%fused_computation.2 | loop fusion | flops 131072 | bytes 131072 | tf_op jit(solution)/shard_map/concatenate | solution.py:311
  25.4 0.0 copy-start.2
  25.4 2.7 %embed.1 = (bf16[256,512]{1,0:T(8,128)(2,1)}, f32[256,512]{1,0:T(8,128)}, f32[256,128]{1,0:T(8,128)}, bf16[4,2,64,256]{3,2,1,0:T(8,128)(2,1)}) custom-call(f32[256,512]{1,0:T(8,128)} %get-tuple-element.18.self_ref, bf16[256,512]{1,0:T(8,128)(2,1)} %get-tuple-element.23.aggregate_ref, bf16[512,512]{1,0:T(8,128)(2,1)} %weight_neigh_ref.3), custom_call_target="tpu_custom_call" | custom-call | flops 134217728 | bytes 2490368 | tf_op jit(solution)/shard_map/embed/pallas_call | solution.py:231
  28.1 0.0 collective-permute-done.1
  28.1 0.0 copy-done.2
  28.1 0.6 %pad_maximum_fusion.1.aggregate_cand_ref = bf16[64,512]{1,0:T(8,128)(2,1)} fusion(bf16[32,512]{1,0:T(8,128)(2,1)S(1)} %collective-permute-done.1, bf16[32,512]{1,0:T(8,128)(2,1)S(1)} %copy-done.2), kind=kLoop, calls=%fused_computation.3 | loop fusion | flops 131072 | bytes 131072 | tf_op jit(solution)/shard_map/concatenate | solution.py:311
  28.8 4.3 %gradient.1 = (bf16[8,64,512]{2,1,0:T(8,128)(2,1)}, bf16[8,64,512]{2,1,0:T(8,128)(2,1)}) custom-call(s32[1]{0:T(128)} %bitcast.3.core_ref, bf16[64,512]{1,0:T(8,128)(2,1)} %pad_maximum_fusion.x_cand_ref, bf16[64,512]{1,0:T(8,128)(2,1)} %pad_maximum_fusion.1.aggregate_cand_ref, bf16[512,512]{1,0:T(8,128)(2,1)} %weight_self_ref.3, ...), custom_call_target="tpu_custom_call" | custom-call | flops 268435456 | bytes 3735556 | tf_op jit(solution)/shard_map/gradient/pallas_call | solution.py:231
  33.1 0.0 collective-permute-start.2
  33.1 2.1 %collective-permute-done.2 = bf16[8,64,512]{2,1,0:T(8,128)(2,1)S(1)} collective-permute-done((bf16[8,64,512]{2,1,0:T(8,128)(2,1)}, bf16[8,64,512]{2,1,0:T(8,128)(2,1)S(1)}, u32[]{:S(2)}, u32[]{:S(2)}) %collective-permute-start.2) | collective-permute-done | bytes 524320 | tf_op jit(solution)/shard_map/ppermute | solution.py:357
  35.2 1.2 %add_convert_fusion = bf16[8,64,512]{2,1,0:T(8,128)(2,1)S(1)} fusion(bf16[8,64,512]{2,1,0:T(8,128)(2,1)S(1)} %collective-permute-done.2, bf16[8,64,512]{2,1,0:T(8,128)(2,1)} %get-tuple-element.32), kind=kLoop, calls=%fused_computation | loop fusion | flops 1048576 | bytes 1572864 | tf_op jit(solution)/shard_map/convert_element_type | solution.py:357
  36.4 17.5 %all_to_all.10 = bf16[8,64,512]{2,1,0:T(8,128)(2,1)S(1)} all-to-all(bf16[8,64,512]{2,1,0:T(8,128)(2,1)S(1)} %add_convert_fusion), channel_id=1, replica_groups={{0,2,4,6,8,10,12,14},{1,3,5,7,9,11,13,15},{16,18,20,22,24,26,28,30},{17..., dimensions={0} | all-to-all | bytes 1048576 | tf_op jit(solution)/shard_map/all_to_all | solution.py:359
  53.8 0.1 reduce_sum.12
  53.9 0.8 %collective-permute-start.3 = (bf16[64,512]{1,0:T(8,128)(2,1)S(1)}, bf16[64,512]{1,0:T(8,128)(2,1)S(1)}, u32[]{:S(2)}, u32[]{:S(2)}) collective-permute-start(bf16[64,512]{1,0:T(8,128)(2,1)S(1)} %reduce_sum.12), channel_id=1, source_target_pairs={{0,16},{16,0},{1,17},{17,1},{2,18},{18,2},{3,19},{19,3},{4,20},{20... | collective-permute-start | bytes 196616 | tf_op jit(solution)/shard_map/ppermute | solution.py:369
  54.8 3.5 %collective-permute-done.3 = bf16[64,512]{1,0:T(8,128)(2,1)S(1)} collective-permute-done((bf16[64,512]{1,0:T(8,128)(2,1)S(1)}, bf16[64,512]{1,0:T(8,128)(2,1)S(1)}, u32[]{:S(2)}, u32[]{:S(2)}) %collective-permute-start.3) | collective-permute-done | bytes 65568 | tf_op jit(solution)/shard_map/ppermute | solution.py:369
  58.2 0.6 %add_convert_fusion.1 = bf16[64,512]{1,0:T(8,128)(2,1)} fusion(bf16[64,512]{1,0:T(8,128)(2,1)S(1)} %collective-permute-done.3, bf16[64,512]{1,0:T(8,128)(2,1)S(1)} %reduce_sum.12), kind=kLoop, calls=%fused_computation.1 | loop fusion | flops 131072 | bytes 196608 | tf_op jit(solution)/shard_map/convert_element_type | solution.py:370
Async XLA Ops:
  2.7 17.4 %all-to-all-start = ((bf16[16,16,512]{2,1,0:T(8,128)(2,1)}), bf16[16,16,512]{2,1,0:T(8,128)(2,1)S(1)}, u32[]{:S(2)}, u32[]{:S(2)}) async-start(bf16[16,16,512]{2,1,0:T(8,128)(2,1)} %bitcast.4), calls=%async_computation | async-start | bytes 524288 | tf_op jit(solution)/shard_map/all_to_all | solution.py:274
  13.2 11.6 %collective-permute-start = (bf16[32,512]{1,0:T(8,128)(2,1)}, bf16[32,512]{1,0:T(8,128)(2,1)S(1)}, u32[]{:S(2)}, u32[]{:S(2)}) collective-permute-start(bf16[32,512]{1,0:T(8,128)(2,1)} %get-tuple-element.25), channel_id=1, source_target_pairs={{16,0},{0,16},{17,1},{1,17},{18,2},{2,18},{19,3},{3,19},{20,4},{4,... | collective-permute-start | bytes 98312 | tf_op jit(solution)/shard_map/ppermute | solution.py:310
  20.2 0.7 %copy-start = (bf16[16,16,512]{2,1,0:T(8,128)(2,1)}, bf16[16,16,512]{2,1,0:T(8,128)(2,1)S(1)}, u32[]{:S(2)}) copy-start(bf16[16,16,512]{2,1,0:T(8,128)(2,1)S(1)} %all-to-all-done) | copy-start | bytes 786436
  20.9 3.9 %copy-start.1 = (bf16[32,512]{1,0:T(8,128)(2,1)S(1)}, bf16[32,512]{1,0:T(8,128)(2,1)}, u32[]{:S(2)}) copy-start(bf16[32,512]{1,0:T(8,128)(2,1)} %get-tuple-element.25) | copy-start | bytes 98308
  23.3 4.8 %collective-permute-start.1 = (bf16[32,512]{1,0:T(8,128)(2,1)}, bf16[32,512]{1,0:T(8,128)(2,1)S(1)}, u32[]{:S(2)}, u32[]{:S(2)}) collective-permute-start(bf16[32,512]{1,0:T(8,128)(2,1)} %get-tuple-element.26), channel_id=1, source_target_pairs={{16,0},{0,16},{17,1},{1,17},{18,2},{2,18},{19,3},{3,19},{20,4},{4,... | collective-permute-start | bytes 98312 | tf_op jit(solution)/shard_map/ppermute | solution.py:310
  25.4 2.7 %copy-start.2 = (bf16[32,512]{1,0:T(8,128)(2,1)S(1)}, bf16[32,512]{1,0:T(8,128)(2,1)}, u32[]{:S(2)}) copy-start(bf16[32,512]{1,0:T(8,128)(2,1)} %get-tuple-element.26) | copy-start | bytes 98308
  33.1 2.1 %collective-permute-start.2 = (bf16[8,64,512]{2,1,0:T(8,128)(2,1)}, bf16[8,64,512]{2,1,0:T(8,128)(2,1)S(1)}, u32[]{:S(2)}, u32[]{:S(2)}) collective-permute-start(bf16[8,64,512]{2,1,0:T(8,128)(2,1)} %get-tuple-element.33), channel_id=1, source_target_pairs={{0,1},{1,0},{2,3},{3,2},{4,5},{5,4},{6,7},{7,6},{8,9},{9,8},{10,11... | collective-permute-start | bytes 1572872 | tf_op jit(solution)/shard_map/ppermute | solution.py:357
  53.9 4.3 %collective-permute-start.3 = (bf16[64,512]{1,0:T(8,128)(2,1)S(1)}, bf16[64,512]{1,0:T(8,128)(2,1)S(1)}, u32[]{:S(2)}, u32[]{:S(2)}) collective-permute-start(bf16[64,512]{1,0:T(8,128)(2,1)S(1)} %reduce_sum.12), channel_id=1, source_target_pairs={{0,16},{16,0},{1,17},{17,1},{2,18},{18,2},{3,19},{19,3},{4,20},{20... | collective-permute-start | bytes 196616 | tf_op jit(solution)/shard_map/ppermute | solution.py:369

commit v2 on v1

v2 whole, which is shorter than its diff:
```python
import functools
import math

import jax
import jax.numpy as jnp
from jax import lax
from jax.experimental import pallas as pl
from jax.experimental.pallas import tpu as pltpu
from jax.sharding import PartitionSpec as P

LOSS_FACTOR = 64.0
EPSILON = 1e-05
DEAD = 256.0
DEAD_FLOOR = 128.0

F32 = jnp.float32
BF16 = jnp.bfloat16


def iota(shape, axis):
    return lax.broadcasted_iota(jnp.int32, shape, axis)


def dot(left, right, left_axis=1, right_axis=0):
    return lax.dot_general(
        left, right, (((left_axis,), (right_axis,)), ((), ())), preferred_element_type=F32
    )


def one_hot(condition):
    return jnp.where(condition, 1.0, 0.0).astype(BF16)


def pack_kernel(core_ref, rows_hbm, count_hbm, x_hbm, keep_ref, send_ref, rows_ref, count_ref, x_ref, sems):
    copies = [
        pltpu.make_async_copy(source, target, sems.at[n])
        for n, (source, target) in enumerate(
            ((rows_hbm, rows_ref), (count_hbm, count_ref), (x_hbm, x_ref))
        )
    ]
    for copy in copies:
        copy.start()
    peers, slots = rows_ref.shape[1:]
    nodes = x_ref.shape[0]
    half = peers // 2 * slots
    shape = (half, peers)
    row, peer = iota(shape, 0), iota(shape, 1)
    first = (peer >> 1) * slots
    chip = (row >= first) & (row < first + slots)
    copies[0].wait()
    copies[1].wait()
    rows = rows_ref[0].astype(F32).astype(BF16)
    counts = count_ref[...].astype(F32)
    picks = []
    for core in (core_ref[0], 1 - core_ref[0]):
        mine = chip & ((peer & 1) == core)
        start = jnp.sum(jnp.where(mine, first.astype(F32), 0.0), axis=1, keepdims=True)
        place = row[:, :1].astype(F32) - start
        at_place = iota((half, slots), 1).astype(F32) == place
        table = dot(one_hot(mine), rows)
        index = jnp.sum(jnp.where(at_place, table, 0.0), axis=1, keepdims=True)
        count = jnp.sum(jnp.where(mine, counts, 0.0), axis=1, keepdims=True)
        pick = one_hot(iota((half, nodes), 1).astype(F32) == index)
        picks.append((pick, place < count))
    copies[2].wait()
    x = x_ref[...]
    for (pick, live), ref in reversed(list(zip(picks, (keep_ref, send_ref)))):
        ref[...] = jnp.where(live, dot(pick, x), DEAD).astype(BF16).reshape(ref.shape)


def local_kernel(
    columns_ref,
    place_ref,
    values_ref,
    x_ref,
    weight_self_ref,
    target_ref,
    query_ref,
    positive_ref,
    negative_ref,
    local_ref,
    degree_ref,
    self_ref,
    pair_ref,
    target_hot_ref,
    negative_hot_ref,
    x_negative_ref,
    x_turned_ref,
):
    row_blocks, tiles_row, tile = values_ref.shape[1:4]
    nodes = x_ref.shape[0]
    peers, slots = target_ref.shape[1:]
    negatives = negative_ref.shape[1]
    queries = query_ref.shape[1]
    candidates = pair_ref.shape[1]

    relative = positive_ref[...] - place_ref[0] * negatives
    relative = jnp.where(relative < 0, relative + candidates, relative)
    query_hot = one_hot(iota((nodes, queries), 0) == query_ref[...])
    positive_hot = one_hot(iota((candidates, queries), 0) == relative)
    pair_ref[...] = dot(query_hot, positive_hot, 1, 1)

    square = (negatives, negatives)
    negative = jnp.sum(
        jnp.where(iota(square, 0) == iota(square, 1), negative_ref[...].astype(F32), 0.0),
        axis=1,
        keepdims=True,
    )
    negative_hot = one_hot(iota((negatives, nodes), 1).astype(F32) == negative)
    negative_hot_ref[...] = negative_hot
    x_negative_ref[...] = dot(negative_hot, x_ref[...]).astype(BF16)

    ones = jnp.ones((tile, 128), BF16)
    for block in range(row_blocks):
        total = jnp.zeros((tile, x_ref.shape[1]), F32)
        weight = jnp.ones((tile, 128), F32)
        for t in range(tiles_row):
            first = pl.multiple_of(columns_ref[0, block, t] * tile, tile)
            values = values_ref[0, block, t]
            total += dot(values, x_ref[pl.ds(first, tile), :])
            weight += dot(values, ones)
        local_ref[block * tile : (block + 1) * tile, :] = total
        degree_ref[block * tile : (block + 1) * tile, :] = weight

    self_ref[...] = dot(x_ref[...], weight_self_ref[...])
    x_turned_ref[...] = x_ref[...].T.reshape(x_turned_ref.shape)

    total = peers * slots
    shape = (peers, total)
    column = iota(shape, 1)
    start = (iota(shape, 0) ^ place_ref[1]) * slots
    mine = (column >= start) & (column < start + slots)
    first = jnp.sum(jnp.where(mine, start.astype(F32), 0.0), axis=0, keepdims=True)
    place = iota((1, total), 1).astype(F32) - first
    spread = one_hot(iota((slots, total), 0).astype(F32) == place)
    table = dot(target_ref[0].astype(F32).astype(BF16), spread)
    target = jnp.sum(jnp.where(mine, table, 0.0), axis=0, keepdims=True)
    target_hot_ref[...] = one_hot(iota((nodes, total), 0).astype(F32) == target)


def aggregate_kernel(
    received_ref,
    target_hot_ref,
    local_ref,
    degree_ref,
    negative_hot_ref,
    x_negative_ref,
    out_ref,
    negative_ref,
):
    received = received_ref[...].astype(F32)
    live = received[:, :1] < DEAD_FLOOR
    weighted = jnp.where(live, received, 0.0).astype(BF16)
    flags = jnp.broadcast_to(jnp.where(live, 1.0, 0.0), (received.shape[0], 128)).astype(BF16)
    hot = target_hot_ref[...]
    degree = degree_ref[...] + dot(hot, flags)
    summed = local_ref[...] + dot(hot, weighted)
    width = summed.shape[1]
    for first in range(0, width, 128):
        out_ref[:, first : first + 128] = (summed[:, first : first + 128] / degree).astype(BF16)
    negative_ref[0] = x_negative_ref[...]
    negative_ref[1] = dot(negative_hot_ref[...], out_ref[...]).astype(BF16)


def embed_kernel(
    self_ref,
    aggregate_ref,
    weight_neigh_ref,
    embeds_hbm,
    embeds_ref,
    exact_ref,
    scale_ref,
    turned_ref,
    sem,
):
    aggregate = aggregate_ref[...]
    pre = self_ref[...] + dot(aggregate, weight_neigh_ref[...])
    scale = lax.rsqrt(jnp.mean(pre * pre, axis=1, keepdims=True) + EPSILON)
    exact = pre * scale
    embeds_ref[...] = exact.astype(BF16)
    copy = pltpu.make_async_copy(embeds_ref, embeds_hbm, sem)
    copy.start()
    exact_ref[...] = exact
    scale_ref[...] = jnp.broadcast_to(scale, scale_ref.shape)
    turned_ref[...] = aggregate.T.reshape(turned_ref.shape)
    copy.wait()


def split_dot(left, right, left_axis):
    high = left.astype(BF16)
    low = (left - high.astype(F32)).astype(BF16)
    return dot(high, right, left_axis, 0) + dot(low, right, left_axis, 0)


def gradient_kernel(
    query_total,
    core_ref,
    cand_ref,
    weight_self_ref,
    weight_neigh_ref,
    embeds_ref,
    exact_ref,
    scale_ref,
    pair_ref,
    x_turned_ref,
    aggregate_turned_ref,
    keep_ref,
    send_ref,
    x_cand_turned_ref,
    aggregate_cand_turned_ref,
):
    width = embeds_ref.shape[1]
    score_factor = 1.0 / math.sqrt(width)
    candidates = cand_ref.shape[1]

    x_cand, aggregate_cand = cand_ref[0], cand_ref[1]
    pre = dot(x_cand, weight_self_ref[...]) + dot(aggregate_cand, weight_neigh_ref[...])
    scale_cand = lax.rsqrt(jnp.mean(pre * pre, axis=1, keepdims=True) + EPSILON)
    exact_cand = pre * scale_cand
    cand = exact_cand.astype(BF16)

    embeds = embeds_ref[...]
    scores = score_factor * dot(embeds, cand, 1, 1)
    sigma = jax.nn.sigmoid(scores)
    factor = LOSS_FACTOR / query_total
    at_positive = ((sigma - 1.0) * factor).astype(BF16).astype(F32)
    elsewhere = ((sigma / (candidates - 1.0)) * factor).astype(BF16).astype(F32)
    pair = pair_ref[...]
    count = jnp.sum(pair, axis=1, keepdims=True)
    grad = (count - pair) * elsewhere + pair * at_positive

    emb_grad = score_factor * split_dot(grad, cand, 1)
    cand_grad = score_factor * split_dot(grad, embeds, 0)

    def through_norm(given, exact, scale):
        inner = jnp.mean(exact * given, axis=1, keepdims=True)
        return (scale * (given - exact * inner)).astype(BF16)

    pre_grad = through_norm(emb_grad, exact_ref[...], scale_ref[:, :1])
    pre_grad_cand = through_norm(cand_grad, exact_cand, scale_cand)

    half, _, rows, _ = x_turned_ref.shape
    x_cand_turned_ref[...] = x_cand.T.reshape(half, 2, rows, candidates)
    aggregate_cand_turned_ref[...] = aggregate_cand.T.reshape(half, 2, rows, candidates)
    own = core_ref[0]
    parts = (
        (x_turned_ref, x_cand_turned_ref),
        (aggregate_turned_ref, aggregate_cand_turned_ref),
    )
    for ref, core in ((send_ref, 1 - own), (keep_ref, own)):
        for part, (turned_ref, cand_turned_ref) in enumerate(parts):
            left = turned_ref[:, core].reshape(half * rows, turned_ref.shape[3])
            left_cand = cand_turned_ref[:, core].reshape(half * rows, candidates)
            block = dot(left, pre_grad) + dot(left_cand, pre_grad_cand)
            ref[part * half : (part + 1) * half] = block.reshape(half, rows, width).astype(BF16)


VMEM = pl.BlockSpec(memory_space=pltpu.VMEM)
SMEM = pl.BlockSpec(memory_space=pltpu.SMEM)
HBM = pl.BlockSpec(memory_space=pltpu.HBM)


def call(kernel, name, outs, args, flops=0, scratch=()):
    shapes = [jax.ShapeDtypeStruct(shape, kind) for shape, kind, _ in outs]
    arrays = [a for a, _ in args]
    moved = sum(math.prod(a.shape) * a.dtype.itemsize for a in arrays + shapes)
    return pl.pallas_call(
        kernel,
        name=name,
        out_shape=shapes,
        in_specs=[place for _, place in args],
        out_specs=[place for _, _, place in outs],
        scratch_shapes=list(scratch),
        compiler_params=pltpu.CompilerParams(vmem_limit_bytes=16 << 20),
        cost_estimate=pl.CostEstimate(flops=flops, bytes_accessed=moved, transcendentals=0),
    )(*arrays)


def on_device(
    features,
    tile_columns,
    tile_values,
    send_rows,
    send_count,
    ghost_target,
    query_rows,
    positive_cand,
    negative_rows,
    weight_self,
    weight_neigh,
):
    nodes, width = features.shape
    peers, slots = send_rows.shape[1:]
    total = peers * slots
    negatives = negative_rows.shape[1]
    groups = lax.axis_size("group")
    candidates = negatives * groups
    chips = peers // 2
    rows = 2 * width // peers
    half = chips // 2
    group = lax.axis_index("group").astype(jnp.int32)
    core = (lax.axis_index("dom") & 1).astype(jnp.int32)
    swap = [(i, i ^ 1) for i in range(peers)]
    same_core = [[c + 2 * chip for chip in range(chips)] for c in range(2)]

    keep, send = call(
        pack_kernel,
        "pack",
        [((chips, slots, width), BF16, VMEM)] * 2,
        [(core.reshape(1), SMEM), (send_rows, HBM), (send_count, HBM), (features, HBM)],
        flops=2 * total * nodes * width,
        scratch=[
            pltpu.VMEM(send_rows.shape, jnp.int32),
            pltpu.VMEM(send_count.shape, jnp.int32),
            pltpu.VMEM(features.shape, BF16),
            pltpu.SemaphoreType.DMA((3,)),
        ],
    )
    swapped = lax.ppermute(send, "dom", swap)
    local, degree, own_pre, pair, target_hot, negative_hot, x_negative, x_turned = call(
        local_kernel,
        "local",
        [
            ((nodes, width), F32, VMEM),
            ((nodes, 128), F32, VMEM),
            ((nodes, width), F32, VMEM),
            ((nodes, candidates), F32, VMEM),
            ((nodes, total), BF16, VMEM),
            ((negatives, nodes), BF16, VMEM),
            ((negatives, width), BF16, VMEM),
            ((half, 2, rows, nodes), BF16, VMEM),
        ],
        [
            (tile_columns, SMEM),
            (jnp.stack([group, core]), SMEM),
            (tile_values, VMEM),
            (features, VMEM),
            (weight_self, VMEM),
            (ghost_target, VMEM),
            (query_rows, VMEM),
            (positive_cand, VMEM),
            (negative_rows, VMEM),
        ],
        flops=2 * nodes * width * (width + tile_values.shape[2] * tile_values.shape[3]),
    )
    swapped, local = lax.optimization_barrier((swapped, local))
    received = lax.all_to_all(
        jnp.concatenate([keep, swapped], axis=1),
        "dom",
        split_axis=0,
        concat_axis=0,
        axis_index_groups=same_core,
        tiled=True,
    ).reshape(total, width)

    aggregate, own_cand = call(
        aggregate_kernel,
        "aggregate",
        [((nodes, width), BF16, VMEM), ((2, negatives, width), BF16, VMEM)],
        [
            (a, VMEM)
            for a in (received, target_hot, local, degree, negative_hot, x_negative)
        ],
        flops=2 * nodes * total * width,
    )
    cand = [own_cand]
    for k in range(1, groups):
        cand.append(
            lax.ppermute(own_cand, "group", [((g + k) % groups, g) for g in range(groups)])
        )
    embeds_out, embeds, exact, scale, aggregate_turned = call(
        embed_kernel,
        "embed",
        [
            ((nodes, width), BF16, HBM),
            ((nodes, width), BF16, VMEM),
            ((nodes, width), F32, VMEM),
            ((nodes, 128), F32, VMEM),
            ((half, 2, rows, nodes), BF16, VMEM),
        ],
        [(own_pre, VMEM), (aggregate, VMEM), (weight_neigh, VMEM)],
        flops=2 * nodes * width * width,
        scratch=[pltpu.SemaphoreType.DMA],
    )
    keep, send = call(
        functools.partial(gradient_kernel, query_rows.shape[1]),
        "gradient",
        [((chips, rows, width), BF16, VMEM)] * 2,
        [(core.reshape(1), SMEM)]
        + [
            (a, VMEM)
            for a in (
                jnp.concatenate(cand, axis=1),
                weight_self,
                weight_neigh,
                embeds,
                exact,
                scale,
                pair,
                x_turned,
                aggregate_turned,
            )
        ],
        flops=4 * nodes * width * width,
        scratch=[pltpu.VMEM((half, 2, rows, candidates), BF16)] * 2,
    )

    part = rows // groups
    chip_sum = (keep.astype(F32) + lax.ppermute(send, "dom", swap).astype(F32)).astype(BF16)
    all_chips = [
        [g * peers + 2 * chip + c for chip in range(chips) for g in range(groups)]
        for c in range(2)
    ]
    parts = lax.all_to_all(
        chip_sum.reshape(chips * groups, part, width),
        ("group", "dom"),
        split_axis=0,
        concat_axis=0,
        axis_index_groups=all_chips,
        tiled=True,
    )
    summed = jnp.sum(parts.astype(F32), axis=0).astype(BF16)
    if groups == 2:
        other = lax.ppermute(summed, "group", [(0, 1), (1, 0)])
        shard = jnp.where(
            group == 0,
            jnp.concatenate([summed, other], axis=0),
            jnp.concatenate([other, summed], axis=0),
        )
    else:
        shard = lax.all_gather(summed, "group", axis=0, tiled=True)
    return (embeds_out, shard)


def solution(mesh):
    placed = (
        P(("group", "dom"), None),
        P(("group", "dom"), None, None),
        P(("group", "dom"), None, None, None, None),
        P(("group", "dom"), None, None),
        P(("group", "dom"), None),
        P(("group", "dom"), None, None),
        P(("group", "dom"), None),
        P(("group", "dom"), None),
        P(("group", "dom"), None),
        P(),
        P(),
    )
    return jax.shard_map(
        on_device,
        mesh=mesh,
        in_specs=placed,
        out_specs=(P(("group", "dom"), None), P("dom", None)),
        check_vma=False,
    )
```

time: 59.3 us -> 57.4 us (0.968)
  blocking collectives: 17.5 us -> 36 us
  Pallas kernels: 14.5 us -> 5.34 us
  starting transfers between devices: 11.3 us -> 2.78 us
  waiting for transfers between devices: 11.1 us -> 6.91 us
  local copies, waits for them, and re-layouts: 0.71 us -> 4.25 us
  other arithmetic: 3.18 us -> 0.96 us
    all_to_all x1 -> x2, blocking collectives: 17.5 us -> 36 us  [the longest x1 19.8 us: on_device(): lax.all_to_all(chip_sum.reshape(chips * groups, part, width), ('group', '...]
    pallas_call x5, Pallas kernels: 14.5 us -> 5.34 us  [call(): pl.pallas_call(kernel, name=name, out_shape=shapes, in_specs=[place for _...]
    all_to_all x1 -> x0, starting transfers between devices: 7.41 us -> none  [on_device(): lax.all_to_all(outgoing.reshape(peers, slots, width), 'dom', split_axis=0...]
    all_to_all x1 -> x0, waiting for transfers between devices: 5.48 us -> none  [on_device(): lax.all_to_all(outgoing.reshape(peers, slots, width), 'dom', split_axis=0...]
    unnamed x6 -> x26, local copies, waits for them, and re-layouts: 0.71 us -> 4.25 us
    ppermute x3, waiting for transfers between devices: 3.5 us -> 5.01 us  [the longest x1 3.35 us: on_device(): other = lax.ppermute(summed, 'group', [(0, 1), (1, 0)])]
    concatenate x2, other arithmetic: 1.27 us -> 0.03 us  [the longest x1 0.02 us: on_device(): jnp.concatenate([keep, swapped], axis=1)]
    ppermute x3, starting transfers between devices: 3.86 us -> 2.71 us  [the longest x1 1.53 us: on_device(): lax.ppermute(own_cand, 'group', [((g + k) % groups, g) for g in range(gro...]
  transfers between devices with their start and end apart: 5 -> 4, of which waited for: 3 -> 3; matrix products, arithmetic and copies ran while one was open for 1% -> 0% of each run, Pallas kernels for 14% -> 4%
where the time goes in v2:
time: 57.4 us; the launch traced here: 57 us
  blocking collectives  36 us (63%)
  waiting for transfers between devices  6.91 us (12%)
  Pallas kernels  5.34 us (9%)
  local copies, waits for them, and re-layouts  4.25 us (7%)
  starting transfers between devices  2.78 us (5%)
  other arithmetic  0.96 us (2%)
  between operations  0.75 us (1%)
    all_to_all x1, blocking collectives, on_device(): lax.all_to_all(chip_sum.reshape(chips * groups, part, width), ('group', '...  19.8 us
    all_to_all x1, blocking collectives, on_device(): lax.all_to_all(jnp.concatenate([keep, swapped], axis=1), 'dom', split_axi...  16.2 us
    pallas_call x5, Pallas kernels, call(): pl.pallas_call(kernel, name=name, out_shape=shapes, in_specs=[place for _...  5.34 us
    unnamed x26, local copies, waits for them, and re-layouts  4.25 us
    ppermute x1, waiting for transfers between devices, on_device(): other = lax.ppermute(summed, 'group', [(0, 1), (1, 0)])  3.35 us
    ppermute x1, waiting for transfers between devices, on_device(): lax.ppermute(send, 'dom', swap).astype(F32)  1.9 us
    ppermute x1, waiting for transfers between devices, on_device(): lax.ppermute(own_cand, 'group', [((g + k) % groups, g) for g in range(gro...  1.66 us
    ppermute x1, starting transfers between devices, on_device(): lax.ppermute(own_cand, 'group', [((g + k) % groups, g) for g in range(gro...  1.53 us
  transfers between devices with their start and end apart: 4, of which 3 were waited for; matrix products, arithmetic and copies ran while one was open for 0% of the time, Pallas kernels for 4%

profile of v2, /device:TPU:0, one launch (start us, length us, event | category | flops | bytes accessed | tf_op | source)
XLA Modules:
  0.0 57.0 jit_solution(2713074569123688559)
XLA Ops:
  0.6 0.0 copy-start.7
  0.6 0.0 copy-start.11
  0.7 0.7 %copy-done.7 = s32[1,16,16]{2,1,0:T(8,128)S(1)} copy-done((s32[1,16,16]{2,1,0:T(8,128)S(1)}, s32[1,16,16]{2,1,0:T(8,128)}, u32[]{:S(2)}) %copy-start.7) | copy-done | bytes 1048
  1.3 0.0 copy-done.11
  1.3 0.0 copy-start.3
  1.3 0.9 %copy-done.3 = bf16[256,512]{1,0:T(8,128)(2,1)S(1)} copy-done((bf16[256,512]{1,0:T(8,128)(2,1)S(1)}, bf16[256,512]{1,0:T(8,128)(2,1)}, u32[]{:S(2)}) %copy-start.3) | copy-done | bytes 262168
  2.3 0.0 copy-start.4
  2.3 0.0 copy-start.9
  2.3 0.0 copy-start.12
  2.3 0.6 pack.1
  2.9 0.0 copy-start.6
  2.9 0.6 collective-permute-start
  3.4 0.0 copy-start.8
  3.4 0.0 copy-start.10
  3.4 0.1 pad_add_fusion.place_ref
  3.5 0.0 copy-done.4
  3.5 0.0 copy-done.9
  3.5 0.0 copy-done.12
  3.5 0.1 copy-done.6
  3.6 0.5 copy-done.8
  4.1 0.0 copy-done.10
  4.1 0.0 copy-start
  4.1 1.0 %copy-done = bf16[512,512]{1,0:T(8,128)(2,1)S(1)} copy-done((bf16[512,512]{1,0:T(8,128)(2,1)S(1)}, bf16[512,512]{1,0:T(8,128)(2,1)}, u32[]{:S(2)}) %copy-start) | copy-done | bytes 524312
  5.2 0.0 copy-start.5
  5.2 0.9 %copy-done.5 = bf16[1,2,4,128,128]{4,3,2,1,0:T(8,128)(2,1)S(1)} copy-done((bf16[1,2,4,128,128]{4,3,2,1,0:T(8,128)(2,1)S(1)}, bf16[1,2,4,128,128]{4,3,2,1,0:T(8,128)(2,1)}, u32[]{:S(2)}) %copy-start.5) | copy-done | bytes 262168
  6.1 1.4 %local.1 = (f32[256,512]{1,0:T(8,128)S(1)}, f32[256,128]{1,0:T(8,128)S(1)}, f32[256,512]{1,0:T(8,128)S(1)}, f32[256,64]{1,0:T(8,128)S(1)}, bf16[256,256]{1,0:T(8...) custom-call(s32[1,2,4]{2,1,0:T(2,128)S(1)} %copy-done.10, ...), custom_call_target="tpu_custom_call" | custom-call | flops 268435456 | bytes 2741416 | tf_op jit(solution)/shard_map/local/pallas_call | solution.py:267
  7.5 0.0 collective-permute-done
  7.5 16.2 %all_to_all.10 = bf16[8,32,512]{2,1,0:T(8,128)(2,1)S(1)} all-to-all(bf16[8,32,512]{2,1,0:T(8,128)(2,1)S(1)} %pad_maximum_fusion), channel_id=1, replica_groups={{0,2,4,6,8,10,12,14},{1,3,5,7,9,11,13,15},{16,18,20,22,24,26,28,30},{17..., dimensions={0} | all-to-all | bytes 524288 | tf_op jit(solution)/shard_map/all_to_all | solution.py:347
  23.8 0.0 copy-start.2
  23.8 0.5 aggregate.1
  24.3 1.5 %collective-permute-start.1 = (bf16[2,32,512]{2,1,0:T(8,128)(2,1)S(1)}, bf16[2,32,512]{2,1,0:T(8,128)(2,1)S(1)}, u32[]{:S(2)}, u32[]{:S(2)}) collective-permute-start(bf16[2,32,512]{2,1,0:T(8,128)(2,1)S(1)} %get-tuple-element.35), channel_id=1, source_target_pairs={{16,0},{0,16},{17,1},{1,17},{18,2},{2,18},{19,3},{3,19},{20,4},{4,... | collective-permute-start | bytes 196616 | tf_op jit(solution)/shard_map/ppermute | solution.py:369
  25.8 0.0 copy-done.2
  25.8 0.0 copy-start.1
  25.8 1.1 %embed.1 = (bf16[256,512]{1,0:T(8,128)(2,1)}, bf16[256,512]{1,0:T(8,128)(2,1)S(1)}, f32[256,512]{1,0:T(8,128)S(1)}, f32[256,128]{1,0:T(8,128)S(1)}, bf16[4,2,64,256]{3,2,1,0:T(8,128)(2,1)S(1)}) custom-call(f32[256,512]{1,0:T(8,128)S(1)} %get-tuple-element.23.self_ref, bf16[256,512]{1,0:T(8,128)(2,1)S(1)} %get-tuple-element.33.aggregate_ref, ...), custom_call_target="tpu_custom_call" | custom-call | flops 134217728 | bytes 2752512 | tf_op jit(solution)/shard_map/embed/pallas_call | solution.py:267
  26.9 1.7 %collective-permute-done.1 = bf16[2,32,512]{2,1,0:T(8,128)(2,1)S(1)} collective-permute-done((bf16[2,32,512]{2,1,0:T(8,128)(2,1)S(1)}, bf16[2,32,512]{2,1,0:T(8,128)(2,1)S(1)}, u32[]{:S(2)}, u32[]{:S(2)}) %collective-permute-start.1) | collective-permute-done | bytes 65568 | tf_op jit(solution)/shard_map/ppermute | solution.py:369
  28.6 0.0 copy-done.1
  28.6 1.8 %gradient.1 = (bf16[8,64,512]{2,1,0:T(8,128)(2,1)S(1)}, bf16[8,64,512]{2,1,0:T(8,128)(2,1)S(1)}) custom-call(s32[1]{0:T(128)} %bitcast.1.core_ref, bf16[2,64,512]{2,1,0:T(8,128)(2,1)S(1)} %pad_maximum_fusion.1.cand_ref, bf16[512,512]{1,0:T(8,128)(2,1)S(1)} %copy-done.1, bf16[512,512]{1,0:T(8,128)(2,1)S(1)} %copy-done.2, ...), custom_call_target="tpu_custom_call" | custom-call | flops 268435456 | bytes 3735556 | tf_op jit(solution)/shard_map/gradient/pallas_call | solution.py:267
  30.4 0.1 collective-permute-start.2
  30.5 1.9 %collective-permute-done.2 = bf16[8,64,512]{2,1,0:T(8,128)(2,1)S(1)} collective-permute-done((bf16[8,64,512]{2,1,0:T(8,128)(2,1)S(1)}, bf16[8,64,512]{2,1,0:T(8,128)(2,1)S(1)}, u32[]{:S(2)}, u32[]{:S(2)}) %collective-permute-start.2) | collective-permute-done | bytes 524320 | tf_op jit(solution)/shard_map/ppermute | solution.py:409
  32.4 0.1 add_convert_fusion
  32.5 19.8 %all_to_all.11 = bf16[16,32,512]{2,1,0:T(8,128)(2,1)S(1)} all-to-all(bf16[16,32,512]{2,1,0:T(8,128)(2,1)S(1)} %bitcast.5), channel_id=1, replica_groups={{0,16,2,18,4,20,6,22,8,24,10,26,12,28,14,30},{1,17,3,19,5,21,7,23,9,25,..., dimensions={0} | all-to-all | bytes 1048576 | tf_op jit(solution)/shard_map/all_to_all | solution.py:414
  52.3 0.1 reduce_sum.12
  52.4 0.6 %collective-permute-start.3 = (bf16[32,512]{1,0:T(8,128)(2,1)S(1)}, bf16[32,512]{1,0:T(8,128)(2,1)S(1)}, u32[]{:S(2)}, u32[]{:S(2)}) collective-permute-start(bf16[32,512]{1,0:T(8,128)(2,1)S(1)} %reduce_sum.12), channel_id=1, source_target_pairs={{0,16},{16,0},{1,17},{17,1},{2,18},{18,2},{3,19},{19,3},{4,20},{20... | collective-permute-start | bytes 98312 | tf_op jit(solution)/shard_map/ppermute | solution.py:424
  53.0 3.4 %collective-permute-done.3 = bf16[32,512]{1,0:T(8,128)(2,1)S(1)} collective-permute-done((bf16[32,512]{1,0:T(8,128)(2,1)S(1)}, bf16[32,512]{1,0:T(8,128)(2,1)S(1)}, u32[]{:S(2)}, u32[]{:S(2)}) %collective-permute-start.3) | collective-permute-done | bytes 32800 | tf_op jit(solution)/shard_map/ppermute | solution.py:424
  56.4 0.6 %maximum_select_fusion = bf16[64,512]{1,0:T(8,128)(2,1)} fusion(bf16[32,512]{1,0:T(8,128)(2,1)S(1)} %collective-permute-done.3, bf16[32,512]{1,0:T(8,128)(2,1)S(1)} %reduce_sum.12, pred[]{:T(512)S(6)} %eq.3), kind=kLoop, calls=%fused_computation.3 | loop fusion | flops 294912 | bytes 131073 | tf_op jit(solution)/shard_map/jit(_where)/select_n | solution.py:425
  (2 shorter events, 0.0 us)
Async XLA Ops:
  0.6 0.7 %copy-start.7 = (s32[1,16,16]{2,1,0:T(8,128)S(1)}, s32[1,16,16]{2,1,0:T(8,128)}, u32[]{:S(2)}) copy-start(s32[1,16,16]{2,1,0:T(8,128)} %rows_hbm.1) | copy-start | bytes 3076
  0.6 0.7 %copy-start.11 = (s32[1,16]{1,0:T(1,128)S(1)}, s32[1,16]{1,0:T(1,128)}, u32[]{:S(2)}) copy-start(s32[1,16]{1,0:T(1,128)} %count_hbm.1) | copy-start | bytes 196
  1.3 1.0 %copy-start.3 = (bf16[256,512]{1,0:T(8,128)(2,1)S(1)}, bf16[256,512]{1,0:T(8,128)(2,1)}, u32[]{:S(2)}) copy-start(bf16[256,512]{1,0:T(8,128)(2,1)} %x_hbm.1) | copy-start | bytes 786436
  2.3 1.2 %copy-start.4 = (bf16[256,512]{1,0:T(8,128)(2,1)S(1)}, bf16[256,512]{1,0:T(8,128)(2,1)}, u32[]{:S(2)}) copy-start(bf16[256,512]{1,0:T(8,128)(2,1)} %x_hbm.1) | copy-start | bytes 786436
  2.3 1.2 %copy-start.9 = (s32[1,512]{1,0:T(1,128)S(1)}, s32[1,512]{1,0:T(1,128)}, u32[]{:S(2)}) copy-start(s32[1,512]{1,0:T(1,128)} %positive_ref.1) | copy-start | bytes 6148
  2.3 1.2 %copy-start.12 = (s32[1,32]{1,0:T(1,128)S(1)}, s32[1,32]{1,0:T(1,128)}, u32[]{:S(2)}) copy-start(s32[1,32]{1,0:T(1,128)} %negative_ref.1) | copy-start | bytes 388
  2.9 0.7 %copy-start.6 = (s32[1,16,16]{2,1,0:T(8,128)S(1)}, s32[1,16,16]{2,1,0:T(8,128)}, u32[]{:S(2)}) copy-start(s32[1,16,16]{2,1,0:T(8,128)} %target_ref.1) | copy-start | bytes 3076
  2.9 4.6 %collective-permute-start = (bf16[8,16,512]{2,1,0:T(8,128)(2,1)S(1)}, bf16[8,16,512]{2,1,0:T(8,128)(2,1)S(1)}, u32[]{:S(2)}, u32[]{:S(2)}) collective-permute-start(bf16[8,16,512]{2,1,0:T(8,128)(2,1)S(1)} %get-tuple-element.25), channel_id=1, source_target_pairs={{0,1},{1,0},{2,3},{3,2},{4,5},{5,4},{6,7},{7,6},{8,9},{9,8},{10,11... | collective-permute-start | bytes 393224 | tf_op jit(solution)/shard_map/ppermute | solution.py:319
  3.4 0.7 %copy-start.8 = (s32[1,512]{1,0:T(1,128)S(1)}, s32[1,512]{1,0:T(1,128)}, u32[]{:S(2)}) copy-start(s32[1,512]{1,0:T(1,128)} %query_ref.1) | copy-start | bytes 6148
  3.4 0.7 %copy-start.10 = (s32[1,2,4]{2,1,0:T(2,128)S(1)}, s32[1,2,4]{2,1,0:T(2,128)}, u32[]{:S(2)}) copy-start(s32[1,2,4]{2,1,0:T(2,128)} %columns_ref.1) | copy-start | bytes 100
  4.1 1.0 %copy-start = (bf16[512,512]{1,0:T(8,128)(2,1)S(1)}, bf16[512,512]{1,0:T(8,128)(2,1)}, u32[]{:S(2)}) copy-start(bf16[512,512]{1,0:T(8,128)(2,1)} %weight_self_ref.3) | copy-start | bytes 1572868
  5.2 0.9 %copy-start.5 = (bf16[1,2,4,128,128]{4,3,2,1,0:T(8,128)(2,1)S(1)}, bf16[1,2,4,128,128]{4,3,2,1,0:T(8,128)(2,1)}, u32[]{:S(2)}) copy-start(bf16[1,2,4,128,128]{4,3,2,1,0:T(8,128)(2,1)} %values_ref.1) | copy-start | bytes 786436
  23.8 2.0 %copy-start.2 = (bf16[512,512]{1,0:T(8,128)(2,1)S(1)}, bf16[512,512]{1,0:T(8,128)(2,1)}, u32[]{:S(2)}) copy-start(bf16[512,512]{1,0:T(8,128)(2,1)} %weight_neigh_ref.3) | copy-start | bytes 1572868
  24.3 4.3 %collective-permute-start.1 = (bf16[2,32,512]{2,1,0:T(8,128)(2,1)S(1)}, bf16[2,32,512]{2,1,0:T(8,128)(2,1)S(1)}, u32[]{:S(2)}, u32[]{:S(2)}) collective-permute-start(bf16[2,32,512]{2,1,0:T(8,128)(2,1)S(1)} %get-tuple-element.35), channel_id=1, source_target_pairs={{16,0},{0,16},{17,1},{1,17},{18,2},{2,18},{19,3},{3,19},{20,4},{4,... | collective-permute-start | bytes 196616 | tf_op jit(solution)/shard_map/ppermute | solution.py:369
  25.8 2.8 %copy-start.1 = (bf16[512,512]{1,0:T(8,128)(2,1)S(1)}, bf16[512,512]{1,0:T(8,128)(2,1)}, u32[]{:S(2)}) copy-start(bf16[512,512]{1,0:T(8,128)(2,1)} %weight_self_ref.3) | copy-start | bytes 1572868
  30.4 2.0 %collective-permute-start.2 = (bf16[8,64,512]{2,1,0:T(8,128)(2,1)S(1)}, bf16[8,64,512]{2,1,0:T(8,128)(2,1)S(1)}, u32[]{:S(2)}, u32[]{:S(2)}) collective-permute-start(bf16[8,64,512]{2,1,0:T(8,128)(2,1)S(1)} %get-tuple-element.43), channel_id=1, source_target_pairs={{0,1},{1,0},{2,3},{3,2},{4,5},{5,4},{6,7},{7,6},{8,9},{9,8},{10,11... | collective-permute-start | bytes 1572872 | tf_op jit(solution)/shard_map/ppermute | solution.py:409
  52.4 4.0 %collective-permute-start.3 = (bf16[32,512]{1,0:T(8,128)(2,1)S(1)}, bf16[32,512]{1,0:T(8,128)(2,1)S(1)}, u32[]{:S(2)}, u32[]{:S(2)}) collective-permute-start(bf16[32,512]{1,0:T(8,128)(2,1)S(1)} %reduce_sum.12), channel_id=1, source_target_pairs={{0,16},{16,0},{1,17},{17,1},{2,18},{18,2},{3,19},{19,3},{4,20},{20... | collective-permute-start | bytes 98312 | tf_op jit(solution)/shard_map/ppermute | solution.py:424

commit v3 on v2

--- a/solution.py
+++ b/solution.py
@@ -31,46 +31,46 @@
     return jnp.where(condition, 1.0, 0.0).astype(BF16)
 
 
-def pack_kernel(core_ref, rows_hbm, count_hbm, x_hbm, keep_ref, send_ref, rows_ref, count_ref, x_ref, sems):
-    copies = [
-        pltpu.make_async_copy(source, target, sems.at[n])
-        for n, (source, target) in enumerate(
-            ((rows_hbm, rows_ref), (count_hbm, count_ref), (x_hbm, x_ref))
+def pack_kernel(rows_hbm, count_hbm, x_hbm, out_hbm, rows_ref, count_ref, x_ref, out_ref, sems):
+    places = ((rows_hbm, rows_ref), (count_hbm, count_ref), (x_hbm, x_ref))
+    loads = [pltpu.make_async_copy(*pair, sems.at[n]) for n, pair in enumerate(places)]
+    for load in loads:
+        load.start()
+    peers, slots = rows_ref.shape[1:]
+    nodes, width = x_ref.shape
+    total = peers * slots
+    row, first = iota((total, peers), 0), iota((total, peers), 1) * slots
+    mine = (row >= first) & (row < first + slots)
+    start = jnp.sum(jnp.where(mine, first.astype(F32), 0.0), axis=1, keepdims=True)
+    place = row[:, :1].astype(F32) - start
+    at_place = iota((total, slots), 1).astype(F32) == place
+    peer = one_hot(mine)
+    loads[0].wait()
+    loads[1].wait()
+    table = dot(peer, rows_ref[0].astype(F32).astype(BF16))
+    index = jnp.sum(jnp.where(at_place, table, 0.0), axis=1, keepdims=True)
+    count = jnp.sum(jnp.where(mine, count_ref[...].astype(F32), 0.0), axis=1, keepdims=True)
+    live = place < count
+    pick = one_hot(iota((total, nodes), 1).astype(F32) == index)
+    loads[2].wait()
+    stores = []
+    part = peers // 2
+    for n in range(2):
+        part_rows = slice(n * part * slots, (n + 1) * part * slots)
+        out = jnp.where(live[part_rows], dot(pick[part_rows], x_ref[...]), DEAD)
+        out_ref[n * part : (n + 1) * part] = out.astype(BF16).reshape(part, slots, width)
+        store = pltpu.make_async_copy(
+            out_ref.at[pl.ds(n * part, part)], out_hbm.at[pl.ds(n * part, part)], sems.at[3 + n]
         )
-    ]
-    for copy in copies:
-        copy.start()
-    peers, slots = rows_ref.shape[1:]
-    nodes = x_ref.shape[0]
-    half = peers // 2 * slots
-    shape = (half, peers)
-    row, peer = iota(shape, 0), iota(shape, 1)
-    first = (peer >> 1) * slots
-    chip = (row >= first) & (row < first + slots)
-    copies[0].wait()
-    copies[1].wait()
-    rows = rows_ref[0].astype(F32).astype(BF16)
-    counts = count_ref[...].astype(F32)
-    picks = []
-    for core in (core_ref[0], 1 - core_ref[0]):
-        mine = chip & ((peer & 1) == core)
-        start = jnp.sum(jnp.where(mine, first.astype(F32), 0.0), axis=1, keepdims=True)
-        place = row[:, :1].astype(F32) - start
-        at_place = iota((half, slots), 1).astype(F32) == place
-        table = dot(one_hot(mine), rows)
-        index = jnp.sum(jnp.where(at_place, table, 0.0), axis=1, keepdims=True)
-        count = jnp.sum(jnp.where(mine, counts, 0.0), axis=1, keepdims=True)
-        pick = one_hot(iota((half, nodes), 1).astype(F32) == index)
-        picks.append((pick, place < count))
-    copies[2].wait()
-    x = x_ref[...]
-    for (pick, live), ref in reversed(list(zip(picks, (keep_ref, send_ref)))):
-        ref[...] = jnp.where(live, dot(pick, x), DEAD).astype(BF16).reshape(ref.shape)
+        store.start()
+        stores.append(store)
+    for store in stores:
+        store.wait()
 
 
 def local_kernel(
     columns_ref,
-    place_ref,
+    group_ref,
     values_ref,
     x_ref,
     weight_self_ref,
@@ -94,7 +94,7 @@
     queries = query_ref.shape[1]
     candidates = pair_ref.shape[1]
 
-    relative = positive_ref[...] - place_ref[0] * negatives
+    relative = positive_ref[...] - group_ref[0] * negatives
     relative = jnp.where(relative < 0, relative + candidates, relative)
     query_hot = one_hot(iota((nodes, queries), 0) == query_ref[...])
     positive_hot = one_hot(iota((candidates, queries), 0) == relative)
@@ -127,11 +127,10 @@
 
     total = peers * slots
     shape = (peers, total)
-    column = iota(shape, 1)
-    start = (iota(shape, 0) ^ place_ref[1]) * slots
-    mine = (column >= start) & (column < start + slots)
-    first = jnp.sum(jnp.where(mine, start.astype(F32), 0.0), axis=0, keepdims=True)
-    place = iota((1, total), 1).astype(F32) - first
+    column, first = iota(shape, 1), iota(shape, 0) * slots
+    mine = (column >= first) & (column < first + slots)
+    start = jnp.sum(jnp.where(mine, first.astype(F32), 0.0), axis=0, keepdims=True)
+    place = iota((1, total), 1).astype(F32) - start
     spread = one_hot(iota((slots, total), 0).astype(F32) == place)
     table = dot(target_ref[0].astype(F32).astype(BF16), spread)
     target = jnp.sum(jnp.where(mine, table, 0.0), axis=0, keepdims=True)
@@ -144,7 +143,6 @@
     local_ref,
     degree_ref,
     negative_hot_ref,
-    x_negative_ref,
     out_ref,
     negative_ref,
 ):
@@ -158,8 +156,7 @@
     width = summed.shape[1]
     for first in range(0, width, 128):
         out_ref[:, first : first + 128] = (summed[:, first : first + 128] / degree).astype(BF16)
-    negative_ref[0] = x_negative_ref[...]
-    negative_ref[1] = dot(negative_hot_ref[...], out_ref[...]).astype(BF16)
+    negative_ref[...] = dot(negative_hot_ref[...], out_ref[...]).astype(BF16)
 
 
 def embed_kernel(
@@ -195,7 +192,8 @@
 def gradient_kernel(
     query_total,
     core_ref,
-    cand_ref,
+    x_cand_ref,
+    aggregate_cand_ref,
     weight_self_ref,
     weight_neigh_ref,
     embeds_ref,
@@ -211,9 +209,9 @@
 ):
     width = embeds_ref.shape[1]
     score_factor = 1.0 / math.sqrt(width)
-    candidates = cand_ref.shape[1]
-
-    x_cand, aggregate_cand = cand_ref[0], cand_ref[1]
+    candidates = x_cand_ref.shape[0]
+
+    x_cand, aggregate_cand = x_cand_ref[...], aggregate_cand_ref[...]
     pre = dot(x_cand, weight_self_ref[...]) + dot(aggregate_cand, weight_neigh_ref[...])
     scale_cand = lax.rsqrt(jnp.mean(pre * pre, axis=1, keepdims=True) + EPSILON)
     exact_cand = pre * scale_cand
@@ -260,7 +258,7 @@
 HBM = pl.BlockSpec(memory_space=pltpu.HBM)
 
 
-def call(kernel, name, outs, args, flops=0, scratch=()):
+def call(kernel, name, outs, args, flops=0, scratch=(), grant=16 << 20):
     shapes = [jax.ShapeDtypeStruct(shape, kind) for shape, kind, _ in outs]
     arrays = [a for a, _ in args]
     moved = sum(math.prod(a.shape) * a.dtype.itemsize for a in arrays + shapes)
@@ -271,7 +269,7 @@
         in_specs=[place for _, place in args],
         out_specs=[place for _, _, place in outs],
         scratch_shapes=list(scratch),
-        compiler_params=pltpu.CompilerParams(vmem_limit_bytes=16 << 20),
+        compiler_params=pltpu.CompilerParams(vmem_limit_bytes=grant),
         cost_estimate=pl.CostEstimate(flops=flops, bytes_accessed=moved, transcendentals=0),
     )(*arrays)
 
@@ -300,23 +298,25 @@
     half = chips // 2
     group = lax.axis_index("group").astype(jnp.int32)
     core = (lax.axis_index("dom") & 1).astype(jnp.int32)
-    swap = [(i, i ^ 1) for i in range(peers)]
-    same_core = [[c + 2 * chip for chip in range(chips)] for c in range(2)]
-
-    keep, send = call(
+
+    (outgoing,) = call(
         pack_kernel,
         "pack",
-        [((chips, slots, width), BF16, VMEM)] * 2,
-        [(core.reshape(1), SMEM), (send_rows, HBM), (send_count, HBM), (features, HBM)],
+        [((peers, slots, width), BF16, HBM)],
+        [(send_rows, HBM), (send_count, HBM), (features, HBM)],
         flops=2 * total * nodes * width,
         scratch=[
             pltpu.VMEM(send_rows.shape, jnp.int32),
             pltpu.VMEM(send_count.shape, jnp.int32),
             pltpu.VMEM(features.shape, BF16),
-            pltpu.SemaphoreType.DMA((3,)),
+            pltpu.VMEM((peers, slots, width), BF16),
+            pltpu.SemaphoreType.DMA((5,)),
         ],
-    )
-    swapped = lax.ppermute(send, "dom", swap)
+        grant=None,
+    )
+    received = lax.all_to_all(
+        outgoing, "dom", split_axis=0, concat_axis=0, tiled=True
+    ).reshape(total, width)
     local, degree, own_pre, pair, target_hot, negative_hot, x_negative, x_turned = call(
         local_kernel,
         "local",
@@ -332,7 +332,7 @@
         ],
         [
             (tile_columns, SMEM),
-            (jnp.stack([group, core]), SMEM),
+            (group.reshape(1), SMEM),
             (tile_values, VMEM),
             (features, VMEM),
             (weight_self, VMEM),
@@ -343,31 +343,23 @@
         ],
         flops=2 * nodes * width * (width + tile_values.shape[2] * tile_values.shape[3]),
     )
-    swapped, local = lax.optimization_barrier((swapped, local))
-    received = lax.all_to_all(
-        jnp.concatenate([keep, swapped], axis=1),
-        "dom",
-        split_axis=0,
-        concat_axis=0,
-        axis_index_groups=same_core,
-        tiled=True,
-    ).reshape(total, width)
-
-    aggregate, own_cand = call(
+
+    def gathered(own):
+        blocks = [own]
+        for k in range(1, groups):
+            pairs = [((g + k) % groups, g) for g in range(groups)]
+            blocks.append(lax.ppermute(own, "group", pairs))
+        return jnp.concatenate(blocks, axis=0)
+
+    x_cand = gathered(x_negative)
+    aggregate, aggregate_negative = call(
         aggregate_kernel,
         "aggregate",
-        [((nodes, width), BF16, VMEM), ((2, negatives, width), BF16, VMEM)],
-        [
-            (a, VMEM)
-            for a in (received, target_hot, local, degree, negative_hot, x_negative)
-        ],
+        [((nodes, width), BF16, VMEM), ((negatives, width), BF16, VMEM)],
+        [(a, VMEM) for a in (received, target_hot, local, degree, negative_hot)],
         flops=2 * nodes * total * width,
     )
-    cand = [own_cand]
-    for k in range(1, groups):
-        cand.append(
-            lax.ppermute(own_cand, "group", [((g + k) % groups, g) for g in range(groups)])
-        )
+    aggregate_cand = gathered(aggregate_negative)
     embeds_out, embeds, exact, scale, aggregate_turned = call(
         embed_kernel,
         "embed",
@@ -390,7 +382,8 @@
         + [
             (a, VMEM)
             for a in (
-                jnp.concatenate(cand, axis=1),
+                x_cand,
+                aggregate_cand,
                 weight_self,
                 weight_neigh,
                 embeds,
@@ -405,30 +398,23 @@
         scratch=[pltpu.VMEM((half, 2, rows, candidates), BF16)] * 2,
     )
 
-    part = rows // groups
+    swap = [(i, i ^ 1) for i in range(peers)]
+    same_core = [[c + 2 * chip for chip in range(chips)] for c in range(2)]
     chip_sum = (keep.astype(F32) + lax.ppermute(send, "dom", swap).astype(F32)).astype(BF16)
-    all_chips = [
-        [g * peers + 2 * chip + c for chip in range(chips) for g in range(groups)]
-        for c in range(2)
-    ]
     parts = lax.all_to_all(
-        chip_sum.reshape(chips * groups, part, width),
-        ("group", "dom"),
+        chip_sum,
+        "dom",
         split_axis=0,
         concat_axis=0,
-        axis_index_groups=all_chips,
+        axis_index_groups=same_core,
         tiled=True,
     )
-    summed = jnp.sum(parts.astype(F32), axis=0).astype(BF16)
+    shard = jnp.sum(parts.astype(F32), axis=0).astype(BF16)
     if groups == 2:
-        other = lax.ppermute(summed, "group", [(0, 1), (1, 0)])
-        shard = jnp.where(
-            group == 0,
-            jnp.concatenate([summed, other], axis=0),
-            jnp.concatenate([other, summed], axis=0),
-        )
+        other = lax.ppermute(shard, "group", [(0, 1), (1, 0)])
+        shard = (shard.astype(F32) + other.astype(F32)).astype(BF16)
     else:
-        shard = lax.all_gather(summed, "group", axis=0, tiled=True)
+        shard = lax.psum(shard, "group")
     return (embeds_out, shard)
 
 

time: 57.4 us -> 51.6 us (0.90)
  blocking collectives: 36 us -> 17.5 us
  starting transfers between devices: 2.78 us -> 12.3 us
  waiting for transfers between devices: 6.91 us -> 12.3 us
  local copies, waits for them, and re-layouts: 4.25 us -> 0.65 us
  Pallas kernels: 5.34 us -> 6.72 us
    all_to_all x2 -> x1, blocking collectives: 36 us -> 17.5 us  [on_device(): lax.all_to_all(chip_sum, 'dom', split_axis=0, concat_axis=0, axis_index_g...]
    all_to_all x0 -> x1, starting transfers between devices: none -> 7.56 us  [on_device(): lax.all_to_all(outgoing, 'dom', split_axis=0, concat_axis=0, tiled=True)]
    all_to_all x0 -> x1, waiting for transfers between devices: none -> 6.38 us  [on_device(): lax.all_to_all(outgoing, 'dom', split_axis=0, concat_axis=0, tiled=True)]
    unnamed x26 -> x18, local copies, waits for them, and re-layouts: 4.25 us -> 0.65 us
    ppermute x3, starting transfers between devices: 2.71 us -> 4.64 us  [the longest x2 3.09 us: gathered(): blocks.append(lax.ppermute(own, 'group', pairs))]
    pallas_call x5, Pallas kernels: 5.34 us -> 6.72 us  [call(): pl.pallas_call(kernel, name=name, out_shape=shapes, in_specs=[place for _...]
    ppermute x3, waiting for transfers between devices: 5.01 us -> 4.07 us  [the longest x1 2.78 us: on_device(): other = lax.ppermute(shard, 'group', [(0, 1), (1, 0)])]
    convert_element_type x0 -> x1, other arithmetic: none -> 0.65 us  [on_device(): shard = (shard.astype(F32) + other.astype(F32)).astype(BF16)]
  transfers between devices with their start and end apart: 4 -> 5, of which waited for: 3 -> 4; matrix products, arithmetic and copies ran while one was open for 0% -> 0% of each run, Pallas kernels for 4% -> 6%
where the time goes in v3:
time: 51.6 us; the launch traced here: 51.2 us
  blocking collectives  17.5 us (34%)
  starting transfers between devices  12.3 us (24%)
  waiting for transfers between devices  12.3 us (24%)
  Pallas kernels  6.72 us (13%)
  other arithmetic  0.87 us (2%)
  between operations  0.82 us (2%)
  local copies, waits for them, and re-layouts  0.65 us (1%)
    all_to_all x1, blocking collectives, on_device(): lax.all_to_all(chip_sum, 'dom', split_axis=0, concat_axis=0, axis_index_g...  17.5 us
    all_to_all x1, starting transfers between devices, on_device(): lax.all_to_all(outgoing, 'dom', split_axis=0, concat_axis=0, tiled=True)  7.56 us
    pallas_call x5, Pallas kernels, call(): pl.pallas_call(kernel, name=name, out_shape=shapes, in_specs=[place for _...  6.72 us
    all_to_all x1, waiting for transfers between devices, on_device(): lax.all_to_all(outgoing, 'dom', split_axis=0, concat_axis=0, tiled=True)  6.38 us
    ppermute x2, starting transfers between devices, gathered(): blocks.append(lax.ppermute(own, 'group', pairs))  3.09 us
    ppermute x1, waiting for transfers between devices, on_device(): other = lax.ppermute(shard, 'group', [(0, 1), (1, 0)])  2.78 us
    ppermute x1, waiting for transfers between devices, on_device(): lax.ppermute(send, 'dom', swap).astype(F32)  1.9 us
    ppermute x1, starting transfers between devices, on_device(): other = lax.ppermute(shard, 'group', [(0, 1), (1, 0)])  1.55 us
  transfers between devices with their start and end apart: 5, of which 4 were waited for; matrix products, arithmetic and copies ran while one was open for 0% of the time, Pallas kernels for 6%

profile of v3, /device:TPU:0, one launch (start us, length us, event | category | flops | bytes accessed | tf_op | source)
XLA Modules:
  0.0 51.2 jit_solution(2259215496725890609)
XLA Ops:
  0.6 0.0 copy-start
  0.6 0.0 copy-start.5
  0.7 0.0 copy-start.6
  0.7 0.0 copy-start.8
  0.7 2.0 %pack.1 = bf16[16,16,512]{2,1,0:T(8,128)(2,1)} custom-call(s32[1,16,16]{2,1,0:T(8,128)} %rows_hbm.1, s32[1,16]{1,0:T(1,128)} %count_hbm.1, bf16[256,512]{1,0:T(8,128)(2,1)} %x_hbm.1), custom_call_target="tpu_custom_call" | custom-call | flops 67108864 | bytes 525376 | tf_op jit(solution)/shard_map/pack/pallas_call | solution.py:265
  2.7 0.0 copy-start.2
  2.7 0.0 copy-start.3
  2.7 7.6 %all-to-all-start = ((bf16[16,16,512]{2,1,0:T(8,128)(2,1)}), bf16[16,16,512]{2,1,0:T(8,128)(2,1)S(1)}, u32[]{:S(2)}, u32[]{:S(2)}) async-start(bf16[16,16,512]{2,1,0:T(8,128)(2,1)} %pack.1), calls=%async_computation | async-start | bytes 524288 | tf_op jit(solution)/shard_map/all_to_all | solution.py:317
  10.2 0.0 copy-start.4
  10.3 0.0 copy-start.7
  10.3 0.0 copy-done
  10.3 0.0 copy-done.5
  10.3 0.0 copy-done.6
  10.3 0.0 copy-done.8
  10.3 0.0 copy-done.2
  10.3 0.0 copy-done.3
  10.3 0.6 %copy-done.4 = s32[1,16,16]{2,1,0:T(8,128)S(1)} copy-done((s32[1,16,16]{2,1,0:T(8,128)S(1)}, s32[1,16,16]{2,1,0:T(8,128)}, u32[]{:S(2)}) %copy-start.4) | copy-done | bytes 1048
  10.9 0.0 copy-done.7
  10.9 1.4 %local.1 = (f32[256,512]{1,0:T(8,128)S(1)}, f32[256,128]{1,0:T(8,128)S(1)}, f32[256,512]{1,0:T(8,128)S(1)}, f32[256,64]{1,0:T(8,128)S(1)}, bf16[256,256]{1,0:T(8...) custom-call(s32[1,2,4]{2,1,0:T(2,128)S(1)} %copy-done.7, ...), custom_call_target="tpu_custom_call" | custom-call | flops 268435456 | bytes 2741412 | tf_op jit(solution)/shard_map/local/pallas_call | solution.py:265
  12.3 1.6 %collective-permute-start = (bf16[32,512]{1,0:T(8,128)(2,1)S(1)}, bf16[32,512]{1,0:T(8,128)(2,1)S(1)}, u32[]{:S(2)}, u32[]{:S(2)}) collective-permute-start(bf16[32,512]{1,0:T(8,128)(2,1)S(1)} %get-tuple-element.26), channel_id=1, source_target_pairs={{16,0},{0,16},{17,1},{1,17},{18,2},{2,18},{19,3},{3,19},{20,4},{4,... | collective-permute-start | bytes 98312 | tf_op jit(solution)/shard_map/ppermute | solution.py:351
  13.9 6.4 %all-to-all-done = bf16[16,16,512]{2,1,0:T(8,128)(2,1)S(1)} async-done(((bf16[16,16,512]{2,1,0:T(8,128)(2,1)}), bf16[16,16,512]{2,1,0:T(8,128)(2,1)S(1)}, u32[]{:S(2)}, u32[]{:S(2)}) %all-to-all-start) | async-done | bytes 262176 | tf_op jit(solution)/shard_map/all_to_all | solution.py:317
  20.3 0.0 copy-start.1
  20.3 0.5 aggregate.1
  20.8 1.5 %collective-permute-start.1 = (bf16[32,512]{1,0:T(8,128)(2,1)S(1)}, bf16[32,512]{1,0:T(8,128)(2,1)S(1)}, u32[]{:S(2)}, u32[]{:S(2)}) collective-permute-start(bf16[32,512]{1,0:T(8,128)(2,1)S(1)} %get-tuple-element.27), channel_id=1, source_target_pairs={{16,0},{0,16},{17,1},{1,17},{18,2},{2,18},{19,3},{3,19},{20,4},{4,... | collective-permute-start | bytes 98312 | tf_op jit(solution)/shard_map/ppermute | solution.py:351
  22.3 0.0 collective-permute-done
  22.3 0.0 copy-done.1
  22.3 1.1 %embed.1 = (bf16[256,512]{1,0:T(8,128)(2,1)}, bf16[256,512]{1,0:T(8,128)(2,1)S(1)}, f32[256,512]{1,0:T(8,128)S(1)}, f32[256,128]{1,0:T(8,128)S(1)}, bf16[4,2,64,256]{3,2,1,0:T(8,128)(2,1)S(1)}) custom-call(f32[256,512]{1,0:T(8,128)S(1)} %get-tuple-element.19.self_ref, bf16[256,512]{1,0:T(8,128)(2,1)S(1)} %get-tuple-element.24.aggregate_ref, ...), custom_call_target="tpu_custom_call" | custom-call | flops 134217728 | bytes 2752512 | tf_op jit(solution)/shard_map/embed/pallas_call | solution.py:265
  23.4 1.3 %collective-permute-done.1 = bf16[32,512]{1,0:T(8,128)(2,1)S(1)} collective-permute-done((bf16[32,512]{1,0:T(8,128)(2,1)S(1)}, bf16[32,512]{1,0:T(8,128)(2,1)S(1)}, u32[]{:S(2)}, u32[]{:S(2)}) %collective-permute-start.1) | collective-permute-done | bytes 32800 | tf_op jit(solution)/shard_map/ppermute | solution.py:351
  24.7 1.8 %gradient.1 = (bf16[8,64,512]{2,1,0:T(8,128)(2,1)S(1)}, bf16[8,64,512]{2,1,0:T(8,128)(2,1)S(1)}) custom-call(s32[1]{0:T(128)} %bitcast.2.core_ref, bf16[64,512]{1,0:T(8,128)(2,1)S(1)} %pad_maximum_fusion.x_cand_ref, bf16[64,512]{1,0:T(8,128)(2,1)S(1)} %pad_maximum_fusion.1.aggregate_cand_ref, bf16[512,512]{1,0:T(8,128)(2,1)S(1)} %copy-done, ...), custom_call_target="tpu_custom_call" | custom-call | flops 268435456 | bytes 3735556 | tf_op jit(solution)/shard_map/gradient/pallas_call | solution.py:265
  26.5 0.1 collective-permute-start.2
  26.6 1.9 %collective-permute-done.2 = bf16[8,64,512]{2,1,0:T(8,128)(2,1)S(1)} collective-permute-done((bf16[8,64,512]{2,1,0:T(8,128)(2,1)S(1)}, bf16[8,64,512]{2,1,0:T(8,128)(2,1)S(1)}, u32[]{:S(2)}, u32[]{:S(2)}) %collective-permute-start.2) | collective-permute-done | bytes 524320 | tf_op jit(solution)/shard_map/ppermute | solution.py:403
  28.5 0.1 add_convert_fusion
  28.6 17.5 %all_to_all.10 = bf16[8,64,512]{2,1,0:T(8,128)(2,1)S(1)} all-to-all(bf16[8,64,512]{2,1,0:T(8,128)(2,1)S(1)} %add_convert_fusion), channel_id=1, replica_groups={{0,2,4,6,8,10,12,14},{1,3,5,7,9,11,13,15},{16,18,20,22,24,26,28,30},{17..., dimensions={0} | all-to-all | bytes 1048576 | tf_op jit(solution)/shard_map/all_to_all | solution.py:404
  46.1 0.1 reduce_sum.12
  46.2 1.6 %collective-permute-start.3 = (bf16[64,512]{1,0:T(8,128)(2,1)S(1)}, bf16[64,512]{1,0:T(8,128)(2,1)S(1)}, u32[]{:S(2)}, u32[]{:S(2)}) collective-permute-start(bf16[64,512]{1,0:T(8,128)(2,1)S(1)} %reduce_sum.12), channel_id=1, source_target_pairs={{0,16},{16,0},{1,17},{17,1},{2,18},{18,2},{3,19},{19,3},{4,20},{20... | collective-permute-start | bytes 196616 | tf_op jit(solution)/shard_map/ppermute | solution.py:414
  47.7 2.8 %collective-permute-done.3 = bf16[64,512]{1,0:T(8,128)(2,1)S(1)} collective-permute-done((bf16[64,512]{1,0:T(8,128)(2,1)S(1)}, bf16[64,512]{1,0:T(8,128)(2,1)S(1)}, u32[]{:S(2)}, u32[]{:S(2)}) %collective-permute-start.3) | collective-permute-done | bytes 65568 | tf_op jit(solution)/shard_map/ppermute | solution.py:414
  50.5 0.6 %add_convert_fusion.1 = bf16[64,512]{1,0:T(8,128)(2,1)} fusion(bf16[64,512]{1,0:T(8,128)(2,1)S(1)} %collective-permute-done.3, bf16[64,512]{1,0:T(8,128)(2,1)S(1)} %reduce_sum.12), kind=kLoop, calls=%fused_computation.1 | loop fusion | flops 131072 | bytes 196608 | tf_op jit(solution)/shard_map/convert_element_type | solution.py:415
  (2 shorter events, 0.0 us)
Async XLA Ops:
  0.6 9.6 %copy-start = (bf16[512,512]{1,0:T(8,128)(2,1)S(1)}, bf16[512,512]{1,0:T(8,128)(2,1)}, u32[]{:S(2)}) copy-start(bf16[512,512]{1,0:T(8,128)(2,1)} %weight_self_ref.3) | copy-start | bytes 1572868
  0.6 9.6 %copy-start.5 = (s32[1,512]{1,0:T(1,128)S(1)}, s32[1,512]{1,0:T(1,128)}, u32[]{:S(2)}) copy-start(s32[1,512]{1,0:T(1,128)} %query_ref.1) | copy-start | bytes 6148
  0.7 9.6 %copy-start.6 = (s32[1,512]{1,0:T(1,128)S(1)}, s32[1,512]{1,0:T(1,128)}, u32[]{:S(2)}) copy-start(s32[1,512]{1,0:T(1,128)} %positive_ref.1) | copy-start | bytes 6148
  0.7 9.6 %copy-start.8 = (s32[1,32]{1,0:T(1,128)S(1)}, s32[1,32]{1,0:T(1,128)}, u32[]{:S(2)}) copy-start(s32[1,32]{1,0:T(1,128)} %negative_ref.1) | copy-start | bytes 388
  2.7 7.7 %copy-start.2 = (bf16[256,512]{1,0:T(8,128)(2,1)S(1)}, bf16[256,512]{1,0:T(8,128)(2,1)}, u32[]{:S(2)}) copy-start(bf16[256,512]{1,0:T(8,128)(2,1)} %x_hbm.1) | copy-start | bytes 786436
  2.7 7.7 %copy-start.3 = (bf16[1,2,4,128,128]{4,3,2,1,0:T(8,128)(2,1)S(1)}, bf16[1,2,4,128,128]{4,3,2,1,0:T(8,128)(2,1)}, u32[]{:S(2)}) copy-start(bf16[1,2,4,128,128]{4,3,2,1,0:T(8,128)(2,1)} %values_ref.1) | copy-start | bytes 786436
  2.7 17.6 %all-to-all-start = ((bf16[16,16,512]{2,1,0:T(8,128)(2,1)}), bf16[16,16,512]{2,1,0:T(8,128)(2,1)S(1)}, u32[]{:S(2)}, u32[]{:S(2)}) async-start(bf16[16,16,512]{2,1,0:T(8,128)(2,1)} %pack.1), calls=%async_computation | async-start | bytes 524288 | tf_op jit(solution)/shard_map/all_to_all | solution.py:317
  10.2 0.7 %copy-start.4 = (s32[1,16,16]{2,1,0:T(8,128)S(1)}, s32[1,16,16]{2,1,0:T(8,128)}, u32[]{:S(2)}) copy-start(s32[1,16,16]{2,1,0:T(8,128)} %target_ref.1) | copy-start | bytes 3076
  10.3 0.7 %copy-start.7 = (s32[1,2,4]{2,1,0:T(2,128)S(1)}, s32[1,2,4]{2,1,0:T(2,128)}, u32[]{:S(2)}) copy-start(s32[1,2,4]{2,1,0:T(2,128)} %columns_ref.1) | copy-start | bytes 100
  12.3 10.0 %collective-permute-start = (bf16[32,512]{1,0:T(8,128)(2,1)S(1)}, bf16[32,512]{1,0:T(8,128)(2,1)S(1)}, u32[]{:S(2)}, u32[]{:S(2)}) collective-permute-start(bf16[32,512]{1,0:T(8,128)(2,1)S(1)} %get-tuple-element.26), channel_id=1, source_target_pairs={{16,0},{0,16},{17,1},{1,17},{18,2},{2,18},{19,3},{3,19},{20,4},{4,... | collective-permute-start | bytes 98312 | tf_op jit(solution)/shard_map/ppermute | solution.py:351
  20.3 2.0 %copy-start.1 = (bf16[512,512]{1,0:T(8,128)(2,1)S(1)}, bf16[512,512]{1,0:T(8,128)(2,1)}, u32[]{:S(2)}) copy-start(bf16[512,512]{1,0:T(8,128)(2,1)} %weight_neigh_ref.3) | copy-start | bytes 1572868
  20.8 4.0 %collective-permute-start.1 = (bf16[32,512]{1,0:T(8,128)(2,1)S(1)}, bf16[32,512]{1,0:T(8,128)(2,1)S(1)}, u32[]{:S(2)}, u32[]{:S(2)}) collective-permute-start(bf16[32,512]{1,0:T(8,128)(2,1)S(1)} %get-tuple-element.27), channel_id=1, source_target_pairs={{16,0},{0,16},{17,1},{1,17},{18,2},{2,18},{19,3},{3,19},{20,4},{4,... | collective-permute-start | bytes 98312 | tf_op jit(solution)/shard_map/ppermute | solution.py:351
  26.5 2.0 %collective-permute-start.2 = (bf16[8,64,512]{2,1,0:T(8,128)(2,1)S(1)}, bf16[8,64,512]{2,1,0:T(8,128)(2,1)S(1)}, u32[]{:S(2)}, u32[]{:S(2)}) collective-permute-start(bf16[8,64,512]{2,1,0:T(8,128)(2,1)S(1)} %get-tuple-element.35), channel_id=1, source_target_pairs={{0,1},{1,0},{2,3},{3,2},{4,5},{5,4},{6,7},{7,6},{8,9},{9,8},{10,11... | collective-permute-start | bytes 1572872 | tf_op jit(solution)/shard_map/ppermute | solution.py:403
  46.2 4.3 %collective-permute-start.3 = (bf16[64,512]{1,0:T(8,128)(2,1)S(1)}, bf16[64,512]{1,0:T(8,128)(2,1)S(1)}, u32[]{:S(2)}, u32[]{:S(2)}) collective-permute-start(bf16[64,512]{1,0:T(8,128)(2,1)S(1)} %reduce_sum.12), channel_id=1, source_target_pairs={{0,16},{16,0},{1,17},{17,1},{2,18},{18,2},{3,19},{19,3},{4,20},{20... | collective-permute-start | bytes 196616 | tf_op jit(solution)/shard_map/ppermute | solution.py:414

commit v4 on v3

v4 whole, which is shorter than its diff:
```python
import functools
import math

import jax
import jax.numpy as jnp
from jax import lax
from jax.experimental import pallas as pl
from jax.experimental.pallas import tpu as pltpu
from jax.sharding import PartitionSpec as P

LOSS_FACTOR = 64.0
EPSILON = 1e-05
DEAD = 256.0
DEAD_FLOOR = 128.0

F32 = jnp.float32
BF16 = jnp.bfloat16


def iota(shape, axis):
    return lax.broadcasted_iota(jnp.int32, shape, axis)


def dot(left, right, left_axis=1, right_axis=0):
    return lax.dot_general(
        left, right, (((left_axis,), (right_axis,)), ((), ())), preferred_element_type=F32
    )


def one_hot(condition):
    return jnp.where(condition, 1.0, 0.0).astype(BF16)


def pack_kernel(
    rows_hbm,
    count_hbm,
    x_hbm,
    query_hbm,
    positive_hbm,
    negative_hbm,
    out_hbm,
    joined_hbm,
    rows_ref,
    count_ref,
    x_ref,
    query_ref,
    positive_ref,
    negative_ref,
    out_ref,
    wide_ref,
    ids_ref,
    sems,
):
    places = (
        (rows_hbm, rows_ref),
        (count_hbm, count_ref),
        (x_hbm, x_ref),
        (query_hbm, query_ref),
        (positive_hbm, positive_ref),
        (negative_hbm, negative_ref),
    )
    loads = [pltpu.make_async_copy(*pair, sems.at[n]) for n, pair in enumerate(places)]
    for load in loads:
        load.start()
    peers, slots = rows_ref.shape[1:]
    nodes, width = x_ref.shape
    total = peers * slots
    row, first = iota((total, peers), 0), iota((total, peers), 1) * slots
    mine = (row >= first) & (row < first + slots)
    start = jnp.sum(jnp.where(mine, first.astype(F32), 0.0), axis=1, keepdims=True)
    place = row[:, :1].astype(F32) - start
    at_place = iota((total, slots), 1).astype(F32) == place
    peer = one_hot(mine)
    loads[0].wait()
    loads[1].wait()
    table = dot(peer, rows_ref[0].astype(F32).astype(BF16))
    index = jnp.sum(jnp.where(at_place, table, 0.0), axis=1, keepdims=True)
    count = jnp.sum(jnp.where(mine, count_ref[...].astype(F32), 0.0), axis=1, keepdims=True)
    live = place < count
    pick = one_hot(iota((total, nodes), 1).astype(F32) == index)
    loads[2].wait()
    stores = [pltpu.make_async_copy(x_ref, joined_hbm.at[pl.ds(0, nodes)], sems.at[len(loads)])]
    part = peers // 4
    for n in range(4):
        part_rows = slice(n * part * slots, (n + 1) * part * slots)
        out = jnp.where(live[part_rows], dot(pick[part_rows], x_ref[...]), DEAD)
        out_ref[n * part : (n + 1) * part] = out.astype(BF16).reshape(part, slots, width)
        piece = pl.ds(n * part, part)
        stores.append(
            pltpu.make_async_copy(out_ref.at[piece], out_hbm.at[piece], sems.at[len(loads) + 1 + n])
        )
        stores[-1].start()
    stores[0].start()
    for load in loads[3:]:
        load.wait()
    wide_ref[...] = jnp.zeros_like(wide_ref)
    for n, ref in enumerate((query_ref, positive_ref, negative_ref)):
        wide_ref[n : n + 1, : ref.shape[1]] = ref[...].astype(F32)
    ids_ref[...] = wide_ref[...].astype(BF16)
    ids = pltpu.make_async_copy(
        ids_ref, joined_hbm.at[pl.ds(nodes, ids_ref.shape[0])], sems.at[len(loads) + 5]
    )
    ids.start()
    for store in stores + [ids]:
        store.wait()


def local_kernel(columns_ref, values_ref, x_ref, target_ref, local_ref, degree_ref):
    row_blocks, tiles_row, tile = values_ref.shape[1:4]
    nodes = x_ref.shape[0]
    peers, slots = target_ref.shape[1:]

    ones = jnp.ones((tile, 128), BF16)
    for block in range(row_blocks):
        total = jnp.zeros((tile, x_ref.shape[1]), F32)
        weight = jnp.ones((tile, 128), F32)
        for t in range(tiles_row):
            first = pl.multiple_of(columns_ref[0, block, t] * tile, tile)
            values = values_ref[0, block, t]
            total += dot(values, x_ref[pl.ds(first, tile), :])
            weight += dot(values, ones)
        local_ref[block * tile : (block + 1) * tile, :] = total
        degree_ref[block * tile : (block + 1) * tile, :128] = weight

    total = peers * slots
    shape = (peers, total)
    column, first = iota(shape, 1), iota(shape, 0) * slots
    mine = (column >= first) & (column < first + slots)
    start = jnp.sum(jnp.where(mine, first.astype(F32), 0.0), axis=0, keepdims=True)
    place = iota((1, total), 1).astype(F32) - start
    spread = one_hot(iota((slots, total), 0).astype(F32) == place)
    table = dot(target_ref[0].astype(F32).astype(BF16), spread)
    target = jnp.sum(jnp.where(mine, table, 0.0), axis=0, keepdims=True)
    degree_ref[:, 128:] = jnp.where(iota((nodes, total), 0).astype(F32) == target, 1.0, 0.0)


def aggregate_kernel(received_ref, local_ref, degree_ref, out_ref):
    received = received_ref[...].astype(F32)
    live = received[:, :1] < DEAD_FLOOR
    weighted = jnp.where(live, received, 0.0).astype(BF16)
    flags = jnp.broadcast_to(jnp.where(live, 1.0, 0.0), (received.shape[0], 128)).astype(BF16)
    hot = degree_ref[:, 128:].astype(BF16)
    degree = degree_ref[:, :128] + dot(hot, flags)
    summed = local_ref[...] + dot(hot, weighted)
    width = summed.shape[1]
    for first in range(0, width, 128):
        out_ref[:, first : first + 128] = (summed[:, first : first + 128] / degree).astype(BF16)


def normed(pre):
    scale = lax.rsqrt(jnp.mean(pre * pre, axis=1, keepdims=True) + EPSILON)
    return pre * scale, scale


def columns_of(group, members, whole):
    columns = whole.shape[1] // members
    part = whole[:, :columns]
    for other in range(1, members):
        there = whole[:, other * columns : (other + 1) * columns]
        part = jnp.where(group == other, there, part)
    return part


def embed_kernel(
    members,
    sizes,
    group_ref,
    aggregate_ref,
    weight_self_ref,
    weight_neigh_ref,
    *refs,
):
    queries, negatives = sizes
    candidates = members * negatives
    joined, refs = refs[:members], refs[members:]
    (embeds_hbm, embeds_ref, part_ref, scale_ref, turned_ref), refs = refs[:5], refs[5:]
    (pair_ref, rest_ref, hot_ref, hot_turned_ref), refs = refs[:4], refs[4:]
    pres, x_turned, sem = refs[: members - 1], refs[members - 1 : -1], refs[-1]
    aggregate = aggregate_ref[...]
    nodes = aggregate.shape[0]

    own_pre = dot(joined[0][:nodes], weight_self_ref[...])
    exact, scale = normed(own_pre + dot(aggregate, weight_neigh_ref[...]))
    embeds_ref[...] = exact.astype(BF16)
    copy = pltpu.make_async_copy(embeds_ref, embeds_hbm, sem)
    copy.start()
    part_ref[...] = columns_of(group_ref[0], members, exact)
    scale_ref[...] = jnp.broadcast_to(scale, scale_ref.shape)
    turned_ref[...] = aggregate.T.reshape(turned_ref.shape)

    for member, joined_ref in enumerate(joined):
        if member:
            pres[member - 1][...] = dot(joined_ref[:nodes], weight_self_ref[...])
        x_turned[member][...] = joined_ref[:nodes].T.reshape(x_turned[member].shape)
        ids = joined_ref[nodes:].astype(F32)
        query, negative = ids[:1, :queries], ids[2:3, :negatives]
        relative = ids[1:2, :queries] - (group_ref[0] * negatives).astype(F32)
        relative = jnp.where(relative < 0.0, relative + candidates, relative)
        query_hot = one_hot(iota((nodes, queries), 0).astype(F32) == query)
        positive_hot = one_hot(iota((candidates, queries), 0).astype(F32) == relative)
        pair = dot(query_hot, positive_hot, 1, 1)
        lanes = slice(member * candidates, (member + 1) * candidates)
        pair_ref[:, lanes] = pair
        rest_ref[:, lanes] = jnp.sum(pair, axis=1, keepdims=True) - pair
        square = (negatives, negatives)
        column = jnp.where(iota(square, 0) == iota(square, 1), negative, 0.0)
        column = jnp.sum(column, axis=1, keepdims=True)
        hot_ref[member] = one_hot(iota((negatives, nodes), 1).astype(F32) == column)
        turned = one_hot(iota((nodes, negatives), 0).astype(F32) == negative)
        hot_turned_ref[:, member * negatives : (member + 1) * negatives] = turned
    copy.wait()


def rows_of_core(core, ref, lefts, rights):
    half, _, rows, nodes = lefts[0][0].shape
    columns = ref.shape[2]
    for part, left_refs in enumerate(lefts):
        block = jnp.zeros((half * rows, columns), F32)
        for left_ref, right in zip(left_refs, rights):
            block += dot(left_ref[:, core].reshape(half * rows, nodes), right)
        ref[part * half : (part + 1) * half] = block.reshape(half, rows, columns).astype(BF16)


def keep_kernel(core_ref, *refs):
    *refs, keep_ref = refs
    members = len(refs) // 3
    lefts = (refs[:members], refs[members : 2 * members])
    rows_of_core(core_ref[0], keep_ref, lefts, [ref[...] for ref in refs[2 * members :]])


def gradient_kernel(
    query_total,
    core_ref,
    group_ref,
    weight_neigh_ref,
    embeds_ref,
    part_ref,
    scale_ref,
    pair_ref,
    rest_ref,
    hot_ref,
    hot_turned_ref,
    x_turned_ref,
    turned_ref,
    *refs,
):
    members, negatives, _ = hot_ref.shape
    others = members - 1
    given, refs = refs[: 3 * others], refs[3 * others :]
    send_ref, pre_grad_refs, other_turned = refs[0], refs[1 : 1 + members], refs[1 + members :]
    candidates = members * negatives
    width = embeds_ref.shape[1]
    columns = width // members
    group = group_ref[0]
    score_factor = 1.0 / math.sqrt(width)
    factor = LOSS_FACTOR / query_total

    parts, scales, embeds = [part_ref[...]], [scale_ref[:, :1]], [embeds_ref[...]]
    x_turned, turned = [x_turned_ref], [turned_ref]
    for other, other_turned_ref in enumerate(other_turned):
        aggregate_ref, pre_ref, other_x_turned_ref = given[3 * other : 3 * other + 3]
        aggregate = aggregate_ref[...]
        exact, scale = normed(pre_ref[...] + dot(aggregate, weight_neigh_ref[...]))
        parts.append(columns_of(group, members, exact))
        scales.append(scale)
        embeds.append(exact.astype(BF16))
        other_turned_ref[...] = aggregate.T.reshape(other_turned_ref.shape)
        x_turned.append(other_x_turned_ref)
        turned.append(other_turned_ref)

    cand = jnp.concatenate(
        [dot(hot_ref[m], embeds[m]).astype(BF16) for m in range(members)], axis=0
    )

    def at(member, block, count=members):
        zero = jnp.zeros_like(block)
        return jnp.concatenate([block if n == member else zero for n in range(count)], axis=0)

    product = sum(dot(embeds[m], at(m, cand), 1, 1) for m in range(members))
    sigma = jax.nn.sigmoid(score_factor * product)
    at_positive = ((sigma - 1.0) * factor).astype(BF16).astype(F32)
    elsewhere = ((sigma / (candidates - 1.0)) * factor).astype(BF16).astype(F32)
    grad = score_factor * (rest_ref[...] * elsewhere + pair_ref[...] * at_positive)
    grad = grad.astype(BF16)

    weighted = grad.astype(F32) * product
    as_cand = jnp.sum(weighted, axis=0, keepdims=True)
    as_cand = sum(as_cand[:, m * candidates : (m + 1) * candidates] for m in range(members))
    hot_turned = hot_turned_ref[...]
    as_cand = hot_turned.astype(F32) * as_cand

    cand_part = columns_of(group, members, cand)
    cand_grad = sum(
        dot(grad, parts[m].astype(BF16), 0, 0)[m * candidates : (m + 1) * candidates]
        for m in range(members)
    ).astype(BF16)
    left = jnp.concatenate([grad, hot_turned], axis=1)
    pre_grads = []
    for m in range(members):
        mine = slice(m * negatives, (m + 1) * negatives)
        right = jnp.concatenate([at(m, cand_part), at(m, cand_grad[mine])], axis=0)
        inner = jnp.sum(
            weighted[:, m * candidates : (m + 1) * candidates], axis=1, keepdims=True
        ) + jnp.sum(as_cand[:, mine], axis=1, keepdims=True)
        pre_grad = scales[m] * (dot(left, right) - parts[m] * (inner / width))
        pre_grads.append(pre_grad.astype(BF16))

    for ref, pre_grad in zip(pre_grad_refs, pre_grads):
        ref[...] = pre_grad
    rows_of_core(1 - core_ref[0], send_ref, (x_turned, turned), pre_grads)


VMEM = pl.BlockSpec(memory_space=pltpu.VMEM)
SMEM = pl.BlockSpec(memory_space=pltpu.SMEM)
HBM = pl.BlockSpec(memory_space=pltpu.HBM)


def call(kernel, name, outs, args, flops=0, scratch=(), grant=16 << 20):
    shapes = [jax.ShapeDtypeStruct(shape, kind) for shape, kind, _ in outs]
    arrays = [a for a, _ in args]
    moved = sum(math.prod(a.shape) * a.dtype.itemsize for a in arrays + shapes)
    return pl.pallas_call(
        kernel,
        name=name,
        out_shape=shapes,
        in_specs=[place for _, place in args],
        out_specs=[place for _, _, place in outs],
        scratch_shapes=list(scratch),
        compiler_params=pltpu.CompilerParams(vmem_limit_bytes=grant),
        cost_estimate=pl.CostEstimate(flops=flops, bytes_accessed=moved, transcendentals=0),
    )(*arrays)


def on_device(
    features,
    tile_columns,
    tile_values,
    send_rows,
    send_count,
    ghost_target,
    query_rows,
    positive_cand,
    negative_rows,
    weight_self,
    weight_neigh,
):
    nodes, width = features.shape
    peers, slots = send_rows.shape[1:]
    total = peers * slots
    queries = query_rows.shape[1]
    negatives = negative_rows.shape[1]
    groups = lax.axis_size("group")
    others = groups - 1
    candidates = negatives * groups
    chips = peers // 2
    rows = 2 * width // peers
    half = chips // 2
    columns = width // groups
    grant = min(8 * groups, 56) << 20
    group = lax.axis_index("group").astype(jnp.int32)
    core = (lax.axis_index("dom") & 1).astype(jnp.int32)

    def of_others(own):
        return [
            lax.ppermute(own, "group", [((g + k) % groups, g) for g in range(groups)])
            for k in range(1, groups)
        ]

    id_rows = 16
    outgoing, joined = call(
        pack_kernel,
        "pack",
        [((peers, slots, width), BF16, HBM), ((nodes + id_rows, width), BF16, HBM)],
        [
            (a, HBM)
            for a in (
                send_rows, send_count, features, query_rows, positive_cand, negative_rows
            )
        ],
        flops=2 * total * nodes * width,
        scratch=[
            pltpu.VMEM(send_rows.shape, jnp.int32),
            pltpu.VMEM(send_count.shape, jnp.int32),
            pltpu.VMEM(features.shape, BF16),
            pltpu.VMEM(query_rows.shape, jnp.int32),
            pltpu.VMEM(positive_cand.shape, jnp.int32),
            pltpu.VMEM(negative_rows.shape, jnp.int32),
            pltpu.VMEM((peers, slots, width), BF16),
            pltpu.VMEM((id_rows, width), F32),
            pltpu.VMEM((id_rows, width), BF16),
            pltpu.SemaphoreType.DMA((12,)),
        ],
        grant=None,
    )
    received = lax.all_to_all(
        outgoing, "dom", split_axis=0, concat_axis=0, tiled=True
    ).reshape(total, width)

    joined = [joined] + of_others(joined)
    local, degree = call(
        local_kernel,
        "local",
        [((nodes, width), F32, VMEM), ((nodes, 128 + total), F32, VMEM)],
        [(tile_columns, SMEM), (tile_values, VMEM), (features, VMEM), (ghost_target, VMEM)],
        flops=2 * nodes * width * tile_values.shape[2] * tile_values.shape[3],
        grant=grant,
    )
    (aggregate,) = call(
        aggregate_kernel,
        "aggregate",
        [((nodes, width), BF16, VMEM)],
        [(a, VMEM) for a in (received, local, degree)],
        flops=2 * nodes * total * width,
    )
    other_aggregate = of_others(aggregate)
    node_turned = ((half, 2, rows, nodes), BF16, VMEM)
    core, group_place = core.reshape(1), (group.reshape(1), SMEM)
    embeds_out, embeds, part, scale, turned, pair, rest, hot, hot_turned, *made = call(
        functools.partial(embed_kernel, groups, (queries, negatives)),
        "embed",
        [
            ((nodes, width), BF16, HBM),
            ((nodes, width), BF16, VMEM),
            ((nodes, columns), F32, VMEM),
            ((nodes, 128), F32, VMEM),
            node_turned,
            ((nodes, groups * candidates), F32, VMEM),
            ((nodes, groups * candidates), F32, VMEM),
            ((groups, negatives, nodes), BF16, VMEM),
            ((nodes, candidates), BF16, VMEM),
        ]
        + [((nodes, width), F32, VMEM)] * others
        + [node_turned] * groups,
        [group_place]
        + [(a, VMEM) for a in (aggregate, weight_self, weight_neigh, *joined)],
        flops=2 * nodes * width * width * groups,
        scratch=[pltpu.SemaphoreType.DMA],
        grant=grant,
    )
    x_turned, *features_turned = made[others:]
    members = []
    for trio in zip(other_aggregate, made[:others], features_turned):
        members += trio
    send, *made = call(
        functools.partial(gradient_kernel, queries),
        "gradient",
        [((chips, rows, columns), BF16, VMEM)]
        + [((nodes, columns), BF16, VMEM)] * groups
        + [node_turned] * others,
        [(core, SMEM), group_place]
        + [
            (a, VMEM)
            for a in (
                weight_neigh,
                embeds,
                part,
                scale,
                pair,
                rest,
                hot,
                hot_turned,
                x_turned,
                turned,
                *members,
            )
        ],
        flops=2 * nodes * width * width,
        grant=grant,
    )
    features_turned = [x_turned] + features_turned
    aggregates_turned = [turned] + made[groups:]
    (keep,) = call(
        keep_kernel,
        "keep",
        [((chips, rows, columns), BF16, VMEM)],
        [(core, SMEM)]
        + [(a, VMEM) for a in (*features_turned, *aggregates_turned, *made[:groups])],
        flops=2 * nodes * width * width,
        grant=grant,
    )

    swap = [(i, i ^ 1) for i in range(peers)]
    same_core = [[c + 2 * chip for chip in range(chips)] for c in range(2)]
    chip_sum = (keep.astype(F32) + lax.ppermute(send, "dom", swap).astype(F32)).astype(BF16)
    parts = lax.all_to_all(
        chip_sum,
        "dom",
        split_axis=0,
        concat_axis=0,
        axis_index_groups=same_core,
        tiled=True,
    )
    summed = jnp.sum(parts.astype(F32), axis=0).astype(BF16)
    if groups == 2:
        (other,) = of_others(summed)
        shard = jnp.where(
            group == 0,
            jnp.concatenate([summed, other], axis=1),
            jnp.concatenate([other, summed], axis=1),
        )
    else:
        shard = lax.all_gather(summed, "group", axis=1, tiled=True)
    return (embeds_out, shard)


def solution(mesh):
    placed = (
        P(("group", "dom"), None),
        P(("group", "dom"), None, None),
        P(("group", "dom"), None, None, None, None),
        P(("group", "dom"), None, None),
        P(("group", "dom"), None),
        P(("group", "dom"), None, None),
        P(("group", "dom"), None),
        P(("group", "dom"), None),
        P(("group", "dom"), None),
        P(),
        P(),
    )
    return jax.shard_map(
        on_device,
        mesh=mesh,
        in_specs=placed,
        out_specs=(P(("group", "dom"), None), P("dom", None)),
        check_vma=False,
    )
```

time: 51.6 us -> 49.4 us (0.957)
  blocking collectives: 17.5 us -> 12.2 us
  waiting for transfers between devices: 12.3 us -> 16.3 us
  local copies, waits for them, and re-layouts: 0.65 us -> 0.03 us
    all_to_all x1, blocking collectives: 17.5 us -> 12.2 us  [on_device(): lax.all_to_all(chip_sum, 'dom', split_axis=0, concat_axis=0, axis_index_g...]
    ppermute x3, waiting for transfers between devices: 4.07 us -> 7.76 us  [of_others(): lax.ppermute(own, 'group', [((g + k) % groups, g) for g in range(groups)])]
    all_to_all x1, waiting for transfers between devices: 6.38 us -> 7.35 us  [on_device(): lax.all_to_all(outgoing, 'dom', split_axis=0, concat_axis=0, tiled=True)]
    ppermute x1, waiting for transfers between devices: 1.9 us -> 1.21 us  [on_device(): lax.ppermute(send, 'dom', swap).astype(F32)]
    convert_element_type x1 -> x0, other arithmetic: 0.65 us -> none  [on_device(): shard = (shard.astype(F32) + other.astype(F32)).astype(BF16)]
    select_n x0 -> x1, other arithmetic: none -> 0.64 us  [on_device(): jnp.where(group == 0, jnp.concatenate([summed, other], axis=1), jnp.conca...]
    unnamed x18 -> x14, local copies, waits for them, and re-layouts: 0.65 us -> 0.03 us
    pallas_call x5 -> x6, Pallas kernels: 6.72 us -> 6.74 us  [call(): pl.pallas_call(kernel, name=name, out_shape=shapes, in_specs=[place for _...]
where the time goes in v4:
time: 49.4 us; the launch traced here: 49.1 us
  waiting for transfers between devices  16.3 us (33%)
  starting transfers between devices  12.3 us (25%)
  blocking collectives  12.2 us (25%)
  Pallas kernels  6.74 us (14%)
  between operations  0.76 us (2%)
  other arithmetic  0.75 us (2%)
    all_to_all x1, blocking collectives, on_device(): lax.all_to_all(chip_sum, 'dom', split_axis=0, concat_axis=0, axis_index_g...  12.2 us
    ppermute x3, waiting for transfers between devices, of_others(): lax.ppermute(own, 'group', [((g + k) % groups, g) for g in range(groups)])  7.76 us
    all_to_all x1, starting transfers between devices, on_device(): lax.all_to_all(outgoing, 'dom', split_axis=0, concat_axis=0, tiled=True)  7.56 us
    all_to_all x1, waiting for transfers between devices, on_device(): lax.all_to_all(outgoing, 'dom', split_axis=0, concat_axis=0, tiled=True)  7.35 us
    pallas_call x6, Pallas kernels, call(): pl.pallas_call(kernel, name=name, out_shape=shapes, in_specs=[place for _...  6.74 us
    ppermute x3, starting transfers between devices, of_others(): lax.ppermute(own, 'group', [((g + k) % groups, g) for g in range(groups)])  4.67 us
    ppermute x1, waiting for transfers between devices, on_device(): lax.ppermute(send, 'dom', swap).astype(F32)  1.21 us
  transfers between devices with their start and end apart: 5, of which 4 were waited for; matrix products, arithmetic and copies ran while one was open for 0% of the time, Pallas kernels for 6%

profile of v4, /device:TPU:0, one launch (start us, length us, event | category | flops | bytes accessed | tf_op | source)
XLA Modules:
  0.0 49.1 jit_solution(10689841427592101318)
XLA Ops:
  0.6 0.0 copy-start.5
  0.6 2.1 %pack.1 = (bf16[16,16,512]{2,1,0:T(8,128)(2,1)}, bf16[272,512]{1,0:T(8,128)(2,1)}) custom-call(s32[1,16,16]{2,1,0:T(8,128)} %rows_hbm.1, s32[1,16]{1,0:T(1,128)} %count_hbm.1, bf16[256,512]{1,0:T(8,128)(2,1)} %x_ref.1, s32[1,512]{1,0:T(1,128)} %query_hbm.1, s32[1,512]{1,0:T(1,128)} %positive_hbm.1, s32[1,32]{1,0:T(1,128)} %negative_hbm.1), custom_call_target="tpu_custom_call" | custom-call | flops 67108864 | bytes 808128 | tf_op jit(solution)/shard_map/pack/pallas_call | solution.py:322
  2.8 0.0 copy-start.1
  2.8 0.0 copy-start.4
  2.8 7.6 %all-to-all-start = ((bf16[16,16,512]{2,1,0:T(8,128)(2,1)}), bf16[16,16,512]{2,1,0:T(8,128)(2,1)S(1)}, u32[]{:S(2)}, u32[]{:S(2)}) async-start(bf16[16,16,512]{2,1,0:T(8,128)(2,1)} %get-tuple-element.22), calls=%async_computation | async-start | bytes 524288 | tf_op jit(solution)/shard_map/all_to_all | solution.py:395
  10.4 0.0 copy-start.6
  10.4 1.6 %collective-permute-start = (bf16[272,512]{1,0:T(8,128)(2,1)}, bf16[272,512]{1,0:T(8,128)(2,1)S(1)}, u32[]{:S(2)}, u32[]{:S(2)}) collective-permute-start(bf16[272,512]{1,0:T(8,128)(2,1)} %get-tuple-element.25.refs_0_), channel_id=1, source_target_pairs={{16,0},{0,16},{17,1},{1,17},{18,2},{2,18},{19,3},{3,19},{20,4},{4,... | collective-permute-start | bytes 835592 | tf_op jit(solution)/shard_map/ppermute | solution.py:365
  11.9 0.0 copy-done.5
  11.9 0.0 copy-done.1
  11.9 0.0 copy-done.4
  11.9 0.0 copy-done.6
  11.9 1.1 %local.1 = (f32[256,512]{1,0:T(8,128)S(1)}, f32[256,384]{1,0:T(8,128)S(1)}) custom-call(s32[1,2,4]{2,1,0:T(2,128)S(1)} %copy-done.6, bf16[1,2,4,128,128]{4,3,2,1,0:T(8,128)(2,1)S(1)} %copy-done.4, bf16[256,512]{1,0:T(8,128)(2,1)S(1)} %copy-done.1, s32[1,16,16]{2,1,0:T(8,128)S(1)} %copy-done.5), custom_call_target="tpu_custom_call" | custom-call | flops 134217728 | bytes 1442848 | tf_op jit(solution)/shard_map/local/pallas_call | solution.py:322
  13.0 7.4 %all-to-all-done = bf16[16,16,512]{2,1,0:T(8,128)(2,1)S(1)} async-done(((bf16[16,16,512]{2,1,0:T(8,128)(2,1)}), bf16[16,16,512]{2,1,0:T(8,128)(2,1)S(1)}, u32[]{:S(2)}, u32[]{:S(2)}) %all-to-all-start) | async-done | bytes 262176 | tf_op jit(solution)/shard_map/all_to_all | solution.py:395
  20.4 0.0 copy-start
  20.4 0.0 copy-start.2
  20.4 0.0 copy-start.3
  20.4 0.3 aggregate.1.aggregate_ref
  20.7 1.6 %collective-permute-start.1 = (bf16[256,512]{1,0:T(8,128)(2,1)S(1)}, bf16[256,512]{1,0:T(8,128)(2,1)S(1)}, u32[]{:S(2)}, u32[]{:S(2)}) collective-permute-start(bf16[256,512]{1,0:T(8,128)(2,1)S(1)} %aggregate.1.aggregate_ref), channel_id=1, source_target_pairs={{16,0},{0,16},{17,1},{1,17},{18,2},{2,18},{19,3},{3,19},{20,4},{4,... | collective-permute-start | bytes 786440 | tf_op jit(solution)/shard_map/ppermute | solution.py:365
  22.3 0.0 collective-permute-done.refs_1_
  22.3 0.0 copy-done
  22.3 0.0 copy-done.2
  22.3 0.0 copy-done.3
  22.3 1.3 %embed.1 = (bf16[256,512]{1,0:T(8,128)(2,1)}, bf16[256,512]{1,0:T(8,128)(2,1)S(1)}, f32[256,256]{1,0:T(8,128)S(1)}, f32[256,128]{1,0:T(8,128)S(1)}, bf16[4,2,64,...) custom-call(s32[1]{0:T(128)} %bitcast.group_ref, ...), custom_call_target="tpu_custom_call" | custom-call | flops 268435456 | bytes 4423684 | tf_op jit(solution)/shard_map/embed/pallas_call | solution.py:322
  23.6 5.3 %collective-permute-done.1.refs_0_ = bf16[256,512]{1,0:T(8,128)(2,1)S(1)} collective-permute-done((bf16[256,512]{1,0:T(8,128)(2,1)S(1)}, bf16[256,512]{1,0:T(8,128)(2,1)S(1)}, u32[]{:S(2)}, u32[]{:S(2)}) %collective-permute-start.1) | collective-permute-done | bytes 262176 | tf_op jit(solution)/shard_map/ppermute | solution.py:365
  28.9 1.6 %gradient.1 = (bf16[8,64,256]{2,1,0:T(8,128)(2,1)S(1)}, bf16[256,256]{1,0:T(8,128)(2,1)S(1)}, bf16[256,256]{1,0:T(8,128)(2,1)S(1)}, bf16[4,2,64,256]{3,2,1,0:T(8,128)(2,1)S(1)}) custom-call(s32[1]{0:T(128)} %bitcast.2.core_ref, s32[1]{0:T(128)} %bitcast.group_ref, bf16[512,512]{1,0:T(8,128)(2,1)S(1)} %copy-done, ...), custom_call_target="tpu_custom_call" | custom-call | flops 134217728 | bytes 3866632 | tf_op jit(solution)/shard_map/gradient/pallas_call | solution.py:322
  30.6 0.1 collective-permute-start.2
  30.6 0.3 keep.1
  30.9 1.2 %collective-permute-done.2 = bf16[8,64,256]{2,1,0:T(8,128)(2,1)S(1)} collective-permute-done((bf16[8,64,256]{2,1,0:T(8,128)(2,1)S(1)}, bf16[8,64,256]{2,1,0:T(8,128)(2,1)S(1)}, u32[]{:S(2)}, u32[]{:S(2)}) %collective-permute-start.2) | collective-permute-done | bytes 262176 | tf_op jit(solution)/shard_map/ppermute | solution.py:484
  32.2 0.1 add_convert_fusion
  32.2 12.2 %all_to_all.10 = bf16[8,64,256]{2,1,0:T(8,128)(2,1)S(1)} all-to-all(bf16[8,64,256]{2,1,0:T(8,128)(2,1)S(1)} %add_convert_fusion), channel_id=1, replica_groups={{0,2,4,6,8,10,12,14},{1,3,5,7,9,11,13,15},{16,18,20,22,24,26,28,30},{17..., dimensions={0} | all-to-all | bytes 524288 | tf_op jit(solution)/shard_map/all_to_all | solution.py:485
  44.4 1.6 %collective-permute-start.3 = (bf16[64,256]{1,0:T(8,128)(2,1)S(1)}, bf16[64,256]{1,0:T(8,128)(2,1)S(1)}, u32[]{:S(2)}, u32[]{:S(2)}) collective-permute-start(bf16[64,256]{1,0:T(8,128)(2,1)S(1)} %reduce_sum.12), channel_id=1, source_target_pairs={{16,0},{0,16},{17,1},{1,17},{18,2},{2,18},{19,3},{3,19},{20,4},{4,... | collective-permute-start | bytes 98312 | tf_op jit(solution)/shard_map/ppermute | solution.py:365
  46.0 2.4 %collective-permute-done.3 = bf16[64,256]{1,0:T(8,128)(2,1)S(1)} collective-permute-done((bf16[64,256]{1,0:T(8,128)(2,1)S(1)}, bf16[64,256]{1,0:T(8,128)(2,1)S(1)}, u32[]{:S(2)}, u32[]{:S(2)}) %collective-permute-start.3) | collective-permute-done | bytes 32800 | tf_op jit(solution)/shard_map/ppermute | solution.py:365
  48.4 0.6 %maximum_select_fusion = bf16[64,512]{1,0:T(8,128)(2,1)} fusion(bf16[64,256]{1,0:T(8,128)(2,1)S(1)} %collective-permute-done.3, bf16[64,256]{1,0:T(8,128)(2,1)S(1)} %reduce_sum.12, pred[]{:T(512)S(6)} %eq.3), kind=kLoop, calls=%fused_computation.1 | loop fusion | flops 294912 | bytes 131073 | tf_op jit(solution)/shard_map/jit(_where)/select_n | solution.py:496
  (1 shorter events, 0.0 us)
Async XLA Ops:
  0.6 11.3 %copy-start.5 = (s32[1,16,16]{2,1,0:T(8,128)S(1)}, s32[1,16,16]{2,1,0:T(8,128)}, u32[]{:S(2)}) copy-start(s32[1,16,16]{2,1,0:T(8,128)} %target_ref.1) | copy-start | bytes 3076
  2.8 9.2 %copy-start.1 = (bf16[256,512]{1,0:T(8,128)(2,1)S(1)}, bf16[256,512]{1,0:T(8,128)(2,1)}, u32[]{:S(2)}) copy-start(bf16[256,512]{1,0:T(8,128)(2,1)} %x_ref.1) | copy-start | bytes 786436
  2.8 9.2 %copy-start.4 = (bf16[1,2,4,128,128]{4,3,2,1,0:T(8,128)(2,1)S(1)}, bf16[1,2,4,128,128]{4,3,2,1,0:T(8,128)(2,1)}, u32[]{:S(2)}) copy-start(bf16[1,2,4,128,128]{4,3,2,1,0:T(8,128)(2,1)} %values_ref.1) | copy-start | bytes 786436
  2.8 17.6 %all-to-all-start = ((bf16[16,16,512]{2,1,0:T(8,128)(2,1)}), bf16[16,16,512]{2,1,0:T(8,128)(2,1)S(1)}, u32[]{:S(2)}, u32[]{:S(2)}) async-start(bf16[16,16,512]{2,1,0:T(8,128)(2,1)} %get-tuple-element.22), calls=%async_computation | async-start | bytes 524288 | tf_op jit(solution)/shard_map/all_to_all | solution.py:395
  10.4 1.6 %copy-start.6 = (s32[1,2,4]{2,1,0:T(2,128)S(1)}, s32[1,2,4]{2,1,0:T(2,128)}, u32[]{:S(2)}) copy-start(s32[1,2,4]{2,1,0:T(2,128)} %columns_ref.1) | copy-start | bytes 100
  10.4 11.9 %collective-permute-start = (bf16[272,512]{1,0:T(8,128)(2,1)}, bf16[272,512]{1,0:T(8,128)(2,1)S(1)}, u32[]{:S(2)}, u32[]{:S(2)}) collective-permute-start(bf16[272,512]{1,0:T(8,128)(2,1)} %get-tuple-element.25.refs_0_), channel_id=1, source_target_pairs={{16,0},{0,16},{17,1},{1,17},{18,2},{2,18},{19,3},{3,19},{20,4},{4,... | collective-permute-start | bytes 835592 | tf_op jit(solution)/shard_map/ppermute | solution.py:365
  20.4 1.9 %copy-start = (bf16[512,512]{1,0:T(8,128)(2,1)S(1)}, bf16[512,512]{1,0:T(8,128)(2,1)}, u32[]{:S(2)}) copy-start(bf16[512,512]{1,0:T(8,128)(2,1)} %weight_neigh_ref.3) | copy-start | bytes 1572868
  20.4 1.9 %copy-start.2 = (bf16[512,512]{1,0:T(8,128)(2,1)S(1)}, bf16[512,512]{1,0:T(8,128)(2,1)}, u32[]{:S(2)}) copy-start(bf16[512,512]{1,0:T(8,128)(2,1)} %weight_self_ref.1) | copy-start | bytes 1572868
  20.4 1.9 %copy-start.3 = (bf16[272,512]{1,0:T(8,128)(2,1)S(1)}, bf16[272,512]{1,0:T(8,128)(2,1)}, u32[]{:S(2)}) copy-start(bf16[272,512]{1,0:T(8,128)(2,1)} %get-tuple-element.25.refs_0_) | copy-start | bytes 835588
  20.7 8.2 %collective-permute-start.1 = (bf16[256,512]{1,0:T(8,128)(2,1)S(1)}, bf16[256,512]{1,0:T(8,128)(2,1)S(1)}, u32[]{:S(2)}, u32[]{:S(2)}) collective-permute-start(bf16[256,512]{1,0:T(8,128)(2,1)S(1)} %aggregate.1.aggregate_ref), channel_id=1, source_target_pairs={{16,0},{0,16},{17,1},{1,17},{18,2},{2,18},{19,3},{3,19},{20,4},{4,... | collective-permute-start | bytes 786440 | tf_op jit(solution)/shard_map/ppermute | solution.py:365
  30.6 1.6 %collective-permute-start.2 = (bf16[8,64,256]{2,1,0:T(8,128)(2,1)S(1)}, bf16[8,64,256]{2,1,0:T(8,128)(2,1)S(1)}, u32[]{:S(2)}, u32[]{:S(2)}) collective-permute-start(bf16[8,64,256]{2,1,0:T(8,128)(2,1)S(1)} %get-tuple-element.41), channel_id=1, source_target_pairs={{0,1},{1,0},{2,3},{3,2},{4,5},{5,4},{6,7},{7,6},{8,9},{9,8},{10,11... | collective-permute-start | bytes 786440 | tf_op jit(solution)/shard_map/ppermute | solution.py:484
  44.4 4.0 %collective-permute-start.3 = (bf16[64,256]{1,0:T(8,128)(2,1)S(1)}, bf16[64,256]{1,0:T(8,128)(2,1)S(1)}, u32[]{:S(2)}, u32[]{:S(2)}) collective-permute-start(bf16[64,256]{1,0:T(8,128)(2,1)S(1)} %reduce_sum.12), channel_id=1, source_target_pairs={{16,0},{0,16},{17,1},{1,17},{18,2},{2,18},{19,3},{3,19},{20,4},{4,... | collective-permute-start | bytes 98312 | tf_op jit(solution)/shard_map/ppermute | solution.py:365

commit v5 on v4

--- a/solution.py
+++ b/solution.py
@@ -78,30 +78,31 @@
     count = jnp.sum(jnp.where(mine, count_ref[...].astype(F32), 0.0), axis=1, keepdims=True)
     live = place < count
     pick = one_hot(iota((total, nodes), 1).astype(F32) == index)
-    loads[2].wait()
-    stores = [pltpu.make_async_copy(x_ref, joined_hbm.at[pl.ds(0, nodes)], sems.at[len(loads)])]
-    part = peers // 4
-    for n in range(4):
-        part_rows = slice(n * part * slots, (n + 1) * part * slots)
-        out = jnp.where(live[part_rows], dot(pick[part_rows], x_ref[...]), DEAD)
-        out_ref[n * part : (n + 1) * part] = out.astype(BF16).reshape(part, slots, width)
-        piece = pl.ds(n * part, part)
-        stores.append(
-            pltpu.make_async_copy(out_ref.at[piece], out_hbm.at[piece], sems.at[len(loads) + 1 + n])
-        )
-        stores[-1].start()
-    stores[0].start()
     for load in loads[3:]:
         load.wait()
     wide_ref[...] = jnp.zeros_like(wide_ref)
     for n, ref in enumerate((query_ref, positive_ref, negative_ref)):
         wide_ref[n : n + 1, : ref.shape[1]] = ref[...].astype(F32)
     ids_ref[...] = wide_ref[...].astype(BF16)
-    ids = pltpu.make_async_copy(
-        ids_ref, joined_hbm.at[pl.ds(nodes, ids_ref.shape[0])], sems.at[len(loads) + 5]
-    )
-    ids.start()
-    for store in stores + [ids]:
+    ids_place = joined_hbm.at[pl.ds(nodes, ids_ref.shape[0])]
+    loads[2].wait()
+    stores = [
+        pltpu.make_async_copy(ids_ref, ids_place, sems.at[len(loads)]),
+        pltpu.make_async_copy(x_ref, joined_hbm.at[pl.ds(0, nodes)], sems.at[len(loads) + 1]),
+    ]
+    for store in stores:
+        store.start()
+    part = peers // 2
+    for n in range(2):
+        part_rows = slice(n * part * slots, (n + 1) * part * slots)
+        out = jnp.where(live[part_rows], dot(pick[part_rows], x_ref[...]), DEAD)
+        out_ref[n * part : (n + 1) * part] = out.astype(BF16).reshape(part, slots, width)
+        piece = pl.ds(n * part, part)
+        stores.append(
+            pltpu.make_async_copy(out_ref.at[piece], out_hbm.at[piece], sems.at[len(loads) + 2 + n])
+        )
+        stores[-1].start()
+    for store in stores:
         store.wait()
 
 
@@ -207,7 +208,10 @@
         column = jnp.sum(column, axis=1, keepdims=True)
         hot_ref[member] = one_hot(iota((negatives, nodes), 1).astype(F32) == column)
         turned = one_hot(iota((nodes, negatives), 0).astype(F32) == negative)
-        hot_turned_ref[:, member * negatives : (member + 1) * negatives] = turned
+        blank = jnp.zeros((nodes, negatives), BF16)
+        hot_turned_ref[:, lanes] = jnp.concatenate(
+            [turned if n == member else blank for n in range(members)], axis=1
+        )
     copy.wait()
 
 
@@ -284,24 +288,24 @@
     grad = grad.astype(BF16)
 
     weighted = grad.astype(F32) * product
+    hot_turned = hot_turned_ref[...]
     as_cand = jnp.sum(weighted, axis=0, keepdims=True)
     as_cand = sum(as_cand[:, m * candidates : (m + 1) * candidates] for m in range(members))
-    hot_turned = hot_turned_ref[...]
-    as_cand = hot_turned.astype(F32) * as_cand
+    weighted += hot_turned.astype(F32) * jnp.concatenate([as_cand] * members, axis=1)
 
     cand_part = columns_of(group, members, cand)
+    grad_turned = grad.T
     cand_grad = sum(
-        dot(grad, parts[m].astype(BF16), 0, 0)[m * candidates : (m + 1) * candidates]
+        dot(grad_turned[m * candidates : (m + 1) * candidates], parts[m].astype(BF16))
         for m in range(members)
     ).astype(BF16)
     left = jnp.concatenate([grad, hot_turned], axis=1)
+    lane = iota(weighted.shape, 1)
     pre_grads = []
     for m in range(members):
-        mine = slice(m * negatives, (m + 1) * negatives)
-        right = jnp.concatenate([at(m, cand_part), at(m, cand_grad[mine])], axis=0)
-        inner = jnp.sum(
-            weighted[:, m * candidates : (m + 1) * candidates], axis=1, keepdims=True
-        ) + jnp.sum(as_cand[:, mine], axis=1, keepdims=True)
+        right = jnp.concatenate([at(m, cand_part), at(m, cand_grad)], axis=0)
+        mine = (lane >= m * candidates) & (lane < (m + 1) * candidates)
+        inner = jnp.sum(jnp.where(mine, weighted, 0.0), axis=1, keepdims=True)
         pre_grad = scales[m] * (dot(left, right) - parts[m] * (inner / width))
         pre_grads.append(pre_grad.astype(BF16))
 
@@ -388,7 +392,7 @@
             pltpu.VMEM((peers, slots, width), BF16),
             pltpu.VMEM((id_rows, width), F32),
             pltpu.VMEM((id_rows, width), BF16),
-            pltpu.SemaphoreType.DMA((12,)),
+            pltpu.SemaphoreType.DMA((10,)),
         ],
         grant=None,
     )
@@ -427,7 +431,7 @@
             ((nodes, groups * candidates), F32, VMEM),
             ((nodes, groups * candidates), F32, VMEM),
             ((groups, negatives, nodes), BF16, VMEM),
-            ((nodes, candidates), BF16, VMEM),
+            ((nodes, groups * candidates), BF16, VMEM),
         ]
         + [((nodes, width), F32, VMEM)] * others
         + [node_turned] * groups,

time: 49.4 us -> 49.2 us (level)
  no operation moved by 1% of the time
where the time goes in v5:
time: 49.2 us; the launch traced here: 48.9 us
  waiting for transfers between devices  16.3 us (33%)
  starting transfers between devices  12.3 us (25%)
  blocking collectives  12.2 us (25%)
  Pallas kernels  6.57 us (13%)
  between operations  0.76 us (2%)
  other arithmetic  0.75 us (2%)
    all_to_all x1, blocking collectives, on_device(): lax.all_to_all(chip_sum, 'dom', split_axis=0, concat_axis=0, axis_index_g...  12.2 us
    ppermute x3, waiting for transfers between devices, of_others(): lax.ppermute(own, 'group', [((g + k) % groups, g) for g in range(groups)])  7.76 us
    all_to_all x1, starting transfers between devices, on_device(): lax.all_to_all(outgoing, 'dom', split_axis=0, concat_axis=0, tiled=True)  7.56 us
    all_to_all x1, waiting for transfers between devices, on_device(): lax.all_to_all(outgoing, 'dom', split_axis=0, concat_axis=0, tiled=True)  7.35 us
    pallas_call x6, Pallas kernels, call(): pl.pallas_call(kernel, name=name, out_shape=shapes, in_specs=[place for _...  6.57 us
    ppermute x3, starting transfers between devices, of_others(): lax.ppermute(own, 'group', [((g + k) % groups, g) for g in range(groups)])  4.67 us
    ppermute x1, waiting for transfers between devices, on_device(): lax.ppermute(send, 'dom', swap).astype(F32)  1.21 us
  transfers between devices with their start and end apart: 5, of which 4 were waited for; matrix products, arithmetic and copies ran while one was open for 0% of the time, Pallas kernels for 6%

profile of v5, /device:TPU:0, one launch (start us, length us, event | category | flops | bytes accessed | tf_op | source)
XLA Modules:
  0.0 48.9 jit_solution(2743383315299682600)
XLA Ops:
  0.6 0.0 copy-start.5
  0.6 2.0 %pack.1 = (bf16[16,16,512]{2,1,0:T(8,128)(2,1)}, bf16[272,512]{1,0:T(8,128)(2,1)}) custom-call(s32[1,16,16]{2,1,0:T(8,128)} %rows_hbm.1, s32[1,16]{1,0:T(1,128)} %count_hbm.1, bf16[256,512]{1,0:T(8,128)(2,1)} %x_ref.1, s32[1,512]{1,0:T(1,128)} %query_hbm.1, s32[1,512]{1,0:T(1,128)} %positive_hbm.1, s32[1,32]{1,0:T(1,128)} %negative_hbm.1), custom_call_target="tpu_custom_call" | custom-call | flops 67108864 | bytes 808128 | tf_op jit(solution)/shard_map/pack/pallas_call | solution.py:326
  2.6 0.0 copy-start.1
  2.6 0.0 copy-start.4
  2.6 7.6 %all-to-all-start = ((bf16[16,16,512]{2,1,0:T(8,128)(2,1)}), bf16[16,16,512]{2,1,0:T(8,128)(2,1)S(1)}, u32[]{:S(2)}, u32[]{:S(2)}) async-start(bf16[16,16,512]{2,1,0:T(8,128)(2,1)} %get-tuple-element.22), calls=%async_computation | async-start | bytes 524288 | tf_op jit(solution)/shard_map/all_to_all | solution.py:399
  10.2 0.0 copy-start.6
  10.2 1.6 %collective-permute-start = (bf16[272,512]{1,0:T(8,128)(2,1)}, bf16[272,512]{1,0:T(8,128)(2,1)S(1)}, u32[]{:S(2)}, u32[]{:S(2)}) collective-permute-start(bf16[272,512]{1,0:T(8,128)(2,1)} %get-tuple-element.25.refs_0_), channel_id=1, source_target_pairs={{16,0},{0,16},{17,1},{1,17},{18,2},{2,18},{19,3},{3,19},{20,4},{4,... | collective-permute-start | bytes 835592 | tf_op jit(solution)/shard_map/ppermute | solution.py:369
  11.8 0.0 copy-done.5
  11.8 0.0 copy-done.1
  11.8 0.0 copy-done.4
  11.8 0.0 copy-done.6
  11.8 1.1 %local.1 = (f32[256,512]{1,0:T(8,128)S(1)}, f32[256,384]{1,0:T(8,128)S(1)}) custom-call(s32[1,2,4]{2,1,0:T(2,128)S(1)} %copy-done.6, bf16[1,2,4,128,128]{4,3,2,1,0:T(8,128)(2,1)S(1)} %copy-done.4, bf16[256,512]{1,0:T(8,128)(2,1)S(1)} %copy-done.1, s32[1,16,16]{2,1,0:T(8,128)S(1)} %copy-done.5), custom_call_target="tpu_custom_call" | custom-call | flops 134217728 | bytes 1442848 | tf_op jit(solution)/shard_map/local/pallas_call | solution.py:326
  12.9 7.4 %all-to-all-done = bf16[16,16,512]{2,1,0:T(8,128)(2,1)S(1)} async-done(((bf16[16,16,512]{2,1,0:T(8,128)(2,1)}), bf16[16,16,512]{2,1,0:T(8,128)(2,1)S(1)}, u32[]{:S(2)}, u32[]{:S(2)}) %all-to-all-start) | async-done | bytes 262176 | tf_op jit(solution)/shard_map/all_to_all | solution.py:399
  20.2 0.0 copy-start
  20.2 0.0 copy-start.2
  20.2 0.0 copy-start.3
  20.2 0.3 aggregate.1.aggregate_ref
  20.6 1.6 %collective-permute-start.1 = (bf16[256,512]{1,0:T(8,128)(2,1)S(1)}, bf16[256,512]{1,0:T(8,128)(2,1)S(1)}, u32[]{:S(2)}, u32[]{:S(2)}) collective-permute-start(bf16[256,512]{1,0:T(8,128)(2,1)S(1)} %aggregate.1.aggregate_ref), channel_id=1, source_target_pairs={{16,0},{0,16},{17,1},{1,17},{18,2},{2,18},{19,3},{3,19},{20,4},{4,... | collective-permute-start | bytes 786440 | tf_op jit(solution)/shard_map/ppermute | solution.py:369
  22.1 0.0 collective-permute-done.refs_1_
  22.1 0.0 copy-done
  22.1 0.0 copy-done.2
  22.1 0.0 copy-done.3
  22.1 1.3 %embed.1 = (bf16[256,512]{1,0:T(8,128)(2,1)}, bf16[256,512]{1,0:T(8,128)(2,1)S(1)}, f32[256,256]{1,0:T(8,128)S(1)}, f32[256,128]{1,0:T(8,128)S(1)}, bf16[4,2,64,...) custom-call(s32[1]{0:T(128)} %bitcast.group_ref, ...), custom_call_target="tpu_custom_call" | custom-call | flops 268435456 | bytes 4456452 | tf_op jit(solution)/shard_map/embed/pallas_call | solution.py:326
  23.4 5.3 %collective-permute-done.1.refs_0_ = bf16[256,512]{1,0:T(8,128)(2,1)S(1)} collective-permute-done((bf16[256,512]{1,0:T(8,128)(2,1)S(1)}, bf16[256,512]{1,0:T(8,128)(2,1)S(1)}, u32[]{:S(2)}, u32[]{:S(2)}) %collective-permute-start.1) | collective-permute-done | bytes 262176 | tf_op jit(solution)/shard_map/ppermute | solution.py:369
  28.8 1.6 %gradient.1 = (bf16[8,64,256]{2,1,0:T(8,128)(2,1)S(1)}, bf16[256,256]{1,0:T(8,128)(2,1)S(1)}, bf16[256,256]{1,0:T(8,128)(2,1)S(1)}, bf16[4,2,64,256]{3,2,1,0:T(8,128)(2,1)S(1)}) custom-call(s32[1]{0:T(128)} %bitcast.2.core_ref, s32[1]{0:T(128)} %bitcast.group_ref, bf16[512,512]{1,0:T(8,128)(2,1)S(1)} %copy-done, ...), custom_call_target="tpu_custom_call" | custom-call | flops 134217728 | bytes 3899400 | tf_op jit(solution)/shard_map/gradient/pallas_call | solution.py:326
  30.4 0.1 collective-permute-start.2
  30.5 0.3 keep.1
  30.8 1.2 %collective-permute-done.2 = bf16[8,64,256]{2,1,0:T(8,128)(2,1)S(1)} collective-permute-done((bf16[8,64,256]{2,1,0:T(8,128)(2,1)S(1)}, bf16[8,64,256]{2,1,0:T(8,128)(2,1)S(1)}, u32[]{:S(2)}, u32[]{:S(2)}) %collective-permute-start.2) | collective-permute-done | bytes 262176 | tf_op jit(solution)/shard_map/ppermute | solution.py:488
  32.0 0.1 add_convert_fusion
  32.1 12.2 %all_to_all.10 = bf16[8,64,256]{2,1,0:T(8,128)(2,1)S(1)} all-to-all(bf16[8,64,256]{2,1,0:T(8,128)(2,1)S(1)} %add_convert_fusion), channel_id=1, replica_groups={{0,2,4,6,8,10,12,14},{1,3,5,7,9,11,13,15},{16,18,20,22,24,26,28,30},{17..., dimensions={0} | all-to-all | bytes 524288 | tf_op jit(solution)/shard_map/all_to_all | solution.py:489
  44.3 1.6 %collective-permute-start.3 = (bf16[64,256]{1,0:T(8,128)(2,1)S(1)}, bf16[64,256]{1,0:T(8,128)(2,1)S(1)}, u32[]{:S(2)}, u32[]{:S(2)}) collective-permute-start(bf16[64,256]{1,0:T(8,128)(2,1)S(1)} %reduce_sum.12), channel_id=1, source_target_pairs={{16,0},{0,16},{17,1},{1,17},{18,2},{2,18},{19,3},{3,19},{20,4},{4,... | collective-permute-start | bytes 98312 | tf_op jit(solution)/shard_map/ppermute | solution.py:369
  45.8 2.4 %collective-permute-done.3 = bf16[64,256]{1,0:T(8,128)(2,1)S(1)} collective-permute-done((bf16[64,256]{1,0:T(8,128)(2,1)S(1)}, bf16[64,256]{1,0:T(8,128)(2,1)S(1)}, u32[]{:S(2)}, u32[]{:S(2)}) %collective-permute-start.3) | collective-permute-done | bytes 32800 | tf_op jit(solution)/shard_map/ppermute | solution.py:369
  48.2 0.6 %maximum_select_fusion = bf16[64,512]{1,0:T(8,128)(2,1)} fusion(bf16[64,256]{1,0:T(8,128)(2,1)S(1)} %collective-permute-done.3, bf16[64,256]{1,0:T(8,128)(2,1)S(1)} %reduce_sum.12, pred[]{:T(512)S(6)} %eq.3), kind=kLoop, calls=%fused_computation.1 | loop fusion | flops 294912 | bytes 131073 | tf_op jit(solution)/shard_map/jit(_where)/select_n | solution.py:500
  (1 shorter events, 0.0 us)
Async XLA Ops:
  0.6 11.2 %copy-start.5 = (s32[1,16,16]{2,1,0:T(8,128)S(1)}, s32[1,16,16]{2,1,0:T(8,128)}, u32[]{:S(2)}) copy-start(s32[1,16,16]{2,1,0:T(8,128)} %target_ref.1) | copy-start | bytes 3076
  2.6 9.2 %copy-start.1 = (bf16[256,512]{1,0:T(8,128)(2,1)S(1)}, bf16[256,512]{1,0:T(8,128)(2,1)}, u32[]{:S(2)}) copy-start(bf16[256,512]{1,0:T(8,128)(2,1)} %x_ref.1) | copy-start | bytes 786436
  2.6 9.2 %copy-start.4 = (bf16[1,2,4,128,128]{4,3,2,1,0:T(8,128)(2,1)S(1)}, bf16[1,2,4,128,128]{4,3,2,1,0:T(8,128)(2,1)}, u32[]{:S(2)}) copy-start(bf16[1,2,4,128,128]{4,3,2,1,0:T(8,128)(2,1)} %values_ref.1) | copy-start | bytes 786436
  2.6 17.6 %all-to-all-start = ((bf16[16,16,512]{2,1,0:T(8,128)(2,1)}), bf16[16,16,512]{2,1,0:T(8,128)(2,1)S(1)}, u32[]{:S(2)}, u32[]{:S(2)}) async-start(bf16[16,16,512]{2,1,0:T(8,128)(2,1)} %get-tuple-element.22), calls=%async_computation | async-start | bytes 524288 | tf_op jit(solution)/shard_map/all_to_all | solution.py:399
  10.2 1.6 %copy-start.6 = (s32[1,2,4]{2,1,0:T(2,128)S(1)}, s32[1,2,4]{2,1,0:T(2,128)}, u32[]{:S(2)}) copy-start(s32[1,2,4]{2,1,0:T(2,128)} %columns_ref.1) | copy-start | bytes 100
  10.2 11.9 %collective-permute-start = (bf16[272,512]{1,0:T(8,128)(2,1)}, bf16[272,512]{1,0:T(8,128)(2,1)S(1)}, u32[]{:S(2)}, u32[]{:S(2)}) collective-permute-start(bf16[272,512]{1,0:T(8,128)(2,1)} %get-tuple-element.25.refs_0_), channel_id=1, source_target_pairs={{16,0},{0,16},{17,1},{1,17},{18,2},{2,18},{19,3},{3,19},{20,4},{4,... | collective-permute-start | bytes 835592 | tf_op jit(solution)/shard_map/ppermute | solution.py:369
  20.2 1.9 %copy-start = (bf16[512,512]{1,0:T(8,128)(2,1)S(1)}, bf16[512,512]{1,0:T(8,128)(2,1)}, u32[]{:S(2)}) copy-start(bf16[512,512]{1,0:T(8,128)(2,1)} %weight_neigh_ref.3) | copy-start | bytes 1572868
  20.2 1.9 %copy-start.2 = (bf16[512,512]{1,0:T(8,128)(2,1)S(1)}, bf16[512,512]{1,0:T(8,128)(2,1)}, u32[]{:S(2)}) copy-start(bf16[512,512]{1,0:T(8,128)(2,1)} %weight_self_ref.1) | copy-start | bytes 1572868
  20.2 1.9 %copy-start.3 = (bf16[272,512]{1,0:T(8,128)(2,1)S(1)}, bf16[272,512]{1,0:T(8,128)(2,1)}, u32[]{:S(2)}) copy-start(bf16[272,512]{1,0:T(8,128)(2,1)} %get-tuple-element.25.refs_0_) | copy-start | bytes 835588
  20.6 8.2 %collective-permute-start.1 = (bf16[256,512]{1,0:T(8,128)(2,1)S(1)}, bf16[256,512]{1,0:T(8,128)(2,1)S(1)}, u32[]{:S(2)}, u32[]{:S(2)}) collective-permute-start(bf16[256,512]{1,0:T(8,128)(2,1)S(1)} %aggregate.1.aggregate_ref), channel_id=1, source_target_pairs={{16,0},{0,16},{17,1},{1,17},{18,2},{2,18},{19,3},{3,19},{20,4},{4,... | collective-permute-start | bytes 786440 | tf_op jit(solution)/shard_map/ppermute | solution.py:369
  30.4 1.6 %collective-permute-start.2 = (bf16[8,64,256]{2,1,0:T(8,128)(2,1)S(1)}, bf16[8,64,256]{2,1,0:T(8,128)(2,1)S(1)}, u32[]{:S(2)}, u32[]{:S(2)}) collective-permute-start(bf16[8,64,256]{2,1,0:T(8,128)(2,1)S(1)} %get-tuple-element.41), channel_id=1, source_target_pairs={{0,1},{1,0},{2,3},{3,2},{4,5},{5,4},{6,7},{7,6},{8,9},{9,8},{10,11... | collective-permute-start | bytes 786440 | tf_op jit(solution)/shard_map/ppermute | solution.py:488
  44.3 4.0 %collective-permute-start.3 = (bf16[64,256]{1,0:T(8,128)(2,1)S(1)}, bf16[64,256]{1,0:T(8,128)(2,1)S(1)}, u32[]{:S(2)}, u32[]{:S(2)}) collective-permute-start(bf16[64,256]{1,0:T(8,128)(2,1)S(1)} %reduce_sum.12), channel_id=1, source_target_pairs={{16,0},{0,16},{17,1},{1,17},{18,2},{2,18},{19,3},{3,19},{20,4},{4,... | collective-permute-start | bytes 98312 | tf_op jit(solution)/shard_map/ppermute | solution.py:369

commit v6 on v5

--- a/solution.py
+++ b/solution.py
@@ -175,7 +175,7 @@
     candidates = members * negatives
     joined, refs = refs[:members], refs[members:]
     (embeds_hbm, embeds_ref, part_ref, scale_ref, turned_ref), refs = refs[:5], refs[5:]
-    (pair_ref, rest_ref, hot_ref, hot_turned_ref), refs = refs[:4], refs[4:]
+    (pair_ref, rest_ref, hot_ref), refs = refs[:3], refs[3:]
     pres, x_turned, sem = refs[: members - 1], refs[members - 1 : -1], refs[-1]
     aggregate = aggregate_ref[...]
     nodes = aggregate.shape[0]
@@ -199,19 +199,17 @@
         relative = jnp.where(relative < 0.0, relative + candidates, relative)
         query_hot = one_hot(iota((nodes, queries), 0).astype(F32) == query)
         positive_hot = one_hot(iota((candidates, queries), 0).astype(F32) == relative)
-        pair = dot(query_hot, positive_hot, 1, 1)
-        lanes = slice(member * candidates, (member + 1) * candidates)
+        pair = dot(positive_hot, query_hot, 1, 1)
+        lanes = slice(member * nodes, (member + 1) * nodes)
         pair_ref[:, lanes] = pair
-        rest_ref[:, lanes] = jnp.sum(pair, axis=1, keepdims=True) - pair
+        rest_ref[:, lanes] = jnp.sum(pair, axis=0, keepdims=True) - pair
         square = (negatives, negatives)
         column = jnp.where(iota(square, 0) == iota(square, 1), negative, 0.0)
         column = jnp.sum(column, axis=1, keepdims=True)
-        hot_ref[member] = one_hot(iota((negatives, nodes), 1).astype(F32) == column)
-        turned = one_hot(iota((nodes, negatives), 0).astype(F32) == negative)
-        blank = jnp.zeros((nodes, negatives), BF16)
-        hot_turned_ref[:, lanes] = jnp.concatenate(
-            [turned if n == member else blank for n in range(members)], axis=1
-        )
+        hot = one_hot(iota((negatives, nodes), 1).astype(F32) == column)
+        for n in range(members):
+            block = hot if n == member else jnp.zeros_like(hot)
+            hot_ref[n * negatives : (n + 1) * negatives, lanes] = block
     copy.wait()
 
 
@@ -243,18 +241,17 @@
     pair_ref,
     rest_ref,
     hot_ref,
-    hot_turned_ref,
     x_turned_ref,
     turned_ref,
     *refs,
 ):
-    members, negatives, _ = hot_ref.shape
+    candidates, nodes = hot_ref.shape[0], embeds_ref.shape[0]
+    members = hot_ref.shape[1] // nodes
+    negatives = candidates // members
     others = members - 1
     given, refs = refs[: 3 * others], refs[3 * others :]
     send_ref, pre_grad_refs, other_turned = refs[0], refs[1 : 1 + members], refs[1 + members :]
-    candidates = members * negatives
     width = embeds_ref.shape[1]
-    columns = width // members
     group = group_ref[0]
     score_factor = 1.0 / math.sqrt(width)
     factor = LOSS_FACTOR / query_total
@@ -272,43 +269,31 @@
         x_turned.append(other_x_turned_ref)
         turned.append(other_turned_ref)
 
-    cand = jnp.concatenate(
-        [dot(hot_ref[m], embeds[m]).astype(BF16) for m in range(members)], axis=0
-    )
-
-    def at(member, block, count=members):
-        zero = jnp.zeros_like(block)
-        return jnp.concatenate([block if n == member else zero for n in range(count)], axis=0)
-
-    product = sum(dot(embeds[m], at(m, cand), 1, 1) for m in range(members))
+    lanes = [slice(m * nodes, (m + 1) * nodes) for m in range(members)]
+    hot = hot_ref[...]
+    own = [hot[m * negatives : (m + 1) * negatives, lanes[m]] for m in range(members)]
+    cand = jnp.concatenate([dot(own[m], embeds[m]).astype(BF16) for m in range(members)], axis=0)
+    product = jnp.concatenate([dot(cand, embeds[m], 1, 1) for m in range(members)], axis=1)
     sigma = jax.nn.sigmoid(score_factor * product)
     at_positive = ((sigma - 1.0) * factor).astype(BF16).astype(F32)
     elsewhere = ((sigma / (candidates - 1.0)) * factor).astype(BF16).astype(F32)
     grad = score_factor * (rest_ref[...] * elsewhere + pair_ref[...] * at_positive)
     grad = grad.astype(BF16)
+    cand_grad = sum(
+        dot(grad[:, lanes[m]], parts[m].astype(BF16)) for m in range(members)
+    ).astype(BF16)
 
     weighted = grad.astype(F32) * product
-    hot_turned = hot_turned_ref[...]
-    as_cand = jnp.sum(weighted, axis=0, keepdims=True)
-    as_cand = sum(as_cand[:, m * candidates : (m + 1) * candidates] for m in range(members))
-    weighted += hot_turned.astype(F32) * jnp.concatenate([as_cand] * members, axis=1)
-
-    cand_part = columns_of(group, members, cand)
-    grad_turned = grad.T
-    cand_grad = sum(
-        dot(grad_turned[m * candidates : (m + 1) * candidates], parts[m].astype(BF16))
+    weighted += hot.astype(F32) * jnp.sum(weighted, axis=1, keepdims=True)
+    inner = jnp.sum(weighted, axis=0, keepdims=True) / width
+    inner = jnp.broadcast_to(inner, (8, inner.shape[1])).T[:, :1]
+
+    left = jnp.concatenate([grad, hot], axis=0)
+    right = jnp.concatenate([columns_of(group, members, cand), cand_grad], axis=0)
+    pre_grads = [
+        (scales[m] * (dot(left[:, lanes[m]], right, 0, 0) - parts[m] * inner[lanes[m]])).astype(BF16)
         for m in range(members)
-    ).astype(BF16)
-    left = jnp.concatenate([grad, hot_turned], axis=1)
-    lane = iota(weighted.shape, 1)
-    pre_grads = []
-    for m in range(members):
-        right = jnp.concatenate([at(m, cand_part), at(m, cand_grad)], axis=0)
-        mine = (lane >= m * candidates) & (lane < (m + 1) * candidates)
-        inner = jnp.sum(jnp.where(mine, weighted, 0.0), axis=1, keepdims=True)
-        pre_grad = scales[m] * (dot(left, right) - parts[m] * (inner / width))
-        pre_grads.append(pre_grad.astype(BF16))
-
+    ]
     for ref, pre_grad in zip(pre_grad_refs, pre_grads):
         ref[...] = pre_grad
     rows_of_core(1 - core_ref[0], send_ref, (x_turned, turned), pre_grads)
@@ -419,7 +404,7 @@
     other_aggregate = of_others(aggregate)
     node_turned = ((half, 2, rows, nodes), BF16, VMEM)
     core, group_place = core.reshape(1), (group.reshape(1), SMEM)
-    embeds_out, embeds, part, scale, turned, pair, rest, hot, hot_turned, *made = call(
+    embeds_out, embeds, part, scale, turned, pair, rest, hot, *made = call(
         functools.partial(embed_kernel, groups, (queries, negatives)),
         "embed",
         [
@@ -428,10 +413,9 @@
             ((nodes, columns), F32, VMEM),
             ((nodes, 128), F32, VMEM),
             node_turned,
-            ((nodes, groups * candidates), F32, VMEM),
-            ((nodes, groups * candidates), F32, VMEM),
-            ((groups, negatives, nodes), BF16, VMEM),
-            ((nodes, groups * candidates), BF16, VMEM),
+            ((candidates, groups * nodes), F32, VMEM),
+            ((candidates, groups * nodes), F32, VMEM),
+            ((candidates, groups * nodes), BF16, VMEM),
         ]
         + [((nodes, width), F32, VMEM)] * others
         + [node_turned] * groups,
@@ -462,7 +446,6 @@
                 pair,
                 rest,
                 hot,
-                hot_turned,
                 x_turned,
                 turned,
                 *members,

time: 49.2 us -> 49 us (level)
  no operation moved by 1% of the time
where the time goes in v6:
time: 49 us; the launch traced here: 48.7 us
  waiting for transfers between devices  16.3 us (33%)
  starting transfers between devices  12.3 us (25%)
  blocking collectives  12.2 us (25%)
  Pallas kernels  6.43 us (13%)
  between operations  0.76 us (2%)
  other arithmetic  0.75 us (2%)
    all_to_all x1, blocking collectives, on_device(): lax.all_to_all(chip_sum, 'dom', split_axis=0, concat_axis=0, axis_index_g...  12.2 us
    ppermute x3, waiting for transfers between devices, of_others(): lax.ppermute(own, 'group', [((g + k) % groups, g) for g in range(groups)])  7.75 us
    all_to_all x1, starting transfers between devices, on_device(): lax.all_to_all(outgoing, 'dom', split_axis=0, concat_axis=0, tiled=True)  7.56 us
    all_to_all x1, waiting for transfers between devices, on_device(): lax.all_to_all(outgoing, 'dom', split_axis=0, concat_axis=0, tiled=True)  7.35 us
    pallas_call x6, Pallas kernels, call(): pl.pallas_call(kernel, name=name, out_shape=shapes, in_specs=[place for _...  6.43 us
    ppermute x3, starting transfers between devices, of_others(): lax.ppermute(own, 'group', [((g + k) % groups, g) for g in range(groups)])  4.67 us
    ppermute x1, waiting for transfers between devices, on_device(): lax.ppermute(send, 'dom', swap).astype(F32)  1.21 us
  transfers between devices with their start and end apart: 5, of which 4 were waited for; matrix products, arithmetic and copies ran while one was open for 0% of the time, Pallas kernels for 6%

profile of v6, /device:TPU:0, one launch (start us, length us, event | category | flops | bytes accessed | tf_op | source)
XLA Modules:
  0.0 48.7 jit_solution(44444032478782839)
XLA Ops:
  0.6 0.0 copy-start.5
  0.6 2.0 %pack.1 = (bf16[16,16,512]{2,1,0:T(8,128)(2,1)}, bf16[272,512]{1,0:T(8,128)(2,1)}) custom-call(s32[1,16,16]{2,1,0:T(8,128)} %rows_hbm.1, s32[1,16]{1,0:T(1,128)} %count_hbm.1, bf16[256,512]{1,0:T(8,128)(2,1)} %x_ref.1, s32[1,512]{1,0:T(1,128)} %query_hbm.1, s32[1,512]{1,0:T(1,128)} %positive_hbm.1, s32[1,32]{1,0:T(1,128)} %negative_hbm.1), custom_call_target="tpu_custom_call" | custom-call | flops 67108864 | bytes 808128 | tf_op jit(solution)/shard_map/pack/pallas_call | solution.py:311
  2.6 0.0 copy-start.1
  2.6 0.0 copy-start.4
  2.6 7.6 %all-to-all-start = ((bf16[16,16,512]{2,1,0:T(8,128)(2,1)}), bf16[16,16,512]{2,1,0:T(8,128)(2,1)S(1)}, u32[]{:S(2)}, u32[]{:S(2)}) async-start(bf16[16,16,512]{2,1,0:T(8,128)(2,1)} %get-tuple-element.21), calls=%async_computation | async-start | bytes 524288 | tf_op jit(solution)/shard_map/all_to_all | solution.py:384
  10.2 0.0 copy-start.6
  10.2 1.6 %collective-permute-start = (bf16[272,512]{1,0:T(8,128)(2,1)}, bf16[272,512]{1,0:T(8,128)(2,1)S(1)}, u32[]{:S(2)}, u32[]{:S(2)}) collective-permute-start(bf16[272,512]{1,0:T(8,128)(2,1)} %get-tuple-element.24.refs_0_), channel_id=1, source_target_pairs={{16,0},{0,16},{17,1},{1,17},{18,2},{2,18},{19,3},{3,19},{20,4},{4,... | collective-permute-start | bytes 835592 | tf_op jit(solution)/shard_map/ppermute | solution.py:354
  11.8 0.0 copy-done.5
  11.8 0.0 copy-done.1
  11.8 0.0 copy-done.4
  11.8 0.0 copy-done.6
  11.8 1.1 %local.1 = (f32[256,512]{1,0:T(8,128)S(1)}, f32[256,384]{1,0:T(8,128)S(1)}) custom-call(s32[1,2,4]{2,1,0:T(2,128)S(1)} %copy-done.6, bf16[1,2,4,128,128]{4,3,2,1,0:T(8,128)(2,1)S(1)} %copy-done.4, bf16[256,512]{1,0:T(8,128)(2,1)S(1)} %copy-done.1, s32[1,16,16]{2,1,0:T(8,128)S(1)} %copy-done.5), custom_call_target="tpu_custom_call" | custom-call | flops 134217728 | bytes 1442848 | tf_op jit(solution)/shard_map/local/pallas_call | solution.py:311
  12.9 7.4 %all-to-all-done = bf16[16,16,512]{2,1,0:T(8,128)(2,1)S(1)} async-done(((bf16[16,16,512]{2,1,0:T(8,128)(2,1)}), bf16[16,16,512]{2,1,0:T(8,128)(2,1)S(1)}, u32[]{:S(2)}, u32[]{:S(2)}) %all-to-all-start) | async-done | bytes 262176 | tf_op jit(solution)/shard_map/all_to_all | solution.py:384
  20.2 0.0 copy-start
  20.2 0.0 copy-start.2
  20.2 0.0 copy-start.3
  20.2 0.3 aggregate.1.aggregate_ref
  20.6 1.6 %collective-permute-start.1 = (bf16[256,512]{1,0:T(8,128)(2,1)S(1)}, bf16[256,512]{1,0:T(8,128)(2,1)S(1)}, u32[]{:S(2)}, u32[]{:S(2)}) collective-permute-start(bf16[256,512]{1,0:T(8,128)(2,1)S(1)} %aggregate.1.aggregate_ref), channel_id=1, source_target_pairs={{16,0},{0,16},{17,1},{1,17},{18,2},{2,18},{19,3},{3,19},{20,4},{4,... | collective-permute-start | bytes 786440 | tf_op jit(solution)/shard_map/ppermute | solution.py:354
  22.1 0.0 collective-permute-done.refs_1_
  22.1 0.0 copy-done
  22.1 0.0 copy-done.2
  22.1 0.0 copy-done.3
  22.1 1.3 %embed.1 = (bf16[256,512]{1,0:T(8,128)(2,1)}, bf16[256,512]{1,0:T(8,128)(2,1)S(1)}, f32[256,256]{1,0:T(8,128)S(1)}, f32[256,128]{1,0:T(8,128)S(1)}, bf16[4,2,64,...) custom-call(s32[1]{0:T(128)} %bitcast.group_ref, ...), custom_call_target="tpu_custom_call" | custom-call | flops 268435456 | bytes 4423684 | tf_op jit(solution)/shard_map/embed/pallas_call | solution.py:311
  23.4 5.3 %collective-permute-done.1.refs_0_ = bf16[256,512]{1,0:T(8,128)(2,1)S(1)} collective-permute-done((bf16[256,512]{1,0:T(8,128)(2,1)S(1)}, bf16[256,512]{1,0:T(8,128)(2,1)S(1)}, u32[]{:S(2)}, u32[]{:S(2)}) %collective-permute-start.1) | collective-permute-done | bytes 262176 | tf_op jit(solution)/shard_map/ppermute | solution.py:354
  28.8 1.5 %gradient.1 = (bf16[8,64,256]{2,1,0:T(8,128)(2,1)S(1)}, bf16[256,256]{1,0:T(8,128)(2,1)S(1)}, bf16[256,256]{1,0:T(8,128)(2,1)S(1)}, bf16[4,2,64,256]{3,2,1,0:T(8,128)(2,1)S(1)}) custom-call(s32[1]{0:T(128)} %bitcast.2.core_ref, s32[1]{0:T(128)} %bitcast.group_ref, bf16[512,512]{1,0:T(8,128)(2,1)S(1)} %copy-done, ...), custom_call_target="tpu_custom_call" | custom-call | flops 134217728 | bytes 3866632 | tf_op jit(solution)/shard_map/gradient/pallas_call | solution.py:311
  30.2 0.1 collective-permute-start.2
  30.3 0.3 keep.1
  30.6 1.2 %collective-permute-done.2 = bf16[8,64,256]{2,1,0:T(8,128)(2,1)S(1)} collective-permute-done((bf16[8,64,256]{2,1,0:T(8,128)(2,1)S(1)}, bf16[8,64,256]{2,1,0:T(8,128)(2,1)S(1)}, u32[]{:S(2)}, u32[]{:S(2)}) %collective-permute-start.2) | collective-permute-done | bytes 262176 | tf_op jit(solution)/shard_map/ppermute | solution.py:471
  31.8 0.1 add_convert_fusion
  31.9 12.2 %all_to_all.10 = bf16[8,64,256]{2,1,0:T(8,128)(2,1)S(1)} all-to-all(bf16[8,64,256]{2,1,0:T(8,128)(2,1)S(1)} %add_convert_fusion), channel_id=1, replica_groups={{0,2,4,6,8,10,12,14},{1,3,5,7,9,11,13,15},{16,18,20,22,24,26,28,30},{17..., dimensions={0} | all-to-all | bytes 524288 | tf_op jit(solution)/shard_map/all_to_all | solution.py:472
  44.1 1.6 %collective-permute-start.3 = (bf16[64,256]{1,0:T(8,128)(2,1)S(1)}, bf16[64,256]{1,0:T(8,128)(2,1)S(1)}, u32[]{:S(2)}, u32[]{:S(2)}) collective-permute-start(bf16[64,256]{1,0:T(8,128)(2,1)S(1)} %reduce_sum.12), channel_id=1, source_target_pairs={{16,0},{0,16},{17,1},{1,17},{18,2},{2,18},{19,3},{3,19},{20,4},{4,... | collective-permute-start | bytes 98312 | tf_op jit(solution)/shard_map/ppermute | solution.py:354
  45.7 2.4 %collective-permute-done.3 = bf16[64,256]{1,0:T(8,128)(2,1)S(1)} collective-permute-done((bf16[64,256]{1,0:T(8,128)(2,1)S(1)}, bf16[64,256]{1,0:T(8,128)(2,1)S(1)}, u32[]{:S(2)}, u32[]{:S(2)}) %collective-permute-start.3) | collective-permute-done | bytes 32800 | tf_op jit(solution)/shard_map/ppermute | solution.py:354
  48.1 0.6 %maximum_select_fusion = bf16[64,512]{1,0:T(8,128)(2,1)} fusion(bf16[64,256]{1,0:T(8,128)(2,1)S(1)} %collective-permute-done.3, bf16[64,256]{1,0:T(8,128)(2,1)S(1)} %reduce_sum.12, pred[]{:T(512)S(6)} %eq.3), kind=kLoop, calls=%fused_computation.1 | loop fusion | flops 294912 | bytes 131073 | tf_op jit(solution)/shard_map/jit(_where)/select_n | solution.py:483
  (1 shorter events, 0.0 us)
Async XLA Ops:
  0.6 11.2 %copy-start.5 = (s32[1,16,16]{2,1,0:T(8,128)S(1)}, s32[1,16,16]{2,1,0:T(8,128)}, u32[]{:S(2)}) copy-start(s32[1,16,16]{2,1,0:T(8,128)} %target_ref.1) | copy-start | bytes 3076
  2.6 9.2 %copy-start.1 = (bf16[256,512]{1,0:T(8,128)(2,1)S(1)}, bf16[256,512]{1,0:T(8,128)(2,1)}, u32[]{:S(2)}) copy-start(bf16[256,512]{1,0:T(8,128)(2,1)} %x_ref.1) | copy-start | bytes 786436
  2.6 9.2 %copy-start.4 = (bf16[1,2,4,128,128]{4,3,2,1,0:T(8,128)(2,1)S(1)}, bf16[1,2,4,128,128]{4,3,2,1,0:T(8,128)(2,1)}, u32[]{:S(2)}) copy-start(bf16[1,2,4,128,128]{4,3,2,1,0:T(8,128)(2,1)} %values_ref.1) | copy-start | bytes 786436
  2.6 17.6 %all-to-all-start = ((bf16[16,16,512]{2,1,0:T(8,128)(2,1)}), bf16[16,16,512]{2,1,0:T(8,128)(2,1)S(1)}, u32[]{:S(2)}, u32[]{:S(2)}) async-start(bf16[16,16,512]{2,1,0:T(8,128)(2,1)} %get-tuple-element.21), calls=%async_computation | async-start | bytes 524288 | tf_op jit(solution)/shard_map/all_to_all | solution.py:384
  10.2 1.6 %copy-start.6 = (s32[1,2,4]{2,1,0:T(2,128)S(1)}, s32[1,2,4]{2,1,0:T(2,128)}, u32[]{:S(2)}) copy-start(s32[1,2,4]{2,1,0:T(2,128)} %columns_ref.1) | copy-start | bytes 100
  10.2 11.9 %collective-permute-start = (bf16[272,512]{1,0:T(8,128)(2,1)}, bf16[272,512]{1,0:T(8,128)(2,1)S(1)}, u32[]{:S(2)}, u32[]{:S(2)}) collective-permute-start(bf16[272,512]{1,0:T(8,128)(2,1)} %get-tuple-element.24.refs_0_), channel_id=1, source_target_pairs={{16,0},{0,16},{17,1},{1,17},{18,2},{2,18},{19,3},{3,19},{20,4},{4,... | collective-permute-start | bytes 835592 | tf_op jit(solution)/shard_map/ppermute | solution.py:354
  20.2 1.9 %copy-start = (bf16[512,512]{1,0:T(8,128)(2,1)S(1)}, bf16[512,512]{1,0:T(8,128)(2,1)}, u32[]{:S(2)}) copy-start(bf16[512,512]{1,0:T(8,128)(2,1)} %weight_neigh_ref.3) | copy-start | bytes 1572868
  20.2 1.9 %copy-start.2 = (bf16[512,512]{1,0:T(8,128)(2,1)S(1)}, bf16[512,512]{1,0:T(8,128)(2,1)}, u32[]{:S(2)}) copy-start(bf16[512,512]{1,0:T(8,128)(2,1)} %weight_self_ref.1) | copy-start | bytes 1572868
  20.2 1.9 %copy-start.3 = (bf16[272,512]{1,0:T(8,128)(2,1)S(1)}, bf16[272,512]{1,0:T(8,128)(2,1)}, u32[]{:S(2)}) copy-start(bf16[272,512]{1,0:T(8,128)(2,1)} %get-tuple-element.24.refs_0_) | copy-start | bytes 835588
  20.6 8.2 %collective-permute-start.1 = (bf16[256,512]{1,0:T(8,128)(2,1)S(1)}, bf16[256,512]{1,0:T(8,128)(2,1)S(1)}, u32[]{:S(2)}, u32[]{:S(2)}) collective-permute-start(bf16[256,512]{1,0:T(8,128)(2,1)S(1)} %aggregate.1.aggregate_ref), channel_id=1, source_target_pairs={{16,0},{0,16},{17,1},{1,17},{18,2},{2,18},{19,3},{3,19},{20,4},{4,... | collective-permute-start | bytes 786440 | tf_op jit(solution)/shard_map/ppermute | solution.py:354
  30.2 1.6 %collective-permute-start.2 = (bf16[8,64,256]{2,1,0:T(8,128)(2,1)S(1)}, bf16[8,64,256]{2,1,0:T(8,128)(2,1)S(1)}, u32[]{:S(2)}, u32[]{:S(2)}) collective-permute-start(bf16[8,64,256]{2,1,0:T(8,128)(2,1)S(1)} %get-tuple-element.39), channel_id=1, source_target_pairs={{0,1},{1,0},{2,3},{3,2},{4,5},{5,4},{6,7},{7,6},{8,9},{9,8},{10,11... | collective-permute-start | bytes 786440 | tf_op jit(solution)/shard_map/ppermute | solution.py:471
  44.1 4.0 %collective-permute-start.3 = (bf16[64,256]{1,0:T(8,128)(2,1)S(1)}, bf16[64,256]{1,0:T(8,128)(2,1)S(1)}, u32[]{:S(2)}, u32[]{:S(2)}) collective-permute-start(bf16[64,256]{1,0:T(8,128)(2,1)S(1)} %reduce_sum.12), channel_id=1, source_target_pairs={{16,0},{0,16},{17,1},{1,17},{18,2},{2,18},{19,3},{3,19},{20,4},{4,... | collective-permute-start | bytes 98312 | tf_op jit(solution)/shard_map/ppermute | solution.py:354

commit v7 on v6

--- a/solution.py
+++ b/solution.py
@@ -135,7 +135,7 @@
     degree_ref[:, 128:] = jnp.where(iota((nodes, total), 0).astype(F32) == target, 1.0, 0.0)
 
 
-def aggregate_kernel(received_ref, local_ref, degree_ref, out_ref):
+def aggregate_kernel(received_ref, local_ref, degree_ref, head_ref, tail_ref):
     received = received_ref[...].astype(F32)
     live = received[:, :1] < DEAD_FLOOR
     weighted = jnp.where(live, received, 0.0).astype(BF16)
@@ -145,7 +145,9 @@
     summed = local_ref[...] + dot(hot, weighted)
     width = summed.shape[1]
     for first in range(0, width, 128):
-        out_ref[:, first : first + 128] = (summed[:, first : first + 128] / degree).astype(BF16)
+        mean = (summed[:, first : first + 128] / degree).astype(BF16)
+        head_ref[:, first : first + 128] = mean[: head_ref.shape[0]]
+        tail_ref[:, first : first + 128] = mean[head_ref.shape[0] :]
 
 
 def normed(pre):
@@ -166,7 +168,8 @@
     members,
     sizes,
     group_ref,
-    aggregate_ref,
+    head_ref,
+    tail_ref,
     weight_self_ref,
     weight_neigh_ref,
     *refs,
@@ -177,7 +180,7 @@
     (embeds_hbm, embeds_ref, part_ref, scale_ref, turned_ref), refs = refs[:5], refs[5:]
     (pair_ref, rest_ref, hot_ref), refs = refs[:3], refs[3:]
     pres, x_turned, sem = refs[: members - 1], refs[members - 1 : -1], refs[-1]
-    aggregate = aggregate_ref[...]
+    aggregate = jnp.concatenate([head_ref[...], tail_ref[...]], axis=0)
     nodes = aggregate.shape[0]
 
     own_pre = dot(joined[0][:nodes], weight_self_ref[...])
@@ -213,21 +216,39 @@
     copy.wait()
 
 
+def ahead_kernel(group_ref, weight_neigh_ref, *refs):
+    others = len(refs) // 6
+    members = others + 1
+    given, made = refs[: 2 * others], refs[2 * others :]
+    for other in range(others):
+        head_ref, pre_ref = given[2 * other : 2 * other + 2]
+        part_ref, embeds_ref, scale_ref, turned_ref = made[4 * other : 4 * other + 4]
+        aggregate = head_ref[...]
+        pre = pre_ref[: aggregate.shape[0]]
+        exact, scale = normed(pre + dot(aggregate, weight_neigh_ref[...]))
+        part_ref[...] = columns_of(group_ref[0], members, exact)
+        embeds_ref[...] = exact.astype(BF16)
+        scale_ref[...] = jnp.broadcast_to(scale, scale_ref.shape)
+        turned_ref[...] = aggregate.T.reshape(turned_ref.shape)
+
+
 def rows_of_core(core, ref, lefts, rights):
-    half, _, rows, nodes = lefts[0][0].shape
+    half, _, rows, nodes = lefts[0][0][0].shape
     columns = ref.shape[2]
     for part, left_refs in enumerate(lefts):
         block = jnp.zeros((half * rows, columns), F32)
-        for left_ref, right in zip(left_refs, rights):
-            block += dot(left_ref[:, core].reshape(half * rows, nodes), right)
+        for pieces, right in zip(left_refs, rights):
+            left = jnp.concatenate([piece[:, core] for piece in pieces], axis=2)
+            block += dot(left.reshape(half * rows, nodes), right)
         ref[part * half : (part + 1) * half] = block.reshape(half, rows, columns).astype(BF16)
 
 
-def keep_kernel(core_ref, *refs):
+def keep_kernel(members, core_ref, *refs):
     *refs, keep_ref = refs
-    members = len(refs) // 3
-    lefts = (refs[:members], refs[members : 2 * members])
-    rows_of_core(core_ref[0], keep_ref, lefts, [ref[...] for ref in refs[2 * members :]])
+    features, refs = [(ref,) for ref in refs[:members]], refs[members:]
+    rights, refs = refs[:members], refs[members:]
+    aggregates = [(refs[0],)] + [refs[n : n + 2] for n in range(1, len(refs), 2)]
+    rows_of_core(core_ref[0], keep_ref, (features, aggregates), [ref[...] for ref in rights])
 
 
 def gradient_kernel(
@@ -249,7 +270,7 @@
     members = hot_ref.shape[1] // nodes
     negatives = candidates // members
     others = members - 1
-    given, refs = refs[: 3 * others], refs[3 * others :]
+    given, refs = refs[: 7 * others], refs[7 * others :]
     send_ref, pre_grad_refs, other_turned = refs[0], refs[1 : 1 + members], refs[1 + members :]
     width = embeds_ref.shape[1]
     group = group_ref[0]
@@ -257,17 +278,19 @@
     factor = LOSS_FACTOR / query_total
 
     parts, scales, embeds = [part_ref[...]], [scale_ref[:, :1]], [embeds_ref[...]]
-    x_turned, turned = [x_turned_ref], [turned_ref]
-    for other, other_turned_ref in enumerate(other_turned):
-        aggregate_ref, pre_ref, other_x_turned_ref = given[3 * other : 3 * other + 3]
-        aggregate = aggregate_ref[...]
-        exact, scale = normed(pre_ref[...] + dot(aggregate, weight_neigh_ref[...]))
-        parts.append(columns_of(group, members, exact))
-        scales.append(scale)
-        embeds.append(exact.astype(BF16))
-        other_turned_ref[...] = aggregate.T.reshape(other_turned_ref.shape)
-        x_turned.append(other_x_turned_ref)
-        turned.append(other_turned_ref)
+    x_turned, turned = [(x_turned_ref,)], [(turned_ref,)]
+    for other, tail_turned_ref in enumerate(other_turned):
+        tail_ref, pre_ref, other_x_turned_ref, *first = given[7 * other : 7 * other + 7]
+        first_part_ref, first_embeds_ref, first_scale_ref, first_turned_ref = first
+        aggregate = tail_ref[...]
+        pre = pre_ref[nodes - aggregate.shape[0] :]
+        exact, scale = normed(pre + dot(aggregate, weight_neigh_ref[...]))
+        part = columns_of(group, members, exact)
+        parts.append(jnp.concatenate([first_part_ref[...], part], axis=0))
+        scales.append(jnp.concatenate([first_scale_ref[:, :1], scale], axis=0))
+        embeds.append(jnp.concatenate([first_embeds_ref[...], exact.astype(BF16)], axis=0))
+        x_turned.append((other_x_turned_ref,))
+        turned.append((first_turned_ref, tail_turned_ref))
 
     lanes = [slice(m * nodes, (m + 1) * nodes) for m in range(members)]
     hot = hot_ref[...]
@@ -294,6 +317,8 @@
         (scales[m] * (dot(left[:, lanes[m]], right, 0, 0) - parts[m] * inner[lanes[m]])).astype(BF16)
         for m in range(members)
     ]
+    for other, tail_turned_ref in enumerate(other_turned):
+        tail_turned_ref[...] = given[7 * other][...].T.reshape(tail_turned_ref.shape)
     for ref, pre_grad in zip(pre_grad_refs, pre_grads):
         ref[...] = pre_grad
     rows_of_core(1 - core_ref[0], send_ref, (x_turned, turned), pre_grads)
@@ -394,14 +419,15 @@
         flops=2 * nodes * width * tile_values.shape[2] * tile_values.shape[3],
         grant=grant,
     )
-    (aggregate,) = call(
+    first, last = nodes // 2, nodes - nodes // 2
+    head, tail = call(
         aggregate_kernel,
         "aggregate",
-        [((nodes, width), BF16, VMEM)],
+        [((first, width), BF16, VMEM), ((last, width), BF16, VMEM)],
         [(a, VMEM) for a in (received, local, degree)],
         flops=2 * nodes * total * width,
     )
-    other_aggregate = of_others(aggregate)
+    other_heads, other_tails = of_others(head), of_others(tail)
     node_turned = ((half, 2, rows, nodes), BF16, VMEM)
     core, group_place = core.reshape(1), (group.reshape(1), SMEM)
     embeds_out, embeds, part, scale, turned, pair, rest, hot, *made = call(
@@ -420,21 +446,37 @@
         + [((nodes, width), F32, VMEM)] * others
         + [node_turned] * groups,
         [group_place]
-        + [(a, VMEM) for a in (aggregate, weight_self, weight_neigh, *joined)],
+        + [(a, VMEM) for a in (head, tail, weight_self, weight_neigh, *joined)],
         flops=2 * nodes * width * width * groups,
         scratch=[pltpu.SemaphoreType.DMA],
         grant=grant,
     )
     x_turned, *features_turned = made[others:]
+    pres = made[:others]
+    ahead = call(
+        ahead_kernel,
+        "ahead",
+        [
+            ((first, columns), F32, VMEM),
+            ((first, width), BF16, VMEM),
+            ((first, 128), F32, VMEM),
+            ((half, 2, rows, first), BF16, VMEM),
+        ]
+        * others,
+        [group_place, (weight_neigh, VMEM)]
+        + [(a, VMEM) for pair_of in zip(other_heads, pres) for a in pair_of],
+        flops=2 * first * width * width,
+        grant=grant,
+    )
     members = []
-    for trio in zip(other_aggregate, made[:others], features_turned):
-        members += trio
+    for n in range(others):
+        members += [other_tails[n], pres[n], features_turned[n], *ahead[4 * n : 4 * n + 4]]
     send, *made = call(
         functools.partial(gradient_kernel, queries),
         "gradient",
         [((chips, rows, columns), BF16, VMEM)]
         + [((nodes, columns), BF16, VMEM)] * groups
-        + [node_turned] * others,
+        + [((half, 2, rows, last), BF16, VMEM)] * others,
         [(core, SMEM), group_place]
         + [
             (a, VMEM)
@@ -454,14 +496,15 @@
         flops=2 * nodes * width * width,
         grant=grant,
     )
-    features_turned = [x_turned] + features_turned
-    aggregates_turned = [turned] + made[groups:]
+    pieces = [turned]
+    for n in range(others):
+        pieces += [ahead[4 * n + 3], made[groups + n]]
     (keep,) = call(
-        keep_kernel,
+        functools.partial(keep_kernel, groups),
         "keep",
         [((chips, rows, columns), BF16, VMEM)],
         [(core, SMEM)]
-        + [(a, VMEM) for a in (*features_turned, *aggregates_turned, *made[:groups])],
+        + [(a, VMEM) for a in (x_turned, *features_turned, *made[:groups], *pieces)],
         flops=2 * nodes * width * width,
         grant=grant,
     )

time: 49 us -> 48.9 us (level)
  waiting for transfers between devices: 16.3 us -> 15.4 us
  starting transfers between devices: 12.3 us -> 12.8 us
    ppermute x3 -> x4, waiting for transfers between devices: 7.75 us -> 6.88 us  [of_others(): lax.ppermute(own, 'group', [((g + k) % groups, g) for g in range(groups)])]
    ppermute x3 -> x4, starting transfers between devices: 4.67 us -> 5.2 us  [of_others(): lax.ppermute(own, 'group', [((g + k) % groups, g) for g in range(groups)])]
    pallas_call x6 -> x7, Pallas kernels: 6.43 us -> 6.62 us  [call(): pl.pallas_call(kernel, name=name, out_shape=shapes, in_specs=[place for _...]
  transfers between devices with their start and end apart: 5 -> 6, of which waited for: 4 -> 5; matrix products, arithmetic and copies ran while one was open for 0% -> 0% of each run, Pallas kernels for 6% -> 7%
where the time goes in v7:
time: 48.9 us; the launch traced here: 48.6 us
  waiting for transfers between devices  15.4 us (31%)
  starting transfers between devices  12.8 us (26%)
  blocking collectives  12.2 us (25%)
  Pallas kernels  6.62 us (14%)
  between operations  0.77 us (2%)
  other arithmetic  0.75 us (2%)
    all_to_all x1, blocking collectives, on_device(): lax.all_to_all(chip_sum, 'dom', split_axis=0, concat_axis=0, axis_index_g...  12.2 us
    all_to_all x1, starting transfers between devices, on_device(): lax.all_to_all(outgoing, 'dom', split_axis=0, concat_axis=0, tiled=True)  7.56 us
    all_to_all x1, waiting for transfers between devices, on_device(): lax.all_to_all(outgoing, 'dom', split_axis=0, concat_axis=0, tiled=True)  7.34 us
    ppermute x4, waiting for transfers between devices, of_others(): lax.ppermute(own, 'group', [((g + k) % groups, g) for g in range(groups)])  6.88 us
    pallas_call x7, Pallas kernels, call(): pl.pallas_call(kernel, name=name, out_shape=shapes, in_specs=[place for _...  6.62 us
    ppermute x4, starting transfers between devices, of_others(): lax.ppermute(own, 'group', [((g + k) % groups, g) for g in range(groups)])  5.2 us
    ppermute x1, waiting for transfers between devices, on_device(): lax.ppermute(send, 'dom', swap).astype(F32)  1.21 us
  transfers between devices with their start and end apart: 6, of which 5 were waited for; matrix products, arithmetic and copies ran while one was open for 0% of the time, Pallas kernels for 7%

profile of v7, /device:TPU:0, one launch (start us, length us, event | category | flops | bytes accessed | tf_op | source)
XLA Modules:
  0.0 48.6 jit_solution(14578607685475511669)
XLA Ops:
  0.6 0.0 copy-start.5
  0.6 2.0 %pack.1 = (bf16[16,16,512]{2,1,0:T(8,128)(2,1)}, bf16[272,512]{1,0:T(8,128)(2,1)}) custom-call(s32[1,16,16]{2,1,0:T(8,128)} %rows_hbm.1, s32[1,16]{1,0:T(1,128)} %count_hbm.1, bf16[256,512]{1,0:T(8,128)(2,1)} %x_ref.1, s32[1,512]{1,0:T(1,128)} %query_hbm.1, s32[1,512]{1,0:T(1,128)} %positive_hbm.1, s32[1,32]{1,0:T(1,128)} %negative_hbm.1), custom_call_target="tpu_custom_call" | custom-call | flops 67108864 | bytes 808128 | tf_op jit(solution)/shard_map/pack/pallas_call | solution.py:336
  2.6 0.0 copy-start.1
  2.6 0.0 copy-start.4
  2.6 7.6 %all-to-all-start = ((bf16[16,16,512]{2,1,0:T(8,128)(2,1)}), bf16[16,16,512]{2,1,0:T(8,128)(2,1)S(1)}, u32[]{:S(2)}, u32[]{:S(2)}) async-start(bf16[16,16,512]{2,1,0:T(8,128)(2,1)} %get-tuple-element.27), calls=%async_computation | async-start | bytes 524288 | tf_op jit(solution)/shard_map/all_to_all | solution.py:409
  10.2 0.0 copy-start.6
  10.2 1.6 %collective-permute-start = (bf16[272,512]{1,0:T(8,128)(2,1)}, bf16[272,512]{1,0:T(8,128)(2,1)S(1)}, u32[]{:S(2)}, u32[]{:S(2)}) collective-permute-start(bf16[272,512]{1,0:T(8,128)(2,1)} %get-tuple-element.32.refs_0_), channel_id=1, source_target_pairs={{16,0},{0,16},{17,1},{1,17},{18,2},{2,18},{19,3},{3,19},{20,4},{4,... | collective-permute-start | bytes 835592 | tf_op jit(solution)/shard_map/ppermute | solution.py:379
  11.8 0.0 copy-done.5
  11.8 0.0 copy-done.1
  11.8 0.0 copy-done.4
  11.8 0.0 copy-done.6
  11.8 0.0 copy-start.3
  11.8 1.1 %local.1 = (f32[256,512]{1,0:T(8,128)S(1)}, f32[256,384]{1,0:T(8,128)S(1)}) custom-call(s32[1,2,4]{2,1,0:T(2,128)S(1)} %copy-done.6, bf16[1,2,4,128,128]{4,3,2,1,0:T(8,128)(2,1)S(1)} %copy-done.4, bf16[256,512]{1,0:T(8,128)(2,1)S(1)} %copy-done.1, s32[1,16,16]{2,1,0:T(8,128)S(1)} %copy-done.5), custom_call_target="tpu_custom_call" | custom-call | flops 134217728 | bytes 1442848 | tf_op jit(solution)/shard_map/local/pallas_call | solution.py:336
  12.9 7.3 %all-to-all-done = bf16[16,16,512]{2,1,0:T(8,128)(2,1)S(1)} async-done(((bf16[16,16,512]{2,1,0:T(8,128)(2,1)}), bf16[16,16,512]{2,1,0:T(8,128)(2,1)S(1)}, u32[]{:S(2)}, u32[]{:S(2)}) %all-to-all-start) | async-done | bytes 262176 | tf_op jit(solution)/shard_map/all_to_all | solution.py:409
  20.2 0.0 copy-start
  20.2 0.0 copy-start.2
  20.2 0.3 aggregate.1
  20.6 1.6 %collective-permute-start.2 = (bf16[128,512]{1,0:T(8,128)(2,1)S(1)}, bf16[128,512]{1,0:T(8,128)(2,1)S(1)}, u32[]{:S(2)}, u32[]{:S(2)}) collective-permute-start(bf16[128,512]{1,0:T(8,128)(2,1)S(1)} %get-tuple-element.30.head_ref), channel_id=1, source_target_pairs={{16,0},{0,16},{17,1},{1,17},{18,2},{2,18},{19,3},{3,19},{20,4},{4,... | collective-permute-start | bytes 393224 | tf_op jit(solution)/shard_map/ppermute | solution.py:379
  22.1 0.5 %collective-permute-start.1 = (bf16[128,512]{1,0:T(8,128)(2,1)S(1)}, bf16[128,512]{1,0:T(8,128)(2,1)S(1)}, u32[]{:S(2)}, u32[]{:S(2)}) collective-permute-start(bf16[128,512]{1,0:T(8,128)(2,1)S(1)} %get-tuple-element.31.tail_ref), channel_id=1, source_target_pairs={{16,0},{0,16},{17,1},{1,17},{18,2},{2,18},{19,3},{3,19},{20,4},{4,... | collective-permute-start | bytes 393224 | tf_op jit(solution)/shard_map/ppermute | solution.py:379
  22.7 0.0 collective-permute-done.refs_1_
  22.7 0.0 copy-done.3
  22.7 0.0 copy-done
  22.7 0.0 copy-done.2
  22.7 1.3 %embed.1 = (bf16[256,512]{1,0:T(8,128)(2,1)}, bf16[256,512]{1,0:T(8,128)(2,1)S(1)}, f32[256,256]{1,0:T(8,128)S(1)}, f32[256,128]{1,0:T(8,128)S(1)}, bf16[4,2,64,...) custom-call(s32[1]{0:T(128)} %bitcast.group_ref, ...), custom_call_target="tpu_custom_call" | custom-call | flops 268435456 | bytes 4423684 | tf_op jit(solution)/shard_map/embed/pallas_call | solution.py:336
  24.0 3.0 %collective-permute-done.2.refs_0_ = bf16[128,512]{1,0:T(8,128)(2,1)S(1)} collective-permute-done((bf16[128,512]{1,0:T(8,128)(2,1)S(1)}, bf16[128,512]{1,0:T(8,128)(2,1)S(1)}, u32[]{:S(2)}, u32[]{:S(2)}) %collective-permute-start.2) | collective-permute-done | bytes 131104 | tf_op jit(solution)/shard_map/ppermute | solution.py:379
  27.0 0.3 ahead.1
  27.3 1.4 %collective-permute-done.1.refs_0_ = bf16[128,512]{1,0:T(8,128)(2,1)S(1)} collective-permute-done((bf16[128,512]{1,0:T(8,128)(2,1)S(1)}, bf16[128,512]{1,0:T(8,128)(2,1)S(1)}, u32[]{:S(2)}, u32[]{:S(2)}) %collective-permute-start.1) | collective-permute-done | bytes 131104 | tf_op jit(solution)/shard_map/ppermute | solution.py:379
  28.8 1.3 %gradient.1 = (bf16[8,64,256]{2,1,0:T(8,128)(2,1)S(1)}, bf16[256,256]{1,0:T(8,128)(2,1)S(1)}, bf16[256,256]{1,0:T(8,128)(2,1)S(1)}, bf16[4,2,64,128]{3,2,1,0:T(8,128)(2,1)S(1)}) custom-call(s32[1]{0:T(128)} %bitcast.2.core_ref, s32[1]{0:T(128)} %bitcast.group_ref, bf16[512,512]{1,0:T(8,128)(2,1)S(1)} %copy-done, ...), custom_call_target="tpu_custom_call" | custom-call | flops 134217728 | bytes 4063240 | tf_op jit(solution)/shard_map/gradient/pallas_call | solution.py:336
  30.1 0.1 collective-permute-start.3
  30.2 0.3 keep.1
  30.5 1.2 %collective-permute-done.3 = bf16[8,64,256]{2,1,0:T(8,128)(2,1)S(1)} collective-permute-done((bf16[8,64,256]{2,1,0:T(8,128)(2,1)S(1)}, bf16[8,64,256]{2,1,0:T(8,128)(2,1)S(1)}, u32[]{:S(2)}, u32[]{:S(2)}) %collective-permute-start.3) | collective-permute-done | bytes 262176 | tf_op jit(solution)/shard_map/ppermute | solution.py:514
  31.7 0.1 add_convert_fusion
  31.8 12.2 %all_to_all.10 = bf16[8,64,256]{2,1,0:T(8,128)(2,1)S(1)} all-to-all(bf16[8,64,256]{2,1,0:T(8,128)(2,1)S(1)} %add_convert_fusion), channel_id=1, replica_groups={{0,2,4,6,8,10,12,14},{1,3,5,7,9,11,13,15},{16,18,20,22,24,26,28,30},{17..., dimensions={0} | all-to-all | bytes 524288 | tf_op jit(solution)/shard_map/all_to_all | solution.py:515
  44.0 1.6 %collective-permute-start.4 = (bf16[64,256]{1,0:T(8,128)(2,1)S(1)}, bf16[64,256]{1,0:T(8,128)(2,1)S(1)}, u32[]{:S(2)}, u32[]{:S(2)}) collective-permute-start(bf16[64,256]{1,0:T(8,128)(2,1)S(1)} %reduce_sum.12), channel_id=1, source_target_pairs={{16,0},{0,16},{17,1},{1,17},{18,2},{2,18},{19,3},{3,19},{20,4},{4,... | collective-permute-start | bytes 98312 | tf_op jit(solution)/shard_map/ppermute | solution.py:379
  45.5 2.4 %collective-permute-done.4 = bf16[64,256]{1,0:T(8,128)(2,1)S(1)} collective-permute-done((bf16[64,256]{1,0:T(8,128)(2,1)S(1)}, bf16[64,256]{1,0:T(8,128)(2,1)S(1)}, u32[]{:S(2)}, u32[]{:S(2)}) %collective-permute-start.4) | collective-permute-done | bytes 32800 | tf_op jit(solution)/shard_map/ppermute | solution.py:379
  48.0 0.6 %maximum_select_fusion = bf16[64,512]{1,0:T(8,128)(2,1)} fusion(bf16[64,256]{1,0:T(8,128)(2,1)S(1)} %collective-permute-done.4, bf16[64,256]{1,0:T(8,128)(2,1)S(1)} %reduce_sum.12, pred[]{:T(512)S(6)} %eq.3), kind=kLoop, calls=%fused_computation.1 | loop fusion | flops 294912 | bytes 131073 | tf_op jit(solution)/shard_map/jit(_where)/select_n | solution.py:526
  (1 shorter events, 0.0 us)
Async XLA Ops:
  0.6 11.2 %copy-start.5 = (s32[1,16,16]{2,1,0:T(8,128)S(1)}, s32[1,16,16]{2,1,0:T(8,128)}, u32[]{:S(2)}) copy-start(s32[1,16,16]{2,1,0:T(8,128)} %target_ref.1) | copy-start | bytes 3076
  2.6 9.2 %copy-start.1 = (bf16[256,512]{1,0:T(8,128)(2,1)S(1)}, bf16[256,512]{1,0:T(8,128)(2,1)}, u32[]{:S(2)}) copy-start(bf16[256,512]{1,0:T(8,128)(2,1)} %x_ref.1) | copy-start | bytes 786436
  2.6 9.2 %copy-start.4 = (bf16[1,2,4,128,128]{4,3,2,1,0:T(8,128)(2,1)S(1)}, bf16[1,2,4,128,128]{4,3,2,1,0:T(8,128)(2,1)}, u32[]{:S(2)}) copy-start(bf16[1,2,4,128,128]{4,3,2,1,0:T(8,128)(2,1)} %values_ref.1) | copy-start | bytes 786436
  2.6 17.6 %all-to-all-start = ((bf16[16,16,512]{2,1,0:T(8,128)(2,1)}), bf16[16,16,512]{2,1,0:T(8,128)(2,1)S(1)}, u32[]{:S(2)}, u32[]{:S(2)}) async-start(bf16[16,16,512]{2,1,0:T(8,128)(2,1)} %get-tuple-element.27), calls=%async_computation | async-start | bytes 524288 | tf_op jit(solution)/shard_map/all_to_all | solution.py:409
  10.2 1.6 %copy-start.6 = (s32[1,2,4]{2,1,0:T(2,128)S(1)}, s32[1,2,4]{2,1,0:T(2,128)}, u32[]{:S(2)}) copy-start(s32[1,2,4]{2,1,0:T(2,128)} %columns_ref.1) | copy-start | bytes 100
  10.2 12.4 %collective-permute-start = (bf16[272,512]{1,0:T(8,128)(2,1)}, bf16[272,512]{1,0:T(8,128)(2,1)S(1)}, u32[]{:S(2)}, u32[]{:S(2)}) collective-permute-start(bf16[272,512]{1,0:T(8,128)(2,1)} %get-tuple-element.32.refs_0_), channel_id=1, source_target_pairs={{16,0},{0,16},{17,1},{1,17},{18,2},{2,18},{19,3},{3,19},{20,4},{4,... | collective-permute-start | bytes 835592 | tf_op jit(solution)/shard_map/ppermute | solution.py:379
  11.8 10.9 %copy-start.3 = (bf16[272,512]{1,0:T(8,128)(2,1)S(1)}, bf16[272,512]{1,0:T(8,128)(2,1)}, u32[]{:S(2)}) copy-start(bf16[272,512]{1,0:T(8,128)(2,1)} %get-tuple-element.32.refs_0_) | copy-start | bytes 835588
  20.2 2.4 %copy-start = (bf16[512,512]{1,0:T(8,128)(2,1)S(1)}, bf16[512,512]{1,0:T(8,128)(2,1)}, u32[]{:S(2)}) copy-start(bf16[512,512]{1,0:T(8,128)(2,1)} %weight_neigh_ref.5) | copy-start | bytes 1572868
  20.2 2.4 %copy-start.2 = (bf16[512,512]{1,0:T(8,128)(2,1)S(1)}, bf16[512,512]{1,0:T(8,128)(2,1)}, u32[]{:S(2)}) copy-start(bf16[512,512]{1,0:T(8,128)(2,1)} %weight_self_ref.1) | copy-start | bytes 1572868
  20.6 6.4 %collective-permute-start.2 = (bf16[128,512]{1,0:T(8,128)(2,1)S(1)}, bf16[128,512]{1,0:T(8,128)(2,1)S(1)}, u32[]{:S(2)}, u32[]{:S(2)}) collective-permute-start(bf16[128,512]{1,0:T(8,128)(2,1)S(1)} %get-tuple-element.30.head_ref), channel_id=1, source_target_pairs={{16,0},{0,16},{17,1},{1,17},{18,2},{2,18},{19,3},{3,19},{20,4},{4,... | collective-permute-start | bytes 393224 | tf_op jit(solution)/shard_map/ppermute | solution.py:379
  22.1 6.6 %collective-permute-start.1 = (bf16[128,512]{1,0:T(8,128)(2,1)S(1)}, bf16[128,512]{1,0:T(8,128)(2,1)S(1)}, u32[]{:S(2)}, u32[]{:S(2)}) collective-permute-start(bf16[128,512]{1,0:T(8,128)(2,1)S(1)} %get-tuple-element.31.tail_ref), channel_id=1, source_target_pairs={{16,0},{0,16},{17,1},{1,17},{18,2},{2,18},{19,3},{3,19},{20,4},{4,... | collective-permute-start | bytes 393224 | tf_op jit(solution)/shard_map/ppermute | solution.py:379
  30.1 1.6 %collective-permute-start.3 = (bf16[8,64,256]{2,1,0:T(8,128)(2,1)S(1)}, bf16[8,64,256]{2,1,0:T(8,128)(2,1)S(1)}, u32[]{:S(2)}, u32[]{:S(2)}) collective-permute-start(bf16[8,64,256]{2,1,0:T(8,128)(2,1)S(1)} %get-tuple-element.51), channel_id=1, source_target_pairs={{0,1},{1,0},{2,3},{3,2},{4,5},{5,4},{6,7},{7,6},{8,9},{9,8},{10,11... | collective-permute-start | bytes 786440 | tf_op jit(solution)/shard_map/ppermute | solution.py:514
  44.0 4.0 %collective-permute-start.4 = (bf16[64,256]{1,0:T(8,128)(2,1)S(1)}, bf16[64,256]{1,0:T(8,128)(2,1)S(1)}, u32[]{:S(2)}, u32[]{:S(2)}) collective-permute-start(bf16[64,256]{1,0:T(8,128)(2,1)S(1)} %reduce_sum.12), channel_id=1, source_target_pairs={{16,0},{0,16},{17,1},{1,17},{18,2},{2,18},{19,3},{3,19},{20,4},{4,... | collective-permute-start | bytes 98312 | tf_op jit(solution)/shard_map/ppermute | solution.py:379

commit v8 on v7

--- a/solution.py
+++ b/solution.py
@@ -77,6 +77,7 @@
     index = jnp.sum(jnp.where(at_place, table, 0.0), axis=1, keepdims=True)
     count = jnp.sum(jnp.where(mine, count_ref[...].astype(F32), 0.0), axis=1, keepdims=True)
     live = place < count
+    index = jnp.where(live, index, -1.0)
     pick = one_hot(iota((total, nodes), 1).astype(F32) == index)
     for load in loads[3:]:
         load.wait()
@@ -95,7 +96,9 @@
     part = peers // 2
     for n in range(2):
         part_rows = slice(n * part * slots, (n + 1) * part * slots)
-        out = jnp.where(live[part_rows], dot(pick[part_rows], x_ref[...]), DEAD)
+        out = dot(pick[part_rows], x_ref[...])
+        marked = jnp.where(live[part_rows], out[:, :128], DEAD)
+        out = jnp.concatenate([marked, out[:, 128:]], axis=1)
         out_ref[n * part : (n + 1) * part] = out.astype(BF16).reshape(part, slots, width)
         piece = pl.ds(n * part, part)
         stores.append(
@@ -135,19 +138,19 @@
     degree_ref[:, 128:] = jnp.where(iota((nodes, total), 0).astype(F32) == target, 1.0, 0.0)
 
 
-def aggregate_kernel(received_ref, local_ref, degree_ref, head_ref, tail_ref):
-    received = received_ref[...].astype(F32)
-    live = received[:, :1] < DEAD_FLOOR
-    weighted = jnp.where(live, received, 0.0).astype(BF16)
+def aggregate_kernel(first, received_ref, local_ref, degree_ref, out_ref):
+    nodes = pl.ds(first, out_ref.shape[0])
+    received = received_ref[...]
+    marked = received[:, :128].astype(F32)
+    live = marked[:, :1] < DEAD_FLOOR
+    marked = jnp.where(live, marked, 0.0).astype(BF16)
+    weighted = jnp.concatenate([marked, received[:, 128:]], axis=1)
     flags = jnp.broadcast_to(jnp.where(live, 1.0, 0.0), (received.shape[0], 128)).astype(BF16)
-    hot = degree_ref[:, 128:].astype(BF16)
-    degree = degree_ref[:, :128] + dot(hot, flags)
-    summed = local_ref[...] + dot(hot, weighted)
-    width = summed.shape[1]
-    for first in range(0, width, 128):
-        mean = (summed[:, first : first + 128] / degree).astype(BF16)
-        head_ref[:, first : first + 128] = mean[: head_ref.shape[0]]
-        tail_ref[:, first : first + 128] = mean[head_ref.shape[0] :]
+    hot = degree_ref[nodes, 128:].astype(BF16)
+    degree = degree_ref[nodes, :128] + dot(hot, flags)
+    summed = local_ref[nodes, :] + dot(hot, weighted)
+    for lane in range(0, summed.shape[1], 128):
+        out_ref[:, lane : lane + 128] = (summed[:, lane : lane + 128] / degree).astype(BF16)
 
 
 def normed(pre):
@@ -420,12 +423,15 @@
         grant=grant,
     )
     first, last = nodes // 2, nodes - nodes // 2
-    head, tail = call(
-        aggregate_kernel,
-        "aggregate",
-        [((first, width), BF16, VMEM), ((last, width), BF16, VMEM)],
-        [(a, VMEM) for a in (received, local, degree)],
-        flops=2 * nodes * total * width,
+    head, tail = (
+        call(
+            functools.partial(aggregate_kernel, start),
+            "aggregate",
+            [((count, width), BF16, VMEM)],
+            [(a, VMEM) for a in (received, local, degree)],
+            flops=2 * count * total * width,
+        )[0]
+        for start, count in ((0, first), (first, last))
     )
     other_heads, other_tails = of_others(head), of_others(tail)
     node_turned = ((half, 2, rows, nodes), BF16, VMEM)

time: 48.9 us -> 48.9 us (level)
    pallas_call x7 -> x8, Pallas kernels: 6.62 us -> 6.88 us  [call(): pl.pallas_call(kernel, name=name, out_shape=shapes, in_specs=[place for _...]
where the time goes in v8:
time: 48.9 us; the launch traced here: 48.6 us
  waiting for transfers between devices  15.1 us (31%)
  starting transfers between devices  12.9 us (26%)
  blocking collectives  12.2 us (25%)
  Pallas kernels  6.88 us (14%)
  between operations  0.79 us (2%)
  other arithmetic  0.75 us (2%)
    all_to_all x1, blocking collectives, on_device(): lax.all_to_all(chip_sum, 'dom', split_axis=0, concat_axis=0, axis_index_g...  12.2 us
    all_to_all x1, starting transfers between devices, on_device(): lax.all_to_all(outgoing, 'dom', split_axis=0, concat_axis=0, tiled=True)  7.56 us
    all_to_all x1, waiting for transfers between devices, on_device(): lax.all_to_all(outgoing, 'dom', split_axis=0, concat_axis=0, tiled=True)  7.35 us
    pallas_call x8, Pallas kernels, call(): pl.pallas_call(kernel, name=name, out_shape=shapes, in_specs=[place for _...  6.88 us
    ppermute x4, waiting for transfers between devices, of_others(): lax.ppermute(own, 'group', [((g + k) % groups, g) for g in range(groups)])  6.51 us
    ppermute x4, starting transfers between devices, of_others(): lax.ppermute(own, 'group', [((g + k) % groups, g) for g in range(groups)])  5.27 us
    ppermute x1, waiting for transfers between devices, on_device(): lax.ppermute(send, 'dom', swap).astype(F32)  1.21 us
  transfers between devices with their start and end apart: 6, of which 5 were waited for; matrix products, arithmetic and copies ran while one was open for 0% of the time, Pallas kernels for 7%

profile of v8, /device:TPU:0, one launch (start us, length us, event | category | flops | bytes accessed | tf_op | source)
XLA Modules:
  0.0 48.6 jit_solution(508469902197918196)
XLA Ops:
  0.6 0.0 copy-start.5
  0.6 2.0 %pack.1 = (bf16[16,16,512]{2,1,0:T(8,128)(2,1)}, bf16[272,512]{1,0:T(8,128)(2,1)}) custom-call(s32[1,16,16]{2,1,0:T(8,128)} %rows_hbm.1, s32[1,16]{1,0:T(1,128)} %count_hbm.1, bf16[256,512]{1,0:T(8,128)(2,1)} %x_ref.1, s32[1,512]{1,0:T(1,128)} %query_hbm.1, s32[1,512]{1,0:T(1,128)} %positive_hbm.1, s32[1,32]{1,0:T(1,128)} %negative_hbm.1), custom_call_target="tpu_custom_call" | custom-call | flops 67108864 | bytes 808128 | tf_op jit(solution)/shard_map/pack/pallas_call | solution.py:339
  2.6 0.0 copy-start.1
  2.6 0.0 copy-start.4
  2.6 7.6 %all-to-all-start = ((bf16[16,16,512]{2,1,0:T(8,128)(2,1)}), bf16[16,16,512]{2,1,0:T(8,128)(2,1)S(1)}, u32[]{:S(2)}, u32[]{:S(2)}) async-start(bf16[16,16,512]{2,1,0:T(8,128)(2,1)} %get-tuple-element.25), calls=%async_computation | async-start | bytes 524288 | tf_op jit(solution)/shard_map/all_to_all | solution.py:412
  10.2 0.0 copy-start.6
  10.2 1.6 %collective-permute-start = (bf16[272,512]{1,0:T(8,128)(2,1)}, bf16[272,512]{1,0:T(8,128)(2,1)S(1)}, u32[]{:S(2)}, u32[]{:S(2)}) collective-permute-start(bf16[272,512]{1,0:T(8,128)(2,1)} %get-tuple-element.28.refs_0_), channel_id=1, source_target_pairs={{16,0},{0,16},{17,1},{1,17},{18,2},{2,18},{19,3},{3,19},{20,4},{4,... | collective-permute-start | bytes 835592 | tf_op jit(solution)/shard_map/ppermute | solution.py:382
  11.8 0.0 copy-done.5
  11.8 0.0 copy-done.1
  11.8 0.0 copy-done.4
  11.8 0.0 copy-done.6
  11.8 1.1 %local.1 = (f32[256,512]{1,0:T(8,128)S(1)}, f32[256,384]{1,0:T(8,128)S(1)}) custom-call(s32[1,2,4]{2,1,0:T(2,128)S(1)} %copy-done.6, bf16[1,2,4,128,128]{4,3,2,1,0:T(8,128)(2,1)S(1)} %copy-done.4, bf16[256,512]{1,0:T(8,128)(2,1)S(1)} %copy-done.1, s32[1,16,16]{2,1,0:T(8,128)S(1)} %copy-done.5), custom_call_target="tpu_custom_call" | custom-call | flops 134217728 | bytes 1442848 | tf_op jit(solution)/shard_map/local/pallas_call | solution.py:339
  12.9 7.4 %all-to-all-done = bf16[16,16,512]{2,1,0:T(8,128)(2,1)S(1)} async-done(((bf16[16,16,512]{2,1,0:T(8,128)(2,1)}), bf16[16,16,512]{2,1,0:T(8,128)(2,1)S(1)}, u32[]{:S(2)}, u32[]{:S(2)}) %all-to-all-start) | async-done | bytes 262176 | tf_op jit(solution)/shard_map/all_to_all | solution.py:412
  20.2 0.0 copy-start.3
  20.2 0.3 aggregate.2.head_ref
  20.5 0.0 copy-start
  20.5 0.0 copy-start.2
  20.6 1.6 %collective-permute-start.2 = (bf16[128,512]{1,0:T(8,128)(2,1)S(1)}, bf16[128,512]{1,0:T(8,128)(2,1)S(1)}, u32[]{:S(2)}, u32[]{:S(2)}) collective-permute-start(bf16[128,512]{1,0:T(8,128)(2,1)S(1)} %aggregate.2.head_ref), channel_id=1, source_target_pairs={{16,0},{0,16},{17,1},{1,17},{18,2},{2,18},{19,3},{3,19},{20,4},{4,... | collective-permute-start | bytes 393224 | tf_op jit(solution)/shard_map/ppermute | solution.py:382
  22.1 0.3 aggregate.3.tail_ref
  22.4 0.6 %collective-permute-start.1 = (bf16[128,512]{1,0:T(8,128)(2,1)S(1)}, bf16[128,512]{1,0:T(8,128)(2,1)S(1)}, u32[]{:S(2)}, u32[]{:S(2)}) collective-permute-start(bf16[128,512]{1,0:T(8,128)(2,1)S(1)} %aggregate.3.tail_ref), channel_id=1, source_target_pairs={{16,0},{0,16},{17,1},{1,17},{18,2},{2,18},{19,3},{3,19},{20,4},{4,... | collective-permute-start | bytes 393224 | tf_op jit(solution)/shard_map/ppermute | solution.py:382
  23.0 0.0 collective-permute-done.refs_1_
  23.0 0.0 copy-done.3
  23.0 0.0 copy-done
  23.0 0.0 copy-done.2
  23.0 1.3 %embed.1 = (bf16[256,512]{1,0:T(8,128)(2,1)}, bf16[256,512]{1,0:T(8,128)(2,1)S(1)}, f32[256,256]{1,0:T(8,128)S(1)}, f32[256,128]{1,0:T(8,128)S(1)}, bf16[4,2,64,...) custom-call(s32[1]{0:T(128)} %bitcast.group_ref, ...), custom_call_target="tpu_custom_call" | custom-call | flops 268435456 | bytes 4423684 | tf_op jit(solution)/shard_map/embed/pallas_call | solution.py:339
  24.3 2.7 %collective-permute-done.2.refs_0_ = bf16[128,512]{1,0:T(8,128)(2,1)S(1)} collective-permute-done((bf16[128,512]{1,0:T(8,128)(2,1)S(1)}, bf16[128,512]{1,0:T(8,128)(2,1)S(1)}, u32[]{:S(2)}, u32[]{:S(2)}) %collective-permute-start.2) | collective-permute-done | bytes 131104 | tf_op jit(solution)/shard_map/ppermute | solution.py:382
  27.0 0.3 ahead.1
  27.3 1.4 %collective-permute-done.1.refs_0_ = bf16[128,512]{1,0:T(8,128)(2,1)S(1)} collective-permute-done((bf16[128,512]{1,0:T(8,128)(2,1)S(1)}, bf16[128,512]{1,0:T(8,128)(2,1)S(1)}, u32[]{:S(2)}, u32[]{:S(2)}) %collective-permute-start.1) | collective-permute-done | bytes 131104 | tf_op jit(solution)/shard_map/ppermute | solution.py:382
  28.7 1.3 %gradient.1 = (bf16[8,64,256]{2,1,0:T(8,128)(2,1)S(1)}, bf16[256,256]{1,0:T(8,128)(2,1)S(1)}, bf16[256,256]{1,0:T(8,128)(2,1)S(1)}, bf16[4,2,64,128]{3,2,1,0:T(8,128)(2,1)S(1)}) custom-call(s32[1]{0:T(128)} %bitcast.2.core_ref, s32[1]{0:T(128)} %bitcast.group_ref, bf16[512,512]{1,0:T(8,128)(2,1)S(1)} %copy-done, ...), custom_call_target="tpu_custom_call" | custom-call | flops 134217728 | bytes 4063240 | tf_op jit(solution)/shard_map/gradient/pallas_call | solution.py:339
  30.1 0.1 collective-permute-start.3
  30.2 0.3 keep.1
  30.5 1.2 %collective-permute-done.3 = bf16[8,64,256]{2,1,0:T(8,128)(2,1)S(1)} collective-permute-done((bf16[8,64,256]{2,1,0:T(8,128)(2,1)S(1)}, bf16[8,64,256]{2,1,0:T(8,128)(2,1)S(1)}, u32[]{:S(2)}, u32[]{:S(2)}) %collective-permute-start.3) | collective-permute-done | bytes 262176 | tf_op jit(solution)/shard_map/ppermute | solution.py:520
  31.7 0.1 add_convert_fusion
  31.8 12.2 %all_to_all.10 = bf16[8,64,256]{2,1,0:T(8,128)(2,1)S(1)} all-to-all(bf16[8,64,256]{2,1,0:T(8,128)(2,1)S(1)} %add_convert_fusion), channel_id=1, replica_groups={{0,2,4,6,8,10,12,14},{1,3,5,7,9,11,13,15},{16,18,20,22,24,26,28,30},{17..., dimensions={0} | all-to-all | bytes 524288 | tf_op jit(solution)/shard_map/all_to_all | solution.py:521
  44.0 1.6 %collective-permute-start.4 = (bf16[64,256]{1,0:T(8,128)(2,1)S(1)}, bf16[64,256]{1,0:T(8,128)(2,1)S(1)}, u32[]{:S(2)}, u32[]{:S(2)}) collective-permute-start(bf16[64,256]{1,0:T(8,128)(2,1)S(1)} %reduce_sum.12), channel_id=1, source_target_pairs={{16,0},{0,16},{17,1},{1,17},{18,2},{2,18},{19,3},{3,19},{20,4},{4,... | collective-permute-start | bytes 98312 | tf_op jit(solution)/shard_map/ppermute | solution.py:382
  45.5 2.4 %collective-permute-done.4 = bf16[64,256]{1,0:T(8,128)(2,1)S(1)} collective-permute-done((bf16[64,256]{1,0:T(8,128)(2,1)S(1)}, bf16[64,256]{1,0:T(8,128)(2,1)S(1)}, u32[]{:S(2)}, u32[]{:S(2)}) %collective-permute-start.4) | collective-permute-done | bytes 32800 | tf_op jit(solution)/shard_map/ppermute | solution.py:382
  47.9 0.6 %maximum_select_fusion = bf16[64,512]{1,0:T(8,128)(2,1)} fusion(bf16[64,256]{1,0:T(8,128)(2,1)S(1)} %collective-permute-done.4, bf16[64,256]{1,0:T(8,128)(2,1)S(1)} %reduce_sum.12, pred[]{:T(512)S(6)} %eq.3), kind=kLoop, calls=%fused_computation.1 | loop fusion | flops 294912 | bytes 131073 | tf_op jit(solution)/shard_map/jit(_where)/select_n | solution.py:532
  (1 shorter events, 0.0 us)
Async XLA Ops:
  0.6 11.2 %copy-start.5 = (s32[1,16,16]{2,1,0:T(8,128)S(1)}, s32[1,16,16]{2,1,0:T(8,128)}, u32[]{:S(2)}) copy-start(s32[1,16,16]{2,1,0:T(8,128)} %target_ref.1) | copy-start | bytes 3076
  2.6 9.2 %copy-start.1 = (bf16[256,512]{1,0:T(8,128)(2,1)S(1)}, bf16[256,512]{1,0:T(8,128)(2,1)}, u32[]{:S(2)}) copy-start(bf16[256,512]{1,0:T(8,128)(2,1)} %x_ref.1) | copy-start | bytes 786436
  2.6 9.2 %copy-start.4 = (bf16[1,2,4,128,128]{4,3,2,1,0:T(8,128)(2,1)S(1)}, bf16[1,2,4,128,128]{4,3,2,1,0:T(8,128)(2,1)}, u32[]{:S(2)}) copy-start(bf16[1,2,4,128,128]{4,3,2,1,0:T(8,128)(2,1)} %values_ref.1) | copy-start | bytes 786436
  2.6 17.6 %all-to-all-start = ((bf16[16,16,512]{2,1,0:T(8,128)(2,1)}), bf16[16,16,512]{2,1,0:T(8,128)(2,1)S(1)}, u32[]{:S(2)}, u32[]{:S(2)}) async-start(bf16[16,16,512]{2,1,0:T(8,128)(2,1)} %get-tuple-element.25), calls=%async_computation | async-start | bytes 524288 | tf_op jit(solution)/shard_map/all_to_all | solution.py:412
  10.2 1.6 %copy-start.6 = (s32[1,2,4]{2,1,0:T(2,128)S(1)}, s32[1,2,4]{2,1,0:T(2,128)}, u32[]{:S(2)}) copy-start(s32[1,2,4]{2,1,0:T(2,128)} %columns_ref.1) | copy-start | bytes 100
  10.2 12.8 %collective-permute-start = (bf16[272,512]{1,0:T(8,128)(2,1)}, bf16[272,512]{1,0:T(8,128)(2,1)S(1)}, u32[]{:S(2)}, u32[]{:S(2)}) collective-permute-start(bf16[272,512]{1,0:T(8,128)(2,1)} %get-tuple-element.28.refs_0_), channel_id=1, source_target_pairs={{16,0},{0,16},{17,1},{1,17},{18,2},{2,18},{19,3},{3,19},{20,4},{4,... | collective-permute-start | bytes 835592 | tf_op jit(solution)/shard_map/ppermute | solution.py:382
  20.2 2.8 %copy-start.3 = (bf16[272,512]{1,0:T(8,128)(2,1)S(1)}, bf16[272,512]{1,0:T(8,128)(2,1)}, u32[]{:S(2)}) copy-start(bf16[272,512]{1,0:T(8,128)(2,1)} %get-tuple-element.28.refs_0_) | copy-start | bytes 835588
  20.5 2.5 %copy-start = (bf16[512,512]{1,0:T(8,128)(2,1)S(1)}, bf16[512,512]{1,0:T(8,128)(2,1)}, u32[]{:S(2)}) copy-start(bf16[512,512]{1,0:T(8,128)(2,1)} %weight_neigh_ref.5) | copy-start | bytes 1572868
  20.5 2.5 %copy-start.2 = (bf16[512,512]{1,0:T(8,128)(2,1)S(1)}, bf16[512,512]{1,0:T(8,128)(2,1)}, u32[]{:S(2)}) copy-start(bf16[512,512]{1,0:T(8,128)(2,1)} %weight_self_ref.1) | copy-start | bytes 1572868
  20.6 6.4 %collective-permute-start.2 = (bf16[128,512]{1,0:T(8,128)(2,1)S(1)}, bf16[128,512]{1,0:T(8,128)(2,1)S(1)}, u32[]{:S(2)}, u32[]{:S(2)}) collective-permute-start(bf16[128,512]{1,0:T(8,128)(2,1)S(1)} %aggregate.2.head_ref), channel_id=1, source_target_pairs={{16,0},{0,16},{17,1},{1,17},{18,2},{2,18},{19,3},{3,19},{20,4},{4,... | collective-permute-start | bytes 393224 | tf_op jit(solution)/shard_map/ppermute | solution.py:382
  22.4 6.3 %collective-permute-start.1 = (bf16[128,512]{1,0:T(8,128)(2,1)S(1)}, bf16[128,512]{1,0:T(8,128)(2,1)S(1)}, u32[]{:S(2)}, u32[]{:S(2)}) collective-permute-start(bf16[128,512]{1,0:T(8,128)(2,1)S(1)} %aggregate.3.tail_ref), channel_id=1, source_target_pairs={{16,0},{0,16},{17,1},{1,17},{18,2},{2,18},{19,3},{3,19},{20,4},{4,... | collective-permute-start | bytes 393224 | tf_op jit(solution)/shard_map/ppermute | solution.py:382
  30.1 1.6 %collective-permute-start.3 = (bf16[8,64,256]{2,1,0:T(8,128)(2,1)S(1)}, bf16[8,64,256]{2,1,0:T(8,128)(2,1)S(1)}, u32[]{:S(2)}, u32[]{:S(2)}) collective-permute-start(bf16[8,64,256]{2,1,0:T(8,128)(2,1)S(1)} %get-tuple-element.47), channel_id=1, source_target_pairs={{0,1},{1,0},{2,3},{3,2},{4,5},{5,4},{6,7},{7,6},{8,9},{9,8},{10,11... | collective-permute-start | bytes 786440 | tf_op jit(solution)/shard_map/ppermute | solution.py:520
  44.0 4.0 %collective-permute-start.4 = (bf16[64,256]{1,0:T(8,128)(2,1)S(1)}, bf16[64,256]{1,0:T(8,128)(2,1)S(1)}, u32[]{:S(2)}, u32[]{:S(2)}) collective-permute-start(bf16[64,256]{1,0:T(8,128)(2,1)S(1)} %reduce_sum.12), channel_id=1, source_target_pairs={{16,0},{0,16},{17,1},{1,17},{18,2},{2,18},{19,3},{3,19},{20,4},{4,... | collective-permute-start | bytes 98312 | tf_op jit(solution)/shard_map/ppermute | solution.py:382

commit v9 on v8

--- a/solution.py
+++ b/solution.py
@@ -309,15 +309,17 @@
         dot(grad[:, lanes[m]], parts[m].astype(BF16)) for m in range(members)
     ).astype(BF16)
 
+    left = jnp.concatenate([grad, hot], axis=0)
+    right = jnp.concatenate([columns_of(group, members, cand), cand_grad], axis=0)
+    emb_grads = [dot(left[:, lanes[m]], right, 0, 0) for m in range(members)]
+
     weighted = grad.astype(F32) * product
     weighted += hot.astype(F32) * jnp.sum(weighted, axis=1, keepdims=True)
     inner = jnp.sum(weighted, axis=0, keepdims=True) / width
     inner = jnp.broadcast_to(inner, (8, inner.shape[1])).T[:, :1]
 
-    left = jnp.concatenate([grad, hot], axis=0)
-    right = jnp.concatenate([columns_of(group, members, cand), cand_grad], axis=0)
     pre_grads = [
-        (scales[m] * (dot(left[:, lanes[m]], right, 0, 0) - parts[m] * inner[lanes[m]])).astype(BF16)
+        (scales[m] * (emb_grads[m] - parts[m] * inner[lanes[m]])).astype(BF16)
         for m in range(members)
     ]
     for other, tail_turned_ref in enumerate(other_turned):

time: 48.9 us -> 48.9 us (level)
  no operation moved by 1% of the time
where the time goes in v9:
time: 48.9 us; the launch traced here: 48.6 us
  waiting for transfers between devices  15.1 us (31%)
  starting transfers between devices  12.9 us (26%)
  blocking collectives  12.2 us (25%)
  Pallas kernels  6.89 us (14%)
  between operations  0.79 us (2%)
  other arithmetic  0.75 us (2%)
    all_to_all x1, blocking collectives, on_device(): lax.all_to_all(chip_sum, 'dom', split_axis=0, concat_axis=0, axis_index_g...  12.2 us
    all_to_all x1, starting transfers between devices, on_device(): lax.all_to_all(outgoing, 'dom', split_axis=0, concat_axis=0, tiled=True)  7.56 us
    all_to_all x1, waiting for transfers between devices, on_device(): lax.all_to_all(outgoing, 'dom', split_axis=0, concat_axis=0, tiled=True)  7.35 us
    pallas_call x8, Pallas kernels, call(): pl.pallas_call(kernel, name=name, out_shape=shapes, in_specs=[place for _...  6.89 us
    ppermute x4, waiting for transfers between devices, of_others(): lax.ppermute(own, 'group', [((g + k) % groups, g) for g in range(groups)])  6.51 us
    ppermute x4, starting transfers between devices, of_others(): lax.ppermute(own, 'group', [((g + k) % groups, g) for g in range(groups)])  5.27 us
    ppermute x1, waiting for transfers between devices, on_device(): lax.ppermute(send, 'dom', swap).astype(F32)  1.21 us
  transfers between devices with their start and end apart: 6, of which 5 were waited for; matrix products, arithmetic and copies ran while one was open for 0% of the time, Pallas kernels for 7%

profile of v9, /device:TPU:0, one launch (start us, length us, event | category | flops | bytes accessed | tf_op | source)
XLA Modules:
  0.0 48.6 jit_solution(11376057370199982795)
XLA Ops:
  0.6 0.0 copy-start.5
  0.6 2.0 %pack.1 = (bf16[16,16,512]{2,1,0:T(8,128)(2,1)}, bf16[272,512]{1,0:T(8,128)(2,1)}) custom-call(s32[1,16,16]{2,1,0:T(8,128)} %rows_hbm.1, s32[1,16]{1,0:T(1,128)} %count_hbm.1, bf16[256,512]{1,0:T(8,128)(2,1)} %x_ref.1, s32[1,512]{1,0:T(1,128)} %query_hbm.1, s32[1,512]{1,0:T(1,128)} %positive_hbm.1, s32[1,32]{1,0:T(1,128)} %negative_hbm.1), custom_call_target="tpu_custom_call" | custom-call | flops 67108864 | bytes 808128 | tf_op jit(solution)/shard_map/pack/pallas_call | solution.py:341
  2.6 0.0 copy-start.1
  2.6 0.0 copy-start.4
  2.6 7.6 %all-to-all-start = ((bf16[16,16,512]{2,1,0:T(8,128)(2,1)}), bf16[16,16,512]{2,1,0:T(8,128)(2,1)S(1)}, u32[]{:S(2)}, u32[]{:S(2)}) async-start(bf16[16,16,512]{2,1,0:T(8,128)(2,1)} %get-tuple-element.25), calls=%async_computation | async-start | bytes 524288 | tf_op jit(solution)/shard_map/all_to_all | solution.py:414
  10.2 0.0 copy-start.6
  10.2 1.6 %collective-permute-start = (bf16[272,512]{1,0:T(8,128)(2,1)}, bf16[272,512]{1,0:T(8,128)(2,1)S(1)}, u32[]{:S(2)}, u32[]{:S(2)}) collective-permute-start(bf16[272,512]{1,0:T(8,128)(2,1)} %get-tuple-element.28.refs_0_), channel_id=1, source_target_pairs={{16,0},{0,16},{17,1},{1,17},{18,2},{2,18},{19,3},{3,19},{20,4},{4,... | collective-permute-start | bytes 835592 | tf_op jit(solution)/shard_map/ppermute | solution.py:384
  11.8 0.0 copy-done.5
  11.8 0.0 copy-done.1
  11.8 0.0 copy-done.4
  11.8 0.0 copy-done.6
  11.8 1.1 %local.1 = (f32[256,512]{1,0:T(8,128)S(1)}, f32[256,384]{1,0:T(8,128)S(1)}) custom-call(s32[1,2,4]{2,1,0:T(2,128)S(1)} %copy-done.6, bf16[1,2,4,128,128]{4,3,2,1,0:T(8,128)(2,1)S(1)} %copy-done.4, bf16[256,512]{1,0:T(8,128)(2,1)S(1)} %copy-done.1, s32[1,16,16]{2,1,0:T(8,128)S(1)} %copy-done.5), custom_call_target="tpu_custom_call" | custom-call | flops 134217728 | bytes 1442848 | tf_op jit(solution)/shard_map/local/pallas_call | solution.py:341
  12.9 7.4 %all-to-all-done = bf16[16,16,512]{2,1,0:T(8,128)(2,1)S(1)} async-done(((bf16[16,16,512]{2,1,0:T(8,128)(2,1)}), bf16[16,16,512]{2,1,0:T(8,128)(2,1)S(1)}, u32[]{:S(2)}, u32[]{:S(2)}) %all-to-all-start) | async-done | bytes 262176 | tf_op jit(solution)/shard_map/all_to_all | solution.py:414
  20.2 0.0 copy-start.3
  20.2 0.3 aggregate.2.head_ref
  20.5 0.0 copy-start
  20.5 0.0 copy-start.2
  20.6 1.6 %collective-permute-start.2 = (bf16[128,512]{1,0:T(8,128)(2,1)S(1)}, bf16[128,512]{1,0:T(8,128)(2,1)S(1)}, u32[]{:S(2)}, u32[]{:S(2)}) collective-permute-start(bf16[128,512]{1,0:T(8,128)(2,1)S(1)} %aggregate.2.head_ref), channel_id=1, source_target_pairs={{16,0},{0,16},{17,1},{1,17},{18,2},{2,18},{19,3},{3,19},{20,4},{4,... | collective-permute-start | bytes 393224 | tf_op jit(solution)/shard_map/ppermute | solution.py:384
  22.1 0.3 aggregate.3.tail_ref
  22.4 0.6 %collective-permute-start.1 = (bf16[128,512]{1,0:T(8,128)(2,1)S(1)}, bf16[128,512]{1,0:T(8,128)(2,1)S(1)}, u32[]{:S(2)}, u32[]{:S(2)}) collective-permute-start(bf16[128,512]{1,0:T(8,128)(2,1)S(1)} %aggregate.3.tail_ref), channel_id=1, source_target_pairs={{16,0},{0,16},{17,1},{1,17},{18,2},{2,18},{19,3},{3,19},{20,4},{4,... | collective-permute-start | bytes 393224 | tf_op jit(solution)/shard_map/ppermute | solution.py:384
  23.0 0.0 collective-permute-done.refs_1_
  23.0 0.0 copy-done.3
  23.0 0.0 copy-done
  23.0 0.0 copy-done.2
  23.0 1.3 %embed.1 = (bf16[256,512]{1,0:T(8,128)(2,1)}, bf16[256,512]{1,0:T(8,128)(2,1)S(1)}, f32[256,256]{1,0:T(8,128)S(1)}, f32[256,128]{1,0:T(8,128)S(1)}, bf16[4,2,64,...) custom-call(s32[1]{0:T(128)} %bitcast.group_ref, ...), custom_call_target="tpu_custom_call" | custom-call | flops 268435456 | bytes 4423684 | tf_op jit(solution)/shard_map/embed/pallas_call | solution.py:341
  24.3 2.7 %collective-permute-done.2.refs_0_ = bf16[128,512]{1,0:T(8,128)(2,1)S(1)} collective-permute-done((bf16[128,512]{1,0:T(8,128)(2,1)S(1)}, bf16[128,512]{1,0:T(8,128)(2,1)S(1)}, u32[]{:S(2)}, u32[]{:S(2)}) %collective-permute-start.2) | collective-permute-done | bytes 131104 | tf_op jit(solution)/shard_map/ppermute | solution.py:384
  27.0 0.3 ahead.1
  27.3 1.4 %collective-permute-done.1.refs_0_ = bf16[128,512]{1,0:T(8,128)(2,1)S(1)} collective-permute-done((bf16[128,512]{1,0:T(8,128)(2,1)S(1)}, bf16[128,512]{1,0:T(8,128)(2,1)S(1)}, u32[]{:S(2)}, u32[]{:S(2)}) %collective-permute-start.1) | collective-permute-done | bytes 131104 | tf_op jit(solution)/shard_map/ppermute | solution.py:384
  28.7 1.3 %gradient.1 = (bf16[8,64,256]{2,1,0:T(8,128)(2,1)S(1)}, bf16[256,256]{1,0:T(8,128)(2,1)S(1)}, bf16[256,256]{1,0:T(8,128)(2,1)S(1)}, bf16[4,2,64,128]{3,2,1,0:T(8,128)(2,1)S(1)}) custom-call(s32[1]{0:T(128)} %bitcast.2.core_ref, s32[1]{0:T(128)} %bitcast.group_ref, bf16[512,512]{1,0:T(8,128)(2,1)S(1)} %copy-done, ...), custom_call_target="tpu_custom_call" | custom-call | flops 134217728 | bytes 4063240 | tf_op jit(solution)/shard_map/gradient/pallas_call | solution.py:341
  30.1 0.1 collective-permute-start.3
  30.2 0.3 keep.1
  30.5 1.2 %collective-permute-done.3 = bf16[8,64,256]{2,1,0:T(8,128)(2,1)S(1)} collective-permute-done((bf16[8,64,256]{2,1,0:T(8,128)(2,1)S(1)}, bf16[8,64,256]{2,1,0:T(8,128)(2,1)S(1)}, u32[]{:S(2)}, u32[]{:S(2)}) %collective-permute-start.3) | collective-permute-done | bytes 262176 | tf_op jit(solution)/shard_map/ppermute | solution.py:522
  31.7 0.1 add_convert_fusion
  31.8 12.2 %all_to_all.10 = bf16[8,64,256]{2,1,0:T(8,128)(2,1)S(1)} all-to-all(bf16[8,64,256]{2,1,0:T(8,128)(2,1)S(1)} %add_convert_fusion), channel_id=1, replica_groups={{0,2,4,6,8,10,12,14},{1,3,5,7,9,11,13,15},{16,18,20,22,24,26,28,30},{17..., dimensions={0} | all-to-all | bytes 524288 | tf_op jit(solution)/shard_map/all_to_all | solution.py:523
  44.0 1.6 %collective-permute-start.4 = (bf16[64,256]{1,0:T(8,128)(2,1)S(1)}, bf16[64,256]{1,0:T(8,128)(2,1)S(1)}, u32[]{:S(2)}, u32[]{:S(2)}) collective-permute-start(bf16[64,256]{1,0:T(8,128)(2,1)S(1)} %reduce_sum.12), channel_id=1, source_target_pairs={{16,0},{0,16},{17,1},{1,17},{18,2},{2,18},{19,3},{3,19},{20,4},{4,... | collective-permute-start | bytes 98312 | tf_op jit(solution)/shard_map/ppermute | solution.py:384
  45.5 2.4 %collective-permute-done.4 = bf16[64,256]{1,0:T(8,128)(2,1)S(1)} collective-permute-done((bf16[64,256]{1,0:T(8,128)(2,1)S(1)}, bf16[64,256]{1,0:T(8,128)(2,1)S(1)}, u32[]{:S(2)}, u32[]{:S(2)}) %collective-permute-start.4) | collective-permute-done | bytes 32800 | tf_op jit(solution)/shard_map/ppermute | solution.py:384
  47.9 0.6 %maximum_select_fusion = bf16[64,512]{1,0:T(8,128)(2,1)} fusion(bf16[64,256]{1,0:T(8,128)(2,1)S(1)} %collective-permute-done.4, bf16[64,256]{1,0:T(8,128)(2,1)S(1)} %reduce_sum.12, pred[]{:T(512)S(6)} %eq.3), kind=kLoop, calls=%fused_computation.1 | loop fusion | flops 294912 | bytes 131073 | tf_op jit(solution)/shard_map/jit(_where)/select_n | solution.py:534
  (1 shorter events, 0.0 us)
Async XLA Ops:
  0.6 11.2 %copy-start.5 = (s32[1,16,16]{2,1,0:T(8,128)S(1)}, s32[1,16,16]{2,1,0:T(8,128)}, u32[]{:S(2)}) copy-start(s32[1,16,16]{2,1,0:T(8,128)} %target_ref.1) | copy-start | bytes 3076
  2.6 9.2 %copy-start.1 = (bf16[256,512]{1,0:T(8,128)(2,1)S(1)}, bf16[256,512]{1,0:T(8,128)(2,1)}, u32[]{:S(2)}) copy-start(bf16[256,512]{1,0:T(8,128)(2,1)} %x_ref.1) | copy-start | bytes 786436
  2.6 9.2 %copy-start.4 = (bf16[1,2,4,128,128]{4,3,2,1,0:T(8,128)(2,1)S(1)}, bf16[1,2,4,128,128]{4,3,2,1,0:T(8,128)(2,1)}, u32[]{:S(2)}) copy-start(bf16[1,2,4,128,128]{4,3,2,1,0:T(8,128)(2,1)} %values_ref.1) | copy-start | bytes 786436
  2.6 17.6 %all-to-all-start = ((bf16[16,16,512]{2,1,0:T(8,128)(2,1)}), bf16[16,16,512]{2,1,0:T(8,128)(2,1)S(1)}, u32[]{:S(2)}, u32[]{:S(2)}) async-start(bf16[16,16,512]{2,1,0:T(8,128)(2,1)} %get-tuple-element.25), calls=%async_computation | async-start | bytes 524288 | tf_op jit(solution)/shard_map/all_to_all | solution.py:414
  10.2 1.6 %copy-start.6 = (s32[1,2,4]{2,1,0:T(2,128)S(1)}, s32[1,2,4]{2,1,0:T(2,128)}, u32[]{:S(2)}) copy-start(s32[1,2,4]{2,1,0:T(2,128)} %columns_ref.1) | copy-start | bytes 100
  10.2 12.8 %collective-permute-start = (bf16[272,512]{1,0:T(8,128)(2,1)}, bf16[272,512]{1,0:T(8,128)(2,1)S(1)}, u32[]{:S(2)}, u32[]{:S(2)}) collective-permute-start(bf16[272,512]{1,0:T(8,128)(2,1)} %get-tuple-element.28.refs_0_), channel_id=1, source_target_pairs={{16,0},{0,16},{17,1},{1,17},{18,2},{2,18},{19,3},{3,19},{20,4},{4,... | collective-permute-start | bytes 835592 | tf_op jit(solution)/shard_map/ppermute | solution.py:384
  20.2 2.8 %copy-start.3 = (bf16[272,512]{1,0:T(8,128)(2,1)S(1)}, bf16[272,512]{1,0:T(8,128)(2,1)}, u32[]{:S(2)}) copy-start(bf16[272,512]{1,0:T(8,128)(2,1)} %get-tuple-element.28.refs_0_) | copy-start | bytes 835588
  20.5 2.5 %copy-start = (bf16[512,512]{1,0:T(8,128)(2,1)S(1)}, bf16[512,512]{1,0:T(8,128)(2,1)}, u32[]{:S(2)}) copy-start(bf16[512,512]{1,0:T(8,128)(2,1)} %weight_neigh_ref.5) | copy-start | bytes 1572868
  20.5 2.5 %copy-start.2 = (bf16[512,512]{1,0:T(8,128)(2,1)S(1)}, bf16[512,512]{1,0:T(8,128)(2,1)}, u32[]{:S(2)}) copy-start(bf16[512,512]{1,0:T(8,128)(2,1)} %weight_self_ref.1) | copy-start | bytes 1572868
  20.6 6.4 %collective-permute-start.2 = (bf16[128,512]{1,0:T(8,128)(2,1)S(1)}, bf16[128,512]{1,0:T(8,128)(2,1)S(1)}, u32[]{:S(2)}, u32[]{:S(2)}) collective-permute-start(bf16[128,512]{1,0:T(8,128)(2,1)S(1)} %aggregate.2.head_ref), channel_id=1, source_target_pairs={{16,0},{0,16},{17,1},{1,17},{18,2},{2,18},{19,3},{3,19},{20,4},{4,... | collective-permute-start | bytes 393224 | tf_op jit(solution)/shard_map/ppermute | solution.py:384
  22.4 6.3 %collective-permute-start.1 = (bf16[128,512]{1,0:T(8,128)(2,1)S(1)}, bf16[128,512]{1,0:T(8,128)(2,1)S(1)}, u32[]{:S(2)}, u32[]{:S(2)}) collective-permute-start(bf16[128,512]{1,0:T(8,128)(2,1)S(1)} %aggregate.3.tail_ref), channel_id=1, source_target_pairs={{16,0},{0,16},{17,1},{1,17},{18,2},{2,18},{19,3},{3,19},{20,4},{4,... | collective-permute-start | bytes 393224 | tf_op jit(solution)/shard_map/ppermute | solution.py:384
  30.1 1.6 %collective-permute-start.3 = (bf16[8,64,256]{2,1,0:T(8,128)(2,1)S(1)}, bf16[8,64,256]{2,1,0:T(8,128)(2,1)S(1)}, u32[]{:S(2)}, u32[]{:S(2)}) collective-permute-start(bf16[8,64,256]{2,1,0:T(8,128)(2,1)S(1)} %get-tuple-element.47), channel_id=1, source_target_pairs={{0,1},{1,0},{2,3},{3,2},{4,5},{5,4},{6,7},{7,6},{8,9},{9,8},{10,11... | collective-permute-start | bytes 786440 | tf_op jit(solution)/shard_map/ppermute | solution.py:522
  44.0 4.0 %collective-permute-start.4 = (bf16[64,256]{1,0:T(8,128)(2,1)S(1)}, bf16[64,256]{1,0:T(8,128)(2,1)S(1)}, u32[]{:S(2)}, u32[]{:S(2)}) collective-permute-start(bf16[64,256]{1,0:T(8,128)(2,1)S(1)} %reduce_sum.12), channel_id=1, source_target_pairs={{16,0},{0,16},{17,1},{1,17},{18,2},{2,18},{19,3},{3,19},{20,4},{4,... | collective-permute-start | bytes 98312 | tf_op jit(solution)/shard_map/ppermute | solution.py:384
